TPU v7x, 32 devices: a whole 2x2x4 slice. The times are simulated.
32 devices in a mesh: dp: 4 (over y, x), seq: 8 (over z, core).
Axes of the slice: x: 2, y: 2, z: 4, core: 2. Of those that a mesh axis runs over, the one named last changes fastest.
Arguments:
- tokens: bfloat16 [16, 2048, 768], P('dp', 'seq'), may hold values from -6 to 6
- lengths: int32 [16], P('dp'), may hold values from 512 to 2048, as said below
- query_weight: bfloat16 [768, 768], P(('dp', 'seq')), may hold values from -0.21875 to 0.21875
- key_weight: bfloat16 [768, 768], P(('dp', 'seq')), may hold values from -0.21875 to 0.21875
- value_weight: bfloat16 [768, 768], P(('dp', 'seq')), may hold values from -0.21875 to 0.21875
- out_weight: bfloat16 [768, 768], P(('dp', 'seq')), may hold values from -6 to 6
- up_weight: bfloat16 [768, 3072], P(('dp', 'seq')), may hold values from -0.21875 to 0.21875
- down_weight: bfloat16 [3072, 768], P(('dp', 'seq')), may hold values from -0.109375 to 0.109375
- query_bias: bfloat16 [768], P(('dp', 'seq')), may hold values from -3 to 3
- value_bias: bfloat16 [768], P(('dp', 'seq')), may hold values from -3 to 3
- out_bias: bfloat16 [768], P(('dp', 'seq')), may hold values from -3 to 3
- up_bias: bfloat16 [3072], P(('dp', 'seq')), may hold values from -3 to 3
- down_bias: bfloat16 [768], P(('dp', 'seq')), may hold values from -3 to 3
- first_gain: bfloat16 [768], P(('dp', 'seq')), may hold values from 0.5 to 1.5
- first_shift: bfloat16 [768], P(('dp', 'seq')), may hold values from -2 to 2
- second_gain: bfloat16 [768], P(('dp', 'seq')), may hold values from 0.5 to 1.5
- second_shift: bfloat16 [768], P(('dp', 'seq')), may hold values from -2 to 2
- cotangent: bfloat16 [16, 2048, 768], P('dp', 'seq'), may hold values from -6 to 6
Outputs:
- output: bfloat16 [16, 2048, 768], P('dp', 'seq')
- tokens_grad: float32 [16, 2048, 768], P('dp', 'seq')
- query_weight_grad: float32 [768, 768], P(('dp', 'seq'))
- key_weight_grad: float32 [768, 768], P(('dp', 'seq'))
- value_weight_grad: float32 [768, 768], P(('dp', 'seq'))
- out_weight_grad: float32 [768, 768], P(('dp', 'seq'))
- up_weight_grad: float32 [768, 3072], P(('dp', 'seq'))
- down_weight_grad: float32 [3072, 768], P(('dp', 'seq'))
- query_bias_grad: float32 [768], P(('dp', 'seq'))
- value_bias_grad: float32 [768], P(('dp', 'seq'))
- out_bias_grad: float32 [768], P(('dp', 'seq'))
- up_bias_grad: float32 [3072], P(('dp', 'seq'))
- down_bias_grad: float32 [768], P(('dp', 'seq'))
- first_gain_grad: float32 [768], P(('dp', 'seq'))
- first_shift_grad: float32 [768], P(('dp', 'seq'))
- second_gain_grad: float32 [768], P(('dp', 'seq'))
- second_shift_grad: float32 [768], P(('dp', 'seq'))
Inputs may be any that keep to these rules, and one draw needn't show every extreme that they name: `lengths`: each length lies in 512 to 2048; some sequence is full and some has exactly 512 valid tokens.
All inputs are finite; a program needn't handle non-finite values.
Results may differ from a plain program's by a relative error of at most 0.018.
Values may be sent and summed in bfloat16 or wider, within the bound.
A program may use at most 192 MiB of HBM per device.

v0:
```python
import jax
import jax.numpy as jnp
from jax import lax
from jax.sharding import PartitionSpec as P

H = 12
HD = 64


EPSILON = 1e-05
ROOT_HALF = 0.7071067811865476
INV_ROOT_TWO_PI = 0.3989422804014327


def matmul(left, right):
    return jnp.dot(left, right, preferred_element_type=jnp.float32)


def left_product(left, right):
    return lax.dot_general(
        left, right, (((0,), (0,)), ((), ())), preferred_element_type=jnp.float32
    )


def right_product(left, right):
    return lax.dot_general(
        left, right, (((1,), (1,)), ((), ())), preferred_element_type=jnp.float32
    )


def normalize(inputs, gains, shifts):
    centre = inputs - jnp.mean(inputs, axis=-1, keepdims=True)
    factor = lax.rsqrt(jnp.mean(centre * centre, axis=-1, keepdims=True) + EPSILON)
    unit_rows = centre * factor
    return (unit_rows * gains + shifts, unit_rows, factor)


def norm_back(grad_in, unit_rows, factor, gains):
    grad_unit = grad_in * gains
    return factor * (
        grad_unit
        - jnp.mean(grad_unit, axis=-1, keepdims=True)
        - unit_rows * jnp.mean(grad_unit * unit_rows, axis=-1, keepdims=True)
    )


def gelu_slope(inputs):
    return 0.5 * (1.0 + lax.erf(inputs * ROOT_HALF)) + inputs * INV_ROOT_TWO_PI * jnp.exp(
        -0.5 * inputs * inputs
    )


def split_heads(array_in):
    return array_in.reshape(array_in.shape[0], array_in.shape[1], H, HD).transpose(2, 0, 1, 3)


def join_heads(array_in):
    return array_in.transpose(1, 2, 0, 3).reshape(array_in.shape[1], array_in.shape[2], H * HD)


def body(
    tokens,
    lengths,
    query_weight,
    key_weight,
    value_weight,
    out_weight,
    up_weight,
    down_weight,
    query_bias,
    value_bias,
    out_bias,
    up_bias,
    down_bias,
    first_gain,
    first_shift,
    second_gain,
    second_shift,
    cotangent,
):
    shards = (
        query_weight,
        key_weight,
        value_weight,
        out_weight,
        up_weight,
        down_weight,
        query_bias,
        value_bias,
        out_bias,
        up_bias,
        down_bias,
        first_gain,
        first_shift,
        second_gain,
        second_shift,
    )
    forward_set = (
        lax.all_gather(shards[0], ("dp", "seq"), axis=0, tiled=True),
        lax.all_gather(shards[1], ("dp", "seq"), axis=0, tiled=True),
        lax.all_gather(shards[2], ("dp", "seq"), axis=0, tiled=True),
        lax.all_gather(shards[3], ("dp", "seq"), axis=0, tiled=True),
        lax.all_gather(shards[4], ("dp", "seq"), axis=0, tiled=True),
        lax.all_gather(shards[5], ("dp", "seq"), axis=0, tiled=True),
        lax.all_gather(shards[6], ("dp", "seq"), axis=0, tiled=True),
        lax.all_gather(shards[7], ("dp", "seq"), axis=0, tiled=True),
        lax.all_gather(shards[8], ("dp", "seq"), axis=0, tiled=True),
        lax.all_gather(shards[9], ("dp", "seq"), axis=0, tiled=True),
        lax.all_gather(shards[10], ("dp", "seq"), axis=0, tiled=True),
        lax.all_gather(shards[11], ("dp", "seq"), axis=0, tiled=True),
        lax.all_gather(shards[12], ("dp", "seq"), axis=0, tiled=True),
        lax.all_gather(shards[13], ("dp", "seq"), axis=0, tiled=True),
        lax.all_gather(shards[14], ("dp", "seq"), axis=0, tiled=True),
    )
    (
        query_full,
        key_full,
        value_full,
        out_full,
        up_full,
        down_full,
        query_add,
        value_add,
        out_add,
        up_add,
        down_add,
        gain_one,
        shift_one,
        gain_two,
        shift_two,
    ) = forward_set
    seq_count, local_len, model_width = tokens.shape
    row_count = seq_count * local_len
    full_len = local_len * lax.axis_size("seq")
    local_pos = lax.axis_index("seq") * local_len + jnp.arange(local_len, dtype=jnp.int32)
    local_live = local_pos[None, :] < lengths[:, None]
    live_rows = local_live.astype(jnp.float32).reshape(row_count, 1)
    key_live = jnp.arange(full_len, dtype=jnp.int32)[None, :] < lengths[:, None]
    flat_in = tokens.reshape(row_count, model_width)
    query_rows = (matmul(flat_in, query_full) + query_add.astype(jnp.float32)).astype(jnp.bfloat16)
    key_rows = matmul(flat_in, key_full).astype(jnp.bfloat16)
    value_rows = (matmul(flat_in, value_full) + value_add.astype(jnp.float32)).astype(jnp.bfloat16)
    key_blocks = key_rows.reshape(seq_count, local_len, model_width)
    value_blocks = value_rows.reshape(seq_count, local_len, model_width)
    query_blocks = query_rows.reshape(seq_count, local_len, model_width)
    keys_all, values_all = (
        lax.all_gather(key_blocks, "seq", axis=1, tiled=True),
        lax.all_gather(value_blocks, "seq", axis=1, tiled=True),
    )
    query_heads = split_heads(query_blocks)
    key_heads = split_heads(keys_all)
    value_heads = split_heads(values_all)

    def masked_scores(query_h, key_h, mask):
        scores = (
            jnp.einsum("sqe,ske->sqk", query_h, key_h, preferred_element_type=jnp.float32) * 0.125
        )
        return jnp.where(mask[:, None, :], scores, -1e30)

    def attend(operands):
        query_h, key_h, value_h = operands
        scores = masked_scores(query_h, key_h, key_live)
        largest = jnp.max(scores, axis=-1, keepdims=True)
        exponent = jnp.exp(scores - largest)
        totals = jnp.sum(exponent, axis=-1, keepdims=True)
        weights_low = (exponent / totals).astype(jnp.bfloat16)
        context_h = jnp.einsum(
            "sqk,ske->sqe", weights_low, value_h, preferred_element_type=jnp.float32
        )
        return (context_h.astype(jnp.bfloat16), (largest + jnp.log(totals))[..., 0])

    context_heads, log_totals = lax.map(attend, (query_heads, key_heads, value_heads))
    context = join_heads(context_heads).reshape(row_count, model_width)
    first_sum = (
        flat_in.astype(jnp.float32) + matmul(context, out_full) + out_add.astype(jnp.float32)
    )
    first_norm, first_unit, first_factor = normalize(
        first_sum, gain_one.astype(jnp.float32), shift_one.astype(jnp.float32)
    )
    first_low = first_norm.astype(jnp.bfloat16)
    up_pre = matmul(first_low, up_full) + up_add.astype(jnp.float32)
    activated = jax.nn.gelu(up_pre, approximate=False).astype(jnp.bfloat16)
    second_sum = (
        first_low.astype(jnp.float32) + matmul(activated, down_full) + down_add.astype(jnp.float32)
    )
    second_norm, second_unit, second_factor = normalize(
        second_sum, gain_two.astype(jnp.float32), shift_two.astype(jnp.float32)
    )
    output = (
        (second_norm * live_rows).astype(jnp.bfloat16).reshape(seq_count, local_len, model_width)
    )
    backward_set = (
        lax.all_gather(shards[0], ("dp", "seq"), axis=0, tiled=True),
        lax.all_gather(shards[1], ("dp", "seq"), axis=0, tiled=True),
        lax.all_gather(shards[2], ("dp", "seq"), axis=0, tiled=True),
        lax.all_gather(shards[3], ("dp", "seq"), axis=0, tiled=True),
        lax.all_gather(shards[4], ("dp", "seq"), axis=0, tiled=True),
        lax.all_gather(shards[5], ("dp", "seq"), axis=0, tiled=True),
        lax.all_gather(shards[6], ("dp", "seq"), axis=0, tiled=True),
        lax.all_gather(shards[7], ("dp", "seq"), axis=0, tiled=True),
        lax.all_gather(shards[8], ("dp", "seq"), axis=0, tiled=True),
        lax.all_gather(shards[9], ("dp", "seq"), axis=0, tiled=True),
        lax.all_gather(shards[10], ("dp", "seq"), axis=0, tiled=True),
        lax.all_gather(shards[11], ("dp", "seq"), axis=0, tiled=True),
        lax.all_gather(shards[12], ("dp", "seq"), axis=0, tiled=True),
        lax.all_gather(shards[13], ("dp", "seq"), axis=0, tiled=True),
        lax.all_gather(shards[14], ("dp", "seq"), axis=0, tiled=True),
    )
    query_back, key_back, value_back, out_back, up_back, down_back = backward_set[0:6]
    gain_one_back = backward_set[11].astype(jnp.float32)
    gain_two_back = backward_set[13].astype(jnp.float32)
    grad_output = cotangent.reshape(row_count, model_width).astype(jnp.float32) * live_rows
    grad_gain_two = jnp.sum(grad_output * second_unit, axis=0)
    grad_shift_two = jnp.sum(grad_output, axis=0)
    grad_second = norm_back(grad_output, second_unit, second_factor, gain_two_back)
    grad_branch = grad_second.astype(jnp.bfloat16)
    grad_down_add = jnp.sum(grad_branch.astype(jnp.float32), axis=0)
    grad_down = left_product(activated, grad_branch)
    grad_up_low = (right_product(grad_branch, down_back) * gelu_slope(up_pre)).astype(jnp.bfloat16)
    grad_up_add = jnp.sum(grad_up_low.astype(jnp.float32), axis=0)
    grad_up = left_product(first_low, grad_up_low)
    grad_first = right_product(grad_up_low, up_back) + grad_second
    grad_gain_one = jnp.sum(grad_first * first_unit, axis=0)
    grad_shift_one = jnp.sum(grad_first, axis=0)
    grad_residual = norm_back(grad_first, first_unit, first_factor, gain_one_back)
    grad_attend = grad_residual.astype(jnp.bfloat16)
    grad_out_add = jnp.sum(grad_attend.astype(jnp.float32), axis=0)
    grad_out = left_product(context, grad_attend)
    grad_context = right_product(grad_attend, out_back).astype(jnp.bfloat16)
    grad_context_blocks = grad_context.reshape(seq_count, local_len, model_width)
    grad_context_heads = split_heads(grad_context_blocks)

    def attend_back(operands):
        query_h, key_h, value_h, grad_h, log_h = operands
        scores = masked_scores(query_h, key_h, key_live)
        exact = jnp.exp(scores - log_h[..., None])
        weights_low = exact.astype(jnp.bfloat16)
        grad_weights = jnp.einsum(
            "sqe,ske->sqk", grad_h, value_h, preferred_element_type=jnp.float32
        )
        grad_value_h = jnp.einsum(
            "sqk,sqe->ske", weights_low, grad_h, preferred_element_type=jnp.float32
        )
        centre_term = jnp.sum(exact * grad_weights, axis=-1, keepdims=True)
        grad_scores = (exact * (grad_weights - centre_term)).astype(jnp.bfloat16)
        grad_query_h = (
            jnp.einsum("sqk,ske->sqe", grad_scores, key_h, preferred_element_type=jnp.float32)
            * 0.125
        )
        grad_key_h = (
            jnp.einsum("sqk,sqe->ske", grad_scores, query_h, preferred_element_type=jnp.float32)
            * 0.125
        )
        return (grad_query_h, grad_key_h, grad_value_h)

    grad_query_heads, grad_key_heads, grad_value_heads = lax.map(
        attend_back, (query_heads, key_heads, value_heads, grad_context_heads, log_totals)
    )
    grad_keys_local, grad_values_local = (
        lax.psum_scatter(
            join_heads(grad_key_heads).astype(jnp.bfloat16), "seq", scatter_dimension=1, tiled=True
        ).astype(jnp.float32),
        lax.psum_scatter(
            join_heads(grad_value_heads).astype(jnp.bfloat16),
            "seq",
            scatter_dimension=1,
            tiled=True,
        ).astype(jnp.float32),
    )
    grad_query_low = (
        join_heads(grad_query_heads).reshape(row_count, model_width).astype(jnp.bfloat16)
    )
    grad_key_low = grad_keys_local.reshape(row_count, model_width).astype(jnp.bfloat16)
    grad_value_low = grad_values_local.reshape(row_count, model_width).astype(jnp.bfloat16)
    grad_query_add = jnp.sum(grad_query_low.astype(jnp.float32), axis=0)
    grad_value_add = jnp.sum(grad_value_low.astype(jnp.float32), axis=0)
    grad_query = left_product(flat_in, grad_query_low)
    grad_key = left_product(flat_in, grad_key_low)
    grad_value = left_product(flat_in, grad_value_low)
    tokens_grad = (
        right_product(grad_query_low, query_back)
        + right_product(grad_key_low, key_back)
        + right_product(grad_value_low, value_back)
        + grad_residual
    )
    owned = (
        lax.psum_scatter(grad_query, ("dp", "seq"), scatter_dimension=0, tiled=True),
        lax.psum_scatter(grad_key, ("dp", "seq"), scatter_dimension=0, tiled=True),
        lax.psum_scatter(grad_value, ("dp", "seq"), scatter_dimension=0, tiled=True),
        lax.psum_scatter(grad_out, ("dp", "seq"), scatter_dimension=0, tiled=True),
        lax.psum_scatter(grad_up, ("dp", "seq"), scatter_dimension=0, tiled=True),
        lax.psum_scatter(grad_down, ("dp", "seq"), scatter_dimension=0, tiled=True),
        lax.psum_scatter(grad_query_add, ("dp", "seq"), scatter_dimension=0, tiled=True),
        lax.psum_scatter(grad_value_add, ("dp", "seq"), scatter_dimension=0, tiled=True),
        lax.psum_scatter(grad_out_add, ("dp", "seq"), scatter_dimension=0, tiled=True),
        lax.psum_scatter(grad_up_add, ("dp", "seq"), scatter_dimension=0, tiled=True),
        lax.psum_scatter(grad_down_add, ("dp", "seq"), scatter_dimension=0, tiled=True),
        lax.psum_scatter(grad_gain_one, ("dp", "seq"), scatter_dimension=0, tiled=True),
        lax.psum_scatter(grad_shift_one, ("dp", "seq"), scatter_dimension=0, tiled=True),
        lax.psum_scatter(grad_gain_two, ("dp", "seq"), scatter_dimension=0, tiled=True),
        lax.psum_scatter(grad_shift_two, ("dp", "seq"), scatter_dimension=0, tiled=True),
    )
    return (output, tokens_grad.reshape(seq_count, local_len, model_width)) + tuple(owned)


def solution(mesh):
    return jax.shard_map(
        body,
        mesh=mesh,
        in_specs=(
            P("dp", "seq", None),
            P("dp"),
            P(("dp", "seq"), None),
            P(("dp", "seq"), None),
            P(("dp", "seq"), None),
            P(("dp", "seq"), None),
            P(("dp", "seq"), None),
            P(("dp", "seq"), None),
            P(("dp", "seq")),
            P(("dp", "seq")),
            P(("dp", "seq")),
            P(("dp", "seq")),
            P(("dp", "seq")),
            P(("dp", "seq")),
            P(("dp", "seq")),
            P(("dp", "seq")),
            P(("dp", "seq")),
            P("dp", "seq", None),
        ),
        out_specs=(
            P("dp", "seq", None),
            P("dp", "seq", None),
            P(("dp", "seq"), None),
            P(("dp", "seq"), None),
            P(("dp", "seq"), None),
            P(("dp", "seq"), None),
            P(("dp", "seq"), None),
            P(("dp", "seq"), None),
            P(("dp", "seq")),
            P(("dp", "seq")),
            P(("dp", "seq")),
            P(("dp", "seq")),
            P(("dp", "seq")),
            P(("dp", "seq")),
            P(("dp", "seq")),
            P(("dp", "seq")),
            P(("dp", "seq")),
        ),
        check_vma=False,
    )
```

profile of v0, /device:TPU:0, one launch (start us, length us, event | category | flops | bytes accessed | tf_op | source)
XLA Modules:
  0.0 1840.4 jit_solution(5184293455723719494)
XLA Ops:
  17.0 42.4 %all-reduce.19 = (bf16[768]{0:T(1024)(128)(2,1)S(1)}, bf16[768]{0:T(1024)(128)(2,1)S(1)}, bf16[768]{0:T(1024)(128)(2,1)S(1)}, bf16[768]{0:T(1024)(128)(2,1)S(1)}...) all-reduce(bf16[768]{0:T(1024)(128)(2,1)S(1)} %dynamic-update-slice, ...), channel_id=1, replica_groups=mesh['dp'=4,'seq'=8] {'dp','seq'}, use_global_device_ids=true, to_apply=%add | all-reduce | flops 9216 | bytes 36864
  73.0 51.1 %all-gather.11.cloned.1.call-done = bf16[768,768]{1,0:T(8,128)(2,1)} async-done(((bf16[24,768]{1,0:T(8,128)(2,1)}), bf16[768,768]{1,0:T(8,128)(2,1)}) %all-gather.11.cloned.1.call-update) | async-done | bytes 1179664 | tf_op jit(solution)/shard_map/all_gather | solution.py:100
  135.0 45.1 %all-gather.9.cloned.1.call-done = bf16[768,768]{1,0:T(8,128)(2,1)} async-done(((bf16[24,768]{1,0:T(8,128)(2,1)}), bf16[768,768]{1,0:T(8,128)(2,1)}) %all-gather.9.cloned.1.call-update) | async-done | bytes 1179664 | tf_op jit(solution)/shard_map/all_gather | solution.py:99
  185.5 112.1 %all-gather.17.cloned.1.call-done = bf16[4,2048,768]{1,2,0:T(8,128)(2,1)} async-done(((bf16[4,256,768]{1,2,0:T(8,128)(2,1)}), bf16[4,2048,768]{1,2,0:T(8,128)(2,1)}) %all-gather.17.cloned.1.call-update) | async-done | bytes 12582928 | tf_op jit(solution)/shard_map/all_gather | solution.py:148
  297.6 11.0 copy.65
  308.6 106.4 %all-gather.13.cloned.1.call-done = bf16[4,2048,768]{1,2,0:T(8,128)(2,1)} async-done(((bf16[4,256,768]{1,2,0:T(8,128)(2,1)}), bf16[4,2048,768]{1,2,0:T(8,128)(2,1)}) %all-gather.13.cloned.1.call-update) | async-done | bytes 12582928 | tf_op jit(solution)/shard_map/all_gather | solution.py:147
  415.0 10.8 copy.64
  425.8 95.6 %while.28 = (s32[]{:T(128)}, bf16[12,4,256,64]{2,3,1,0:T(8,128)(2,1)S(1)}, f32[12,4,256]{2,1,0:T(4,128)S(1)}, bf16[12,4,256,64]{2,3,1,0:T(8,128)(2,1)S(1)}, bf16...) while((s32[]{:T(128)}, ...), condition=%wide.region_3.4_spmd.clone, body=%wide.region_0.3_spmd.clone.sunk | while | flops 562109440 | bytes 27592816 | solution.py:172
  535.8 37.4 %fusion.55 = (bf16[1024,3072]{1,0:T(8,128)(2,1)}, f32[1024,3072]{1,0:T(8,128)}) fusion(f32[3072]{0:T(1024)S(1)} %convert_element_type.171, bf16[768,3072]{1,0:T(8,128)(2,1)} %all-gather.21.cloned.1.call-done, f32[1024,768]{1,0:T(8,128)S(1)} %get-tuple-element.311, f32[768]{0:T(1024)S(1)} %convert_element_type.168, f32[768]{0:T(1024)S(1)} %convert_element_type.167, ...), kind=kOutput, calls=%fused_computation.64 | convolution fusion | flops 5043388416 | bytes 26765312 | tf_op jit(solution)/shard_map/dot_general | solution.py:16
  573.2 27.7 %all-gather.23.cloned.1.call-done = bf16[3072,768]{1,0:T(8,128)(2,1)} async-done(((bf16[96,768]{1,0:T(8,128)(2,1)}), bf16[3072,768]{1,0:T(8,128)(2,1)}) %all-gather.23.cloned.1.call-update) | async-done | bytes 4718608 | tf_op jit(solution)/shard_map/all_gather | solution.py:104
  600.9 8.8 fusion.78
  616.6 13.5 convert_reduce_fusion
  649.1 226.7 %while.29 = (s32[]{:T(128)}, bf16[12,4,256,64]{2,3,1,0:T(8,128)(2,1)}, bf16[12,4,2048,64]{2,3,0,1:T(8,128)(2,1)}, bf16[12,4,2048,64]{2,3,0,1:T(8,128)(2,1)}, bf1...) while((s32[]{:T(128)}, ...), condition=%wide.region_14.15_spmd.clone, body=%wide.region_12.14_spmd.clone.sunk | while | flops 1374231552 | bytes 71367824 | solution.py:256
  892.2 11.1 fusion.79
  905.1 10.3 fusion.73
  915.5 87.9 %reduce-scatter.17.cloned.1.call-done = bf16[4,256,768]{1,2,0:T(8,128)(2,1)} async-done(((bf16[4,2048,768]{1,2,0:T(8,128)(2,1)}), bf16[4,256,768]{1,2,0:T(8,128)(2,1)}) %reduce-scatter.17.cloned.1.call-update) | async-done | bytes 1572880 | tf_op jit(solution)/shard_map/reduce_scatter | solution.py:263
  1008.7 124.5 %reduce-scatter.15.cloned.1.call-done = bf16[4,256,768]{1,2,0:T(8,128)(2,1)} async-done(((bf16[4,2048,768]{1,2,0:T(8,128)(2,1)}), bf16[4,256,768]{1,2,0:T(8,128)(2,1)}) %reduce-scatter.15.cloned.1.call-update) | async-done | bytes 1572880 | tf_op jit(solution)/shard_map/reduce_scatter | solution.py:260
  1147.4 38.9 %all-reduce.18 = (f32[768]{0:T(1024)S(1)}, f32[768]{0:T(1024)S(1)}, f32[768]{0:T(1024)S(1)}, f32[3072]{0:T(1024)S(1)}, f32[768]{0:T(1024)S(1)}, /*index=5*/f32[7...) all-reduce(f32[768]{0:T(1024)S(1)} %reduce_sum.182, ...), channel_id=10, replica_groups=mesh['dp'=4,'seq'=8] {'dp','seq'}, use_global_device_ids=true, to_apply=%region_24.25.clone | all-reduce | flops 9216 | bytes 73728
  1200.8 36.5 %reduce-scatter.19.cloned.1.call-done = f32[24,768]{1,0:T(8,128)} async-done(((f32[768,768]{1,0:T(8,128)}), f32[24,768]{1,0:T(8,128)}) %reduce-scatter.19.cloned.1.call-update) | async-done | bytes 73744 | tf_op jit(solution)/shard_map/reduce_scatter | solution.py:290
  1237.2 104.3 %reduce-scatter.25.cloned.1.call-done = f32[24,768]{1,0:T(8,128)} async-done(((f32[768,768]{1,0:T(8,128)}), f32[24,768]{1,0:T(8,128)}) %reduce-scatter.25.cloned.1.call-update) | async-done | bytes 73744
  1341.5 141.7 %reduce-scatter.21.cloned.1.call-done = f32[24,3072]{1,0:T(8,128)} async-done(((f32[768,3072]{1,0:T(8,128)}), f32[24,3072]{1,0:T(8,128)}) %reduce-scatter.21.cloned.1.call-update) | async-done | bytes 294928 | tf_op jit(solution)/shard_map/reduce_scatter | solution.py:291
  1483.3 141.5 %reduce-scatter.23.cloned.1.call-done = f32[96,768]{1,0:T(8,128)} async-done(((f32[3072,768]{1,0:T(8,128)}), f32[96,768]{1,0:T(8,128)}) %reduce-scatter.23.cloned.1.call-update) | async-done | bytes 294928 | tf_op jit(solution)/shard_map/reduce_scatter | solution.py:292
  1624.8 104.2 %reduce-scatter.29.cloned.1.call-done = f32[24,768]{1,0:T(8,128)} async-done(((f32[768,768]{1,0:T(8,128)}), f32[24,768]{1,0:T(8,128)}) %reduce-scatter.29.cloned.1.call-update) | async-done | bytes 73744
  1729.0 104.4 %reduce-scatter.27.cloned.1.call-done = f32[24,768]{1,0:T(8,128)} async-done(((f32[768,768]{1,0:T(8,128)}), f32[24,768]{1,0:T(8,128)}) %reduce-scatter.27.cloned.1.call-update) | async-done | bytes 73744
  (366 shorter events, 452.8 us)
Async XLA Ops:
  7.2 61.0 %all-gather.15.cloned.1.call-start = ((), (), s32[]{:S(2)}) async-start(), calls=%async_computation.11 | async-start | bytes 1216512 | tf_op jit(solution)/shard_map/all_gather | solution.py:101
  7.9 116.1 %all-gather.11.cloned.1.call-start = ((), (), s32[]{:S(2)}) async-start(), calls=%async_computation.9 | async-start | bytes 1216512 | tf_op jit(solution)/shard_map/all_gather | solution.py:100
  8.7 171.4 %all-gather.9.cloned.1.call-start = ((), (), s32[]{:S(2)}) async-start(), calls=%async_computation.8 | async-start | bytes 1216512 | tf_op jit(solution)/shard_map/all_gather | solution.py:99
  9.4 288.2 %all-gather.17.cloned.1.call-start = ((), (), s32[]{:S(2)}) async-start(), calls=%async_computation.12 | async-start | bytes 14155776 | tf_op jit(solution)/shard_map/all_gather | solution.py:148
  72.9 342.0 %all-gather.13.cloned.1.call-start = ((), (), s32[]{:S(2)}) async-start(), calls=%async_computation.10 | async-start | bytes 14155776 | tf_op jit(solution)/shard_map/all_gather | solution.py:147
  127.2 5.9 copy-start
  128.8 395.4 %all-gather.19.cloned.1.call-start = ((), (), s32[]{:S(2)}) async-start(), calls=%async_computation.13 | async-start | bytes 1216512 | tf_op jit(solution)/shard_map/all_gather | solution.py:102
  129.4 406.5 %all-gather.21.cloned.1.call-start = ((), (), s32[]{:S(2)}) async-start(), calls=%async_computation.14 | async-start | bytes 4866048 | tf_op jit(solution)/shard_map/all_gather | solution.py:103
  130.1 470.8 %all-gather.23.cloned.1.call-start = ((), (), s32[]{:S(2)}) async-start(), calls=%async_computation.15 | async-start | bytes 4866048 | tf_op jit(solution)/shard_map/all_gather | solution.py:104
  130.9 872.6 %reduce-scatter.17.cloned.1.call-start = ((), (), s32[]{:S(2)}) async-start(), calls=%async_computation.17 | async-start | bytes 14155776 | tf_op jit(solution)/shard_map/reduce_scatter | solution.py:263
  131.2 469.7 %copy-start.15 = (f32[768]{0:T(1024)}, f32[768]{0:T(1024)S(1)}, u32[]{:S(2)}) copy-start(f32[768]{0:T(1024)S(1)} %convert_element_type.168) | copy-start | bytes 9220
  415.0 10.8 copy-start.13
  528.6 72.4 %copy-start.28 = (f32[768]{0:T(1024)S(1)}, f32[768]{0:T(1024)}, u32[]{:S(2)}) copy-start(f32[768]{0:T(1024)} %convert_element_type.173) | copy-start | bytes 9220
  613.3 16.7 slice-start
  616.6 13.5 copy-start.8
  616.6 13.5 slice-start.1
  630.0 6.5 copy-start.5
  875.8 257.4 %reduce-scatter.15.cloned.1.call-start = ((), (), s32[]{:S(2)}) async-start(), calls=%async_computation.16 | async-start | bytes 14155776 | tf_op jit(solution)/shard_map/reduce_scatter | solution.py:260
  876.4 360.8 %reduce-scatter.19.cloned.1.call-start = ((), (), s32[]{:S(2)}) async-start(), calls=%async_computation.18 | async-start | bytes 2433024 | tf_op jit(solution)/shard_map/reduce_scatter | solution.py:290
  881.7 459.9 %reduce-scatter.25.cloned.1.call-start = ((), (), s32[]{:S(2)}) async-start(), calls=%async_computation.21 | async-start | bytes 2433024
  892.1 591.2 %reduce-scatter.21.cloned.1.call-start = ((), (), s32[]{:S(2)}) async-start(), calls=%async_computation.19 | async-start | bytes 9732096 | tf_op jit(solution)/shard_map/reduce_scatter | solution.py:291
  903.2 721.5 %reduce-scatter.23.cloned.1.call-start = ((), (), s32[]{:S(2)}) async-start(), calls=%async_computation.20 | async-start | bytes 9732096 | tf_op jit(solution)/shard_map/reduce_scatter | solution.py:292
  915.4 813.5 %reduce-scatter.29.cloned.1.call-start = ((), (), s32[]{:S(2)}) async-start(), calls=%async_computation.23 | async-start | bytes 2433024
  1008.7 824.7 %reduce-scatter.27.cloned.1.call-start = ((), (), s32[]{:S(2)}) async-start(), calls=%async_computation.22 | async-start | bytes 2433024
  (28 other events, 93.8 us)
Sparse Core Ops, SparseCore 0:
  11.0 57.0 all-gather.14
  71.2 52.8 all-gather.10
  127.1 52.9 all-gather.8
  181.5 116.0 all-gather.16
  299.6 115.3 all-gather.12
  417.8 52.3 all-gather.18
  473.2 62.5 all-gather.20
  538.8 62.0 all-gather.22
  875.9 127.4 reduce-scatter.16
  1005.6 127.6 reduce-scatter.14
  1139.1 98.0 reduce-scatter.18
  1242.9 98.5 reduce-scatter.24
  1348.0 135.2 reduce-scatter.20
  1489.6 135.1 reduce-scatter.22
  1630.5 98.4 reduce-scatter.28
  1734.7 98.6 reduce-scatter.26
where the time goes:
time: 1850 us; the launch traced here: 1840 us
  waiting for transfers between devices  1210 us (65%)
  matrix products  385 us (21%)
  local copies, waits for them, and re-layouts  83.2 us (4%)
  blocking collectives  81.4 us (4%)
  other arithmetic  65.5 us (4%)
    unnamed x19, waiting for transfers between devices  318 us
    reduce_scatter x1, waiting for transfers between devices, body(): lax.psum_scatter(grad_up, ('dp', 'seq'), scatter_dimension=0, tiled=True)  142 us
    reduce_scatter x1, waiting for transfers between devices, body(): lax.psum_scatter(grad_down, ('dp', 'seq'), scatter_dimension=0, tiled=True)  141 us
    reduce_scatter x1, waiting for transfers between devices, body(): lax.psum_scatter(join_heads(grad_key_heads).astype(jnp.bfloat16), 'seq',...  125 us
    all_gather x1, waiting for transfers between devices, body(): lax.all_gather(value_blocks, 'seq', axis=1, tiled=True)  112 us
    all_gather x1, waiting for transfers between devices, body(): lax.all_gather(key_blocks, 'seq', axis=1, tiled=True)  106 us
    reduce_scatter x1, waiting for transfers between devices, body(): lax.psum_scatter(join_heads(grad_value_heads).astype(jnp.bfloat16), 'seq'...  87.9 us
    unnamed x2, blocking collectives  81.4 us
  transfers between devices with their start and end apart: 16, of which 15 were waited for; matrix products, arithmetic and copies ran while one was open for 14% of the time, Pallas kernels for 0%

commit v1 on v0

v1 whole, which is shorter than its diff:
```python
import jax
import jax.numpy as jnp
from jax import lax
from jax.experimental import pallas as pl
from jax.experimental.pallas import tpu as pltpu
from jax.sharding import PartitionSpec as P

H = 12
HD = 64

EPSILON = 1e-05
ROOT_HALF = 0.7071067811865476
INV_ROOT_TWO_PI = 0.3989422804014327
BF = jnp.bfloat16
F32 = jnp.float32


def matmul(left, right):
    return jnp.dot(left, right, preferred_element_type=F32)


def left_product(left, right):
    return lax.dot_general(left, right, (((0,), (0,)), ((), ())), preferred_element_type=F32)


def right_product(left, right):
    return lax.dot_general(left, right, (((1,), (1,)), ((), ())), preferred_element_type=F32)


def normalize(inputs, gains, shifts):
    centre = inputs - jnp.mean(inputs, axis=-1, keepdims=True)
    factor = lax.rsqrt(jnp.mean(centre * centre, axis=-1, keepdims=True) + EPSILON)
    unit_rows = centre * factor
    return (unit_rows * gains + shifts, unit_rows, factor)


def norm_back(grad_in, unit_rows, factor, gains):
    grad_unit = grad_in * gains
    return factor * (
        grad_unit
        - jnp.mean(grad_unit, axis=-1, keepdims=True)
        - unit_rows * jnp.mean(grad_unit * unit_rows, axis=-1, keepdims=True)
    )


def gelu_slope(inputs):
    return 0.5 * (1.0 + lax.erf(inputs * ROOT_HALF)) + inputs * INV_ROOT_TWO_PI * jnp.exp(
        -0.5 * inputs * inputs
    )


def swap_index(place, step, count):
    if count & (count - 1) == 0:
        return place ^ step
    return (place + step) % count


def source_index(place, step, count):
    if count & (count - 1) == 0:
        return place ^ step
    return (place - step) % count


class Grid:
    def __init__(self, seqs):
        self.columns = lax.axis_size("dp")
        self.n = lax.axis_size("seq")
        self.seqs = seqs
        self.group = self.n // seqs
        self.chips = self.n // 2
        self.column = lax.axis_index("dp")
        place = lax.axis_index("seq")
        self.chip = place // 2
        self.core = place % 2
        self.owner = place // self.group
        self.member = place % self.group

    def to_chip(self, array_in, step):
        pairs = [(s, swap_index(s // 2, step, self.chips) * 2 + s % 2) for s in range(self.n)]
        return lax.ppermute(array_in, "seq", pairs)

    def to_column(self, array_in, step):
        pairs = [(s, swap_index(s, step, self.columns)) for s in range(self.columns)]
        return lax.ppermute(array_in, "dp", pairs)

    def to_core(self, array_in):
        return lax.ppermute(array_in, "seq", [(s, s ^ 1) for s in range(self.n)])

    def to_owner(self, array_in, step, back=False):
        move = source_index if back else swap_index
        pairs = [
            (s, move(s // self.group, step, self.seqs) * self.group + s % self.group)
            for s in range(self.n)
        ]
        return lax.ppermute(array_in, "seq", pairs)

    def to_member(self, array_in, step, back=False):
        shift = -step if back else step
        pairs = [
            (s, (s // self.group) * self.group + (s % self.group + shift) % self.group)
            for s in range(self.n)
        ]
        return lax.ppermute(array_in, "seq", pairs)


def take_block(array_in, index):
    return lax.dynamic_index_in_dim(array_in, index, 0, keepdims=False)


def to_sequences(grid, array_in):
    parts = [take_block(array_in, grid.owner)]
    for step in range(1, grid.seqs):
        target = swap_index(grid.owner, step, grid.seqs)
        parts.append(grid.to_owner(take_block(array_in, target), step))
    return jnp.concatenate(parts, axis=0)


def from_sequences(grid, rows, length):
    blocks = rows.reshape(grid.seqs, length, rows.shape[1])
    out = jnp.zeros_like(blocks)
    out = lax.dynamic_update_index_in_dim(out, blocks[0], grid.owner, 0)
    for step in range(1, grid.seqs):
        got = grid.to_owner(blocks[step], step, back=True)
        place = swap_index(grid.owner, step, grid.seqs)
        out = lax.dynamic_update_index_in_dim(out, got, place, 0)
    return out


def row_positions(grid, length):
    def positions(member):
        spots = []
        for step in range(grid.seqs):
            source = source_index(grid.owner, step, grid.seqs)
            spots.append((source * grid.group + member) * length + jnp.arange(length, dtype=jnp.int32))
        return jnp.concatenate(spots)

    return positions


def gather_packed(grid, shard):
    parts = [shard] + [grid.to_chip(shard, step) for step in range(1, grid.chips)]
    chips = jnp.stack(parts)
    wide = [chips] + [grid.to_column(chips, step) for step in range(1, grid.columns)]
    mine = jnp.concatenate(wide, axis=0)
    other = grid.to_core(mine)
    return mine, other


def relative_order(grid):
    column = jnp.arange(grid.columns, dtype=jnp.int32)[:, None]
    chip = jnp.arange(grid.chips, dtype=jnp.int32)[None, :]
    if grid.columns & (grid.columns - 1) == 0:
        column_step = column ^ grid.column
    else:
        column_step = (grid.column - column) % grid.columns
    if grid.chips & (grid.chips - 1) == 0:
        chip_step = chip ^ grid.chip
    else:
        chip_step = (grid.chip - chip) % grid.chips
    return (column_step * grid.chips + chip_step).reshape(-1)


def assemble(grid, mine, other, cuts):
    order = relative_order(grid)
    count, rows, width = mine.shape
    spot = jnp.concatenate([grid.core[None].astype(jnp.int32), order])
    if any(cut[1] % 8 for cut in cuts):
        first = jnp.where(grid.core == 0, mine, other)[order]
        second = jnp.where(grid.core == 0, other, mine)[order]
        both = jnp.stack([first, second], axis=1).reshape(2 * count, rows, width)
        outs = []
        for start, height, blocks in cuts:
            piece = both[:, start : start + height * blocks]
            piece = piece.reshape(2 * count, blocks, height, width).transpose(0, 2, 1, 3)
            outs.append(piece.reshape(2 * count * height, blocks * width))
        return outs

    def kernel(spot_ref, mine_ref, other_ref, *out_refs):
        for core in range(2):

            @pl.when(spot_ref[0] == core)
            def _(core=core):
                for source, place in ((mine_ref, core), (other_ref, 1 - core)):
                    for (start, height, blocks), out_ref in zip(cuts, out_refs):
                        for block in range(blocks):
                            out_ref[
                                place * height : (place + 1) * height,
                                block * width : (block + 1) * width,
                            ] = source[start + block * height : start + (block + 1) * height, :]

    return pl.pallas_call(
        kernel,
        grid_spec=pltpu.PrefetchScalarGridSpec(
            num_scalar_prefetch=1,
            grid=(count,),
            in_specs=[
                pl.BlockSpec((None, rows, width), lambda i, spot: (spot[i + 1], 0, 0)),
                pl.BlockSpec((None, rows, width), lambda i, spot: (spot[i + 1], 0, 0)),
            ],
            out_specs=[
                pl.BlockSpec((2 * height, blocks * width), lambda i, spot: (i, 0))
                for _, height, blocks in cuts
            ],
        ),
        out_shape=[
            jax.ShapeDtypeStruct((2 * count * height, blocks * width), mine.dtype)
            for _, height, blocks in cuts
        ],
        name="assemble",
    )(spot, mine, other)


def scatter_sum(grid, array_in):
    width = array_in.shape[1]
    blocks = array_in.reshape(grid.columns * grid.chips, 2, -1, width)
    keep = lax.dynamic_index_in_dim(blocks, grid.core, 1, keepdims=False)
    send = lax.dynamic_index_in_dim(blocks, 1 - grid.core, 1, keepdims=False)
    half = (keep.astype(F32) + grid.to_core(send).astype(F32)).astype(BF)
    half = half.reshape(grid.columns, -1, width)
    total = take_block(half, grid.column).astype(F32)
    for step in range(1, grid.columns):
        target = swap_index(grid.column, step, grid.columns)
        total = total + grid.to_column(take_block(half, target), step).astype(F32)
    part = total.astype(BF).reshape(grid.chips, -1, width)
    total = take_block(part, grid.chip).astype(F32)
    for step in range(1, grid.chips):
        target = swap_index(grid.chip, step, grid.chips)
        total = total + grid.to_chip(take_block(part, target), step).astype(F32)
    return total


def split_heads(rows):
    return rows.reshape(rows.shape[0], H, HD).transpose(1, 0, 2)


def join_heads(heads):
    return heads.transpose(1, 0, 2).reshape(heads.shape[1], H * HD)


def attention(query, keys, values, key_bias):
    def attend(operands):
        query_h, key_h, value_h = operands
        scores = right_product(query_h, key_h) * 0.125 + key_bias[None, :]
        largest = jnp.max(scores, axis=-1, keepdims=True)
        exponent = jnp.exp(scores - largest)
        totals = jnp.sum(exponent, axis=-1, keepdims=True)
        context_h = matmul((exponent / totals).astype(BF), value_h)
        return (context_h.astype(BF), (largest + jnp.log(totals))[..., 0])

    context, log_totals = lax.map(attend, (split_heads(query), split_heads(keys), split_heads(values)))
    return join_heads(context), log_totals


def attention_back(query, keys, values, key_bias, log_totals, grad_context):
    def attend_back(operands):
        query_h, key_h, value_h, grad_h, log_h = operands
        scores = right_product(query_h, key_h) * 0.125 + key_bias[None, :]
        exact = jnp.exp(scores - log_h[..., None])
        grad_weights = right_product(grad_h, value_h)
        grad_value_h = left_product(exact.astype(BF), grad_h)
        centre_term = jnp.sum(exact * grad_weights, axis=-1, keepdims=True)
        grad_scores = (exact * (grad_weights - centre_term)).astype(BF)
        grad_query_h = matmul(grad_scores, key_h) * 0.125
        grad_key_h = left_product(grad_scores, query_h) * 0.125
        return (grad_query_h.astype(BF), grad_key_h.astype(BF), grad_value_h.astype(BF))

    heads = tuple(split_heads(a) for a in (query, keys, values, grad_context))
    grads = lax.map(attend_back, heads + (log_totals,))
    return tuple(join_heads(a) for a in grads)


def body(
    tokens,
    lengths,
    query_weight,
    key_weight,
    value_weight,
    out_weight,
    up_weight,
    down_weight,
    query_bias,
    value_bias,
    out_bias,
    up_bias,
    down_bias,
    first_gain,
    first_shift,
    second_gain,
    second_shift,
    cotangent,
):
    seqs, length, width = tokens.shape
    grid = Grid(seqs)
    devices = grid.columns * grid.n
    slim = query_weight.shape[0]
    hidden = up_weight.shape[1]
    tall = hidden // devices
    wide = hidden // width

    flat_in = to_sequences(grid, tokens)

    vectors = (
        query_bias,
        value_bias,
        out_bias,
        down_bias,
        first_gain,
        first_shift,
        second_gain,
        second_shift,
    )
    vector_row = jnp.concatenate(vectors + (up_bias,))
    vector_size = vector_row.shape[0]
    vector_rows = jnp.zeros((8, width), BF).at[0, :vector_size].set(vector_row)
    early = jnp.concatenate([query_weight, key_weight, value_weight, vector_rows], axis=0)
    late = jnp.concatenate(
        [out_weight]
        + [up_weight[:, i * width : (i + 1) * width] for i in range(wide)]
        + [down_weight],
        axis=0,
    )
    mine, other = gather_packed(grid, early)
    into_full, vector_full = assemble(
        grid, mine, other, ((0, slim, 3), (3 * slim, 8, 1))
    )
    late_mine, late_other = gather_packed(grid, late)
    out_full, up_full, down_full = assemble(
        grid,
        late_mine,
        late_other,
        ((0, slim, 1), (slim, slim, wide), (slim * (1 + wide), tall, 1)),
    )
    vector_table = vector_full.reshape(devices, 8, width)[:, 0, :vector_size]
    small = vector_table[:, : 8 * slim].reshape(devices, 8, slim).transpose(1, 0, 2)
    small = small.reshape(8, width).astype(F32)
    query_add, value_add, out_add, down_add, gain_one, shift_one, gain_two, shift_two = (
        small[i] for i in range(8)
    )
    up_add = vector_table[:, 8 * slim :].reshape(hidden).astype(F32)

    positions = row_positions(grid, length)
    my_length = take_block(lengths, grid.owner)
    live_rows = (positions(grid.member) < my_length).astype(F32)[:, None]
    key_bias = jnp.concatenate(
        [
            jnp.where(positions((grid.member - step) % grid.group) < my_length, 0.0, -1e30)
            for step in range(grid.group)
        ]
    ).astype(F32)

    into = matmul(flat_in, into_full)
    query = (into[:, :width] + query_add).astype(BF)
    key_value = jnp.concatenate([into[:, width : 2 * width], into[:, 2 * width :] + value_add], axis=1)
    key_value = key_value.astype(BF)
    key_value_all = jnp.concatenate(
        [key_value] + [grid.to_member(key_value, step) for step in range(1, grid.group)], axis=0
    )
    keys, values = key_value_all[:, :width], key_value_all[:, width:]

    context, log_totals = attention(query, keys, values, key_bias)
    grad_in = to_sequences(grid, cotangent)

    first_sum = flat_in.astype(F32) + matmul(context, out_full) + out_add
    first_norm, first_unit, first_factor = normalize(first_sum, gain_one, shift_one)
    first_low = first_norm.astype(BF)
    up_pre = matmul(first_low, up_full) + up_add
    activated = jax.nn.gelu(up_pre, approximate=False).astype(BF)
    second_sum = first_low.astype(F32) + matmul(activated, down_full) + down_add
    second_norm, second_unit, second_factor = normalize(second_sum, gain_two, shift_two)
    output = from_sequences(grid, (second_norm * live_rows).astype(BF), length)

    grad_output = grad_in.astype(F32) * live_rows
    grad_gain_two = jnp.sum(grad_output * second_unit, axis=0)
    grad_shift_two = jnp.sum(grad_output, axis=0)
    grad_second = norm_back(grad_output, second_unit, second_factor, gain_two)
    grad_branch = grad_second.astype(BF)
    grad_down_add = jnp.sum(grad_branch.astype(F32), axis=0)
    grad_down = left_product(activated, grad_branch).astype(BF)
    grad_up_low = (right_product(grad_branch, down_full) * gelu_slope(up_pre)).astype(BF)
    grad_up_add = jnp.sum(grad_up_low.astype(F32), axis=0)
    grad_up = left_product(first_low, grad_up_low).astype(BF)
    grad_first = right_product(grad_up_low, up_full) + grad_second
    grad_gain_one = jnp.sum(grad_first * first_unit, axis=0)
    grad_shift_one = jnp.sum(grad_first, axis=0)
    grad_residual = norm_back(grad_first, first_unit, first_factor, gain_one)
    grad_attend = grad_residual.astype(BF)
    grad_out_add = jnp.sum(grad_attend.astype(F32), axis=0)
    grad_out = left_product(context, grad_attend).astype(BF)
    grad_context = right_product(grad_attend, out_full).astype(BF)

    grad_down_own = scatter_sum(grid, grad_down)
    grad_up_own = scatter_sum(grid, grad_up)
    grad_out_own = scatter_sum(grid, grad_out)

    grad_query_low, grad_keys, grad_values = attention_back(
        query, keys, values, key_bias, log_totals, grad_context
    )
    rows = seqs * length
    grad_kv = jnp.concatenate([grad_keys, grad_values], axis=1)
    grad_kv_sum = grad_kv[:rows].astype(F32)
    for step in range(1, grid.group):
        piece = grad_kv[step * rows : (step + 1) * rows]
        grad_kv_sum = grad_kv_sum + grid.to_member(piece, step, back=True).astype(F32)
    grad_kv_low = grad_kv_sum.astype(BF)
    grad_into_low = jnp.concatenate([grad_query_low, grad_kv_low], axis=1)
    grad_query_add = jnp.sum(grad_query_low.astype(F32), axis=0)
    grad_value_add = jnp.sum(grad_kv_low[:, width:].astype(F32), axis=0)
    tokens_grad = right_product(grad_into_low, into_full) + grad_residual
    tokens_grad = from_sequences(grid, tokens_grad.astype(BF), length).astype(F32)
    grad_into = left_product(flat_in, grad_into_low).astype(BF)
    grad_into_own = scatter_sum(grid, grad_into)

    small_grads = jnp.stack(
        [
            grad_query_add,
            grad_value_add,
            grad_out_add,
            grad_down_add,
            grad_gain_one,
            grad_shift_one,
            grad_gain_two,
            grad_shift_two,
        ]
    )
    small_grads = small_grads.reshape(8, devices, slim).transpose(1, 0, 2).reshape(devices, 8 * slim)
    vector_grads = jnp.concatenate([small_grads, grad_up_add.reshape(devices, tall)], axis=1).astype(BF)
    vector_own = scatter_sum(grid, vector_grads)[0]
    vector_outs = [vector_own[i * slim : (i + 1) * slim] for i in range(8)]
    up_add_own = vector_own[8 * slim :]
    return (
        output,
        tokens_grad,
        grad_into_own[:, :width],
        grad_into_own[:, width : 2 * width],
        grad_into_own[:, 2 * width :],
        grad_out_own,
        grad_up_own,
        grad_down_own,
        vector_outs[0],
        vector_outs[1],
        vector_outs[2],
        up_add_own,
        vector_outs[3],
        vector_outs[4],
        vector_outs[5],
        vector_outs[6],
        vector_outs[7],
    )


def solution(mesh):
    whole = ("dp", "seq")
    matrix, vector, rows = P(whole, None), P(whole), P("dp", "seq", None)
    return jax.shard_map(
        body,
        mesh=mesh,
        in_specs=(rows, P("dp")) + (matrix,) * 6 + (vector,) * 9 + (rows,),
        out_specs=(rows, rows) + (matrix,) * 6 + (vector,) * 9,
        check_vma=False,
    )
```

time: 1850 us -> 986 us (0.53)
  waiting for transfers between devices: 1210 us -> 160 us
  local copies, waits for them, and re-layouts: 83.2 us -> 188 us
  starting transfers between devices: 0.85 us -> 102 us
  blocking collectives: 81.4 us -> 0 us
  other arithmetic: 65.5 us -> 116 us
  Pallas kernels: 0 us -> 25.3 us
    reduce_scatter x5 -> x0, waiting for transfers between devices: 532 us -> none  [the longest x1 142 us: body(): lax.psum_scatter(grad_up, ('dp', 'seq'), scatter_dimension=0, tiled=True)]
    all_gather x8 -> x0, waiting for transfers between devices: 358 us -> none  [the longest x1 112 us: body(): lax.all_gather(value_blocks, 'seq', axis=1, tiled=True)]
    unnamed x19 -> x0, waiting for transfers between devices: 318 us -> none
    ppermute x0 -> x63, waiting for transfers between devices: none -> 160 us  [the longest x21 88.6 us: to_column(): return lax.ppermute(array_in, 'dp', pairs)]
    dot_general x90 -> x28, matrix products: 315 us -> 166 us  [matmul(): return jnp.dot(left, right, preferred_element_type=F32)]
    ppermute x0 -> x63, starting transfers between devices: none -> 102 us  [the longest x21 41.9 us: to_chip(): return lax.ppermute(array_in, 'seq', pairs)]
    dot_general x6 -> x40, matrix products: 33 us -> 127 us  [right_product(): lax.dot_general(left, right, (((1,), (1,)), ((), ())), preferred_element_...]
    unnamed x2 -> x0, blocking collectives: 81.4 us -> none
  transfers between devices with their start and end apart: 16 -> 63, of which waited for: 15 -> 21; matrix products, arithmetic and copies ran while one was open for 14% -> 38% of each run, Pallas kernels for 0% -> 3%
where the time goes in v1:
time: 986 us; the launch traced here: 975 us
  matrix products  381 us (39%)
  local copies, waits for them, and re-layouts  188 us (19%)
  waiting for transfers between devices  160 us (16%)
  other arithmetic  116 us (12%)
  starting transfers between devices  102 us (10%)
  Pallas kernels  25.3 us (3%)
    dot_general x28, matrix products, matmul(): return jnp.dot(left, right, preferred_element_type=F32)  166 us
    dot_general x40, matrix products, right_product(): lax.dot_general(left, right, (((1,), (1,)), ((), ())), preferred_element_...  127 us
    ppermute x21, waiting for transfers between devices, to_column(): return lax.ppermute(array_in, 'dp', pairs)  88.6 us
    dot_general x28, matrix products, left_product(): lax.dot_general(left, right, (((0,), (0,)), ((), ())), preferred_element_...  87.9 us
    ppermute x21, waiting for transfers between devices, to_chip(): return lax.ppermute(array_in, 'seq', pairs)  44.2 us
    ppermute x21, starting transfers between devices, to_chip(): return lax.ppermute(array_in, 'seq', pairs)  41.9 us
    ppermute x12, starting transfers between devices, to_owner(): return lax.ppermute(array_in, 'seq', pairs)  32.5 us
    unnamed x112, local copies, waits for them, and re-layouts  32.5 us
  transfers between devices with their start and end apart: 63, of which 21 were waited for; matrix products, arithmetic and copies ran while one was open for 38% of the time, Pallas kernels for 3%

profile of v1, /device:TPU:0, one launch (start us, length us, event | category | flops | bytes accessed | tf_op | source)
XLA Modules:
  0.0 975.1 jit_solution(17530818118841304484)
XLA Ops:
  15.4 7.6 collective-permute-done.4
  26.7 10.6 %collective-permute-done.6 = bf16[4,80,768]{2,1,0:T(8,128)(2,1)S(1)} collective-permute-done((bf16[4,80,768]{2,1,0:T(8,128)(2,1)S(1)}, bf16[4,80,768]{2,1,0:T(8,128)(2,1)S(1)}, u32[]{:S(2)}, u32[]{:S(2)}) %collective-permute-start.6) | collective-permute-done | bytes 491552 | tf_op jit(solution)/shard_map/ppermute | solution.py:84
  37.3 8.2 collective-permute-done.7
  76.0 11.2 %assemble.2 = (bf16[768,2304]{1,0:T(8,128)(2,1)}, bf16[256,768]{1,0:T(8,128)(2,1)}) custom-call(s32[17]{0:T(128)} %pad_add_fusion.spot_ref, bf16[16,80,768]{2,1,0:T(8,128)(2,1)} %copy-done.17, bf16[16,80,768]{2,1,0:T(8,128)(2,1)} %collective-permute-done.9.other_ref), custom_call_target="tpu_custom_call" | custom-call | tf_op jit(solution)/shard_map/assemble/pallas_call | solution.py:191
  102.6 13.4 %collective-permute-done.12 = bf16[216,768]{1,0:T(8,128)(2,1)S(1)} collective-permute-done((bf16[216,768]{1,0:T(8,128)(2,1)}, bf16[216,768]{1,0:T(8,128)(2,1)S(1)}, u32[]{:S(2)}, u32[]{:S(2)}) %collective-permute-start.12) | collective-permute-done | bytes 331808 | tf_op jit(solution)/shard_map/ppermute | solution.py:80
  132.9 17.8 %collective-permute-done.14 = bf16[4,216,768]{2,1,0:T(8,128)(2,1)} collective-permute-done((bf16[4,216,768]{2,1,0:T(8,128)(2,1)}, bf16[4,216,768]{2,1,0:T(8,128)(2,1)}, u32[]{:S(2)}, u32[]{:S(2)}) %collective-permute-start.14) | collective-permute-done | bytes 1327136 | tf_op jit(solution)/shard_map/ppermute | solution.py:84
  150.8 7.8 collective-permute-start.22
  161.0 18.3 %collective-permute-done.15 = bf16[4,216,768]{2,1,0:T(8,128)(2,1)S(1)} collective-permute-done((bf16[4,216,768]{2,1,0:T(8,128)(2,1)}, bf16[4,216,768]{2,1,0:T(8,128)(2,1)S(1)}, u32[]{:S(2)}, u32[]{:S(2)}) %collective-permute-start.15) | collective-permute-done | bytes 1327136 | tf_op jit(solution)/shard_map/ppermute | solution.py:84
  212.7 6.6 copy.67
  224.0 6.7 copy.68
  232.0 170.6 %while.27 = (s32[]{:T(128)}, bf16[12,1024,64]{1,2,0:T(8,128)(2,1)}, f32[12,1024]{1,0:T(8,128)}, bf16[12,1024,64]{2,1,0:T(8,128)(2,1)S(1)}, bf16[12,2048,64]{2,1,...) while((s32[]{:T(128)}, bf16[12,1024,64]{1,2,0:T(8,128)(2,1)}, ...), condition=%wide.region_3.4_spmd, body=%wide.region_0.3_spmd.sunk | while | flops 562101248 | bytes 60229756 | solution.py:250
  402.6 14.2 %assemble.3 = (bf16[768,768]{1,0:T(8,128)(2,1)}, bf16[768,3072]{1,0:T(8,128)(2,1)}, bf16[3072,768]{1,0:T(8,128)(2,1)}) custom-call(s32[17]{0:T(128)} %pad_add_fusion.spot_ref, bf16[16,216,768]{2,1,0:T(8,128)(2,1)} %constant_dynamic-update-slice_fusion.13.mine_ref, bf16[16,216,768]{2,1,0:T(8,128)(2,1)} %collective-permute-done.17.other_ref), custom_call_target="tpu_custom_call" | custom-call | tf_op jit(solution)/shard_map/assemble/pallas_call | solution.py:191
  421.4 35.5 %fusion.58 = (bf16[1024,3072]{1,0:T(8,128)(2,1)S(1)}, f32[1024,3072]{1,0:T(8,128)}) fusion(f32[3072]{0:T(1024)S(1)} %copy-done.33, bf16[768,3072]{1,0:T(8,128)(2,1)S(1)} %bitcast.380, f32[1024,768]{0,1:T(8,128)S(1)} %get-tuple-element.207, f32[768]{0:T(1024)S(1)} %copy-done.36, f32[768]{0:T(1024)S(1)} %copy-done.31, f32[1024]{0:T(1024)S(1)} %add_rsqrt_fusion.1, ...), kind=kOutput, calls=%fused_computation.63 | convolution fusion | flops 5043388416 | bytes 26765312 | tf_op jit(solution)/shard_map/dot_general | solution.py:19
  471.8 7.0 convolution_convert_fusion
  478.8 12.6 %fusion.138 = (bf16[3072]{0:T(1024)(128)(2,1)}, bf16[1024,3072]{1,0:T(8,128)(2,1)S(1)}) fusion(f32[1024,3072]{1,0:T(8,128)} %get-tuple-element.278, f32[3072]{0:T(1024)S(1)} %copy-done.33, bf16[1024,768]{0,1:T(8,128)(2,1)S(1)} %get-tuple-element.203, bf16[3072,768]{1,0:T(8,128)(2,1)S(1)} %bitcast.382), kind=kOutput, calls=%fused_computation.336 | convolution fusion | flops 4869583872 | bytes 25184256 | tf_op jit(solution)/shard_map/dot_general | solution.py:27
  491.4 7.1 convolution_convert_fusion.1
  498.5 8.7 multiply_reduce_fusion.2
  519.4 211.9 %while.28 = (s32[]{:T(128)}, bf16[12,1024,64]{1,2,0:T(8,128)(2,1)}, bf16[12,2048,64]{1,2,0:T(8,128)(2,1)S(1)}, bf16[12,2048,64]{1,2,0:T(8,128)(2,1)}, bf16[12,10...) while((s32[]{:T(128)}, bf16[12,1024,64]{1,2,0:T(8,128)(2,1)}, ...), condition=%wide.region_14.15_spmd, body=%wide.region_12.14_spmd.sunk | while | flops 1374157824 | bytes 66249840 | solution.py:268
  764.2 10.2 %collective-permute-done.18 = bf16[256,768]{0,1:T(8,128)(2,1)S(1)} collective-permute-done((bf16[256,768]{0,1:T(8,128)(2,1)S(1)}, bf16[256,768]{0,1:T(8,128)(2,1)S(1)}, u32[]{:S(2)}, u32[]{:S(2)}) %collective-permute-start.18) | collective-permute-done | bytes 393248 | tf_op jit(solution)/shard_map/ppermute | solution.py:95
  823.3 10.1 %collective-permute-done.51 = bf16[384,768]{1,0:T(8,128)(2,1)S(1)} collective-permute-done((bf16[384,768]{1,0:T(8,128)(2,1)S(1)}, bf16[384,768]{1,0:T(8,128)(2,1)S(1)}, u32[]{:S(2)}, u32[]{:S(2)}) %collective-permute-start.51) | collective-permute-done | bytes 589856 | tf_op jit(solution)/shard_map/ppermute | solution.py:84
  838.8 9.0 collective-permute-done.43
  849.4 8.6 collective-permute-done.44
  888.9 6.7 convolution_convert_fusion.2
  935.3 14.9 %collective-permute-done.26 = bf16[256,768]{0,1:T(8,128)(2,1)} collective-permute-done((bf16[256,768]{0,1:T(8,128)(2,1)}, bf16[256,768]{0,1:T(8,128)(2,1)}, u32[]{:S(2)}, u32[]{:S(2)}) %collective-permute-start.26) | collective-permute-done | bytes 393248 | tf_op jit(solution)/shard_map/ppermute | solution.py:95
  (551 shorter events, 719.1 us)
Async XLA Ops:
  45.6 28.0 %collective-permute-start.9 = (bf16[16,80,768]{2,1,0:T(8,128)(2,1)S(1)}, bf16[16,80,768]{2,1,0:T(8,128)(2,1)}, u32[]{:S(2)}, u32[]{:S(2)}) collective-permute-start(bf16[16,80,768]{2,1,0:T(8,128)(2,1)S(1)} %constant_dynamic-update-slice_fusion.mine_ref), channel_id=1, source_target_pairs={{0,1},{1,0},{2,3},{3,2},{4,5},{5,4},{6,7},{7,6},{8,9},{9,8},{10,11... | collective-permute-start | bytes 5898248 | tf_op jit(solution)/shard_map/ppermute | solution.py:87
  51.3 38.7 %collective-permute-start = (bf16[256,768]{0,1:T(8,128)(2,1)}, bf16[256,768]{0,1:T(8,128)(2,1)}, u32[]{:S(2)}, u32[]{:S(2)}) collective-permute-start(bf16[256,768]{0,1:T(8,128)(2,1)} %bitcast.373), channel_id=1, source_target_pairs={{0,2},{1,3},{2,0},{3,1},{4,6},{5,7},{6,4},{7,5},{8,10},{9,11},{10,... | collective-permute-start | bytes 1179656 | tf_op jit(solution)/shard_map/ppermute | solution.py:95
  56.1 35.4 %collective-permute-start.1 = (bf16[256,768]{0,1:T(8,128)(2,1)}, bf16[256,768]{0,1:T(8,128)(2,1)}, u32[]{:S(2)}, u32[]{:S(2)}) collective-permute-start(bf16[256,768]{0,1:T(8,128)(2,1)} %bitcast.372), channel_id=1, source_target_pairs={{0,4},{1,5},{2,6},{3,7},{4,0},{5,1},{6,2},{7,3},{8,12},{9,13},{10,... | collective-permute-start | bytes 1179656 | tf_op jit(solution)/shard_map/ppermute | solution.py:95
  59.5 32.0 %collective-permute-start.2 = (bf16[256,768]{0,1:T(8,128)(2,1)}, bf16[256,768]{0,1:T(8,128)(2,1)}, u32[]{:S(2)}, u32[]{:S(2)}) collective-permute-start(bf16[256,768]{0,1:T(8,128)(2,1)} %bitcast.371), channel_id=1, source_target_pairs={{0,6},{1,7},{2,4},{3,5},{4,2},{5,3},{6,0},{7,1},{8,14},{9,15},{10,... | collective-permute-start | bytes 1179656 | tf_op jit(solution)/shard_map/ppermute | solution.py:95
  69.4 33.1 %collective-permute-start.11 = (bf16[216,768]{1,0:T(8,128)(2,1)}, bf16[216,768]{1,0:T(8,128)(2,1)}, u32[]{:S(2)}, u32[]{:S(2)}) collective-permute-start(bf16[216,768]{1,0:T(8,128)(2,1)} %constant_dynamic-update-slice_fusion.7), channel_id=1, source_target_pairs={{0,2},{1,3},{2,0},{3,1},{4,6},{5,7},{6,4},{7,5},{8,10},{9,11},{10,... | collective-permute-start | bytes 995336 | tf_op jit(solution)/shard_map/ppermute | solution.py:80
  73.6 42.3 %collective-permute-start.12 = (bf16[216,768]{1,0:T(8,128)(2,1)}, bf16[216,768]{1,0:T(8,128)(2,1)S(1)}, u32[]{:S(2)}, u32[]{:S(2)}) collective-permute-start(bf16[216,768]{1,0:T(8,128)(2,1)} %constant_dynamic-update-slice_fusion.7), channel_id=1, source_target_pairs={{0,4},{1,5},{2,6},{3,7},{4,0},{5,1},{6,2},{7,3},{8,12},{9,13},{10,... | collective-permute-start | bytes 995336 | tf_op jit(solution)/shard_map/ppermute | solution.py:80
  91.5 371.8 %collective-permute-start.21 = (bf16[256,768]{0,1:T(8,128)(2,1)}, bf16[256,768]{0,1:T(8,128)(2,1)}, u32[]{:S(2)}, u32[]{:S(2)}) collective-permute-start(bf16[256,768]{0,1:T(8,128)(2,1)} %bitcast.45), channel_id=1, source_target_pairs={{0,2},{1,3},{2,0},{3,1},{4,6},{5,7},{6,4},{7,5},{8,10},{9,11},{10,... | collective-permute-start | bytes 1179656 | tf_op jit(solution)/shard_map/ppermute | solution.py:95
  101.2 99.2 %collective-permute-start.10 = (bf16[1024,1536]{1,0:T(8,128)(2,1)}, bf16[1024,1536]{1,0:T(8,128)(2,1)}, u32[]{:S(2)}, u32[]{:S(2)}) collective-permute-start(bf16[1024,1536]{1,0:T(8,128)(2,1)} %pad_maximum_fusion.3), channel_id=1, source_target_pairs={{0,1},{1,0},{2,3},{3,2},{4,5},{5,4},{6,7},{7,6},{8,9},{9,8},{10,11... | collective-permute-start | bytes 9437192 | tf_op jit(solution)/shard_map/ppermute | solution.py:103
  118.4 32.3 %collective-permute-start.14 = (bf16[4,216,768]{2,1,0:T(8,128)(2,1)}, bf16[4,216,768]{2,1,0:T(8,128)(2,1)}, u32[]{:S(2)}, u32[]{:S(2)}) collective-permute-start(bf16[4,216,768]{2,1,0:T(8,128)(2,1)} %pad_maximum_fusion.10), channel_id=1, source_target_pairs={{0,8},{8,0},{16,24},{24,16},{1,9},{9,1},{17,25},{25,17},{2,10},{10... | collective-permute-start | bytes 3981320 | tf_op jit(solution)/shard_map/ppermute | solution.py:84
  122.5 56.8 %collective-permute-start.15 = (bf16[4,216,768]{2,1,0:T(8,128)(2,1)}, bf16[4,216,768]{2,1,0:T(8,128)(2,1)S(1)}, u32[]{:S(2)}, u32[]{:S(2)}) collective-permute-start(bf16[4,216,768]{2,1,0:T(8,128)(2,1)} %pad_maximum_fusion.10), channel_id=1, source_target_pairs={{0,16},{8,24},{16,0},{24,8},{1,17},{9,25},{17,1},{25,9},{2,18},{10... | collective-permute-start | bytes 3981320 | tf_op jit(solution)/shard_map/ppermute | solution.py:84
  123.3 60.1 %collective-permute-start.16 = (bf16[4,216,768]{2,1,0:T(8,128)(2,1)}, bf16[4,216,768]{2,1,0:T(8,128)(2,1)S(1)}, u32[]{:S(2)}, u32[]{:S(2)}) collective-permute-start(bf16[4,216,768]{2,1,0:T(8,128)(2,1)} %pad_maximum_fusion.10), channel_id=1, source_target_pairs={{0,24},{8,16},{16,8},{24,0},{1,25},{9,17},{17,9},{25,1},{2,26},{10... | collective-permute-start | bytes 3981320 | tf_op jit(solution)/shard_map/ppermute | solution.py:84
  150.8 312.6 %collective-permute-start.22 = (bf16[256,768]{0,1:T(8,128)(2,1)}, bf16[256,768]{0,1:T(8,128)(2,1)}, u32[]{:S(2)}, u32[]{:S(2)}) collective-permute-start(bf16[256,768]{0,1:T(8,128)(2,1)} %bitcast.370), channel_id=1, source_target_pairs={{0,4},{1,5},{2,6},{3,7},{4,0},{5,1},{6,2},{7,3},{8,12},{9,13},{10,... | collective-permute-start | bytes 1179656 | tf_op jit(solution)/shard_map/ppermute | solution.py:95
  179.3 284.0 %collective-permute-start.23 = (bf16[256,768]{0,1:T(8,128)(2,1)}, bf16[256,768]{0,1:T(8,128)(2,1)}, u32[]{:S(2)}, u32[]{:S(2)}) collective-permute-start(bf16[256,768]{0,1:T(8,128)(2,1)} %bitcast.47), channel_id=1, source_target_pairs={{0,6},{1,7},{2,4},{3,5},{4,2},{5,3},{6,0},{7,1},{8,14},{9,15},{10,... | collective-permute-start | bytes 1179656 | tf_op jit(solution)/shard_map/ppermute | solution.py:95
  184.5 218.1 %collective-permute-start.17 = (bf16[16,216,768]{2,1,0:T(8,128)(2,1)}, bf16[16,216,768]{2,1,0:T(8,128)(2,1)}, u32[]{:S(2)}, u32[]{:S(2)}) collective-permute-start(bf16[16,216,768]{2,1,0:T(8,128)(2,1)} %constant_dynamic-update-slice_fusion.13.mine_ref), channel_id=1, source_target_pairs={{0,1},{1,0},{2,3},{3,2},{4,5},{5,4},{6,7},{7,6},{8,9},{9,8},{10,11... | collective-permute-start | bytes 15925256 | tf_op jit(solution)/shard_map/ppermute | solution.py:87
  734.5 68.4 %collective-permute-start.49 = (bf16[16,96,768]{2,1,0:T(8,128)(2,1)}, bf16[16,96,768]{2,1,0:T(8,128)(2,1)}, u32[]{:S(2)}, u32[]{:S(2)}) collective-permute-start(bf16[16,96,768]{2,1,0:T(8,128)(2,1)} %dynamic-slice_bitcast_fusion), channel_id=1, source_target_pairs={{0,1},{1,0},{2,3},{3,2},{4,5},{5,4},{6,7},{7,6},{8,9},{9,8},{10,11... | collective-permute-start | bytes 7077896 | tf_op jit(solution)/shard_map/ppermute | solution.py:87
  738.5 68.6 %collective-permute-start.42 = (bf16[16,24,3072]{2,1,0:T(8,128)(2,1)}, bf16[16,24,3072]{2,1,0:T(8,128)(2,1)}, u32[]{:S(2)}, u32[]{:S(2)}) collective-permute-start(bf16[16,24,3072]{2,1,0:T(8,128)(2,1)} %dynamic-slice_bitcast_fusion.1), channel_id=1, source_target_pairs={{0,1},{1,0},{2,3},{3,2},{4,5},{5,4},{6,7},{7,6},{8,9},{9,8},{10,11... | collective-permute-start | bytes 7077896 | tf_op jit(solution)/shard_map/ppermute | solution.py:87
  739.4 41.1 %collective-permute-start.35 = (bf16[16,24,768]{2,1,0:T(8,128)(2,1)}, bf16[16,24,768]{2,1,0:T(8,128)(2,1)}, u32[]{:S(2)}, u32[]{:S(2)}) collective-permute-start(bf16[16,24,768]{2,1,0:T(8,128)(2,1)} %dynamic-slice_bitcast_fusion.9), channel_id=1, source_target_pairs={{0,1},{1,0},{2,3},{3,2},{4,5},{5,4},{6,7},{7,6},{8,9},{9,8},{10,11... | collective-permute-start | bytes 1769480 | tf_op jit(solution)/shard_map/ppermute | solution.py:87
  741.9 37.4 %collective-permute-start.19 = (bf16[256,768]{0,1:T(8,128)(2,1)}, bf16[256,768]{0,1:T(8,128)(2,1)}, u32[]{:S(2)}, u32[]{:S(2)}) collective-permute-start(bf16[256,768]{0,1:T(8,128)(2,1)} %get-tuple-element.236), channel_id=1, source_target_pairs={{0,4},{1,5},{2,6},{3,7},{4,0},{5,1},{6,2},{7,3},{8,12},{9,13},{10,... | collective-permute-start | bytes 1179656 | tf_op jit(solution)/shard_map/ppermute | solution.py:95
  792.2 82.9 %collective-permute-start.24 = (bf16[1024,1536]{0,1:T(8,128)(2,1)}, bf16[1024,1536]{0,1:T(8,128)(2,1)S(1)}, u32[]{:S(2)}, u32[]{:S(2)}) collective-permute-start(bf16[1024,1536]{0,1:T(8,128)(2,1)} %pad_maximum_fusion.2), channel_id=1, source_target_pairs={{0,1},{1,0},{2,3},{3,2},{4,5},{5,4},{6,7},{7,6},{8,9},{9,8},{10,11... | collective-permute-start | bytes 9437192 | tf_op jit(solution)/shard_map/ppermute | solution.py:103
  817.7 30.0 %collective-permute-start.43 = (bf16[96,3072]{1,0:T(8,128)(2,1)S(1)}, bf16[96,3072]{1,0:T(8,128)(2,1)S(1)}, u32[]{:S(2)}, u32[]{:S(2)}) collective-permute-start(bf16[96,3072]{1,0:T(8,128)(2,1)S(1)} %get-tuple-element.220), channel_id=1, source_target_pairs={{0,8},{8,0},{16,24},{24,16},{1,9},{9,1},{17,25},{25,17},{2,10},{10... | collective-permute-start | bytes 1769480 | tf_op jit(solution)/shard_map/ppermute | solution.py:84
  822.4 35.6 %collective-permute-start.44 = (bf16[96,3072]{1,0:T(8,128)(2,1)S(1)}, bf16[96,3072]{1,0:T(8,128)(2,1)S(1)}, u32[]{:S(2)}, u32[]{:S(2)}) collective-permute-start(bf16[96,3072]{1,0:T(8,128)(2,1)S(1)} %get-tuple-element.222), channel_id=1, source_target_pairs={{0,16},{8,24},{16,0},{24,8},{1,17},{9,25},{17,1},{25,9},{2,18},{10... | collective-permute-start | bytes 1769480 | tf_op jit(solution)/shard_map/ppermute | solution.py:84
  895.8 30.0 %collective-permute-start.28 = (bf16[16,24,2304]{2,1,0:T(8,128)(2,1)S(1)}, bf16[16,24,2304]{2,1,0:T(8,128)(2,1)}, u32[]{:S(2)}, u32[]{:S(2)}) collective-permute-start(bf16[16,24,2304]{2,1,0:T(8,128)(2,1)S(1)} %dynamic-slice_bitcast_fusion.2), channel_id=1, source_target_pairs={{0,1},{1,0},{2,3},{3,2},{4,5},{5,4},{6,7},{7,6},{8,9},{9,8},{10,11... | collective-permute-start | bytes 5308424 | tf_op jit(solution)/shard_map/ppermute | solution.py:87
  921.0 29.2 %collective-permute-start.26 = (bf16[256,768]{0,1:T(8,128)(2,1)}, bf16[256,768]{0,1:T(8,128)(2,1)}, u32[]{:S(2)}, u32[]{:S(2)}) collective-permute-start(bf16[256,768]{0,1:T(8,128)(2,1)} %get-tuple-element.228), channel_id=1, source_target_pairs={{0,4},{1,5},{2,6},{3,7},{4,0},{5,1},{6,2},{7,3},{8,12},{9,13},{10,... | collective-permute-start | bytes 1179656 | tf_op jit(solution)/shard_map/ppermute | solution.py:95
  923.0 29.2 %collective-permute-start.27 = (bf16[256,768]{0,1:T(8,128)(2,1)}, bf16[256,768]{0,1:T(8,128)(2,1)}, u32[]{:S(2)}, u32[]{:S(2)}) collective-permute-start(bf16[256,768]{0,1:T(8,128)(2,1)} %get-tuple-element.227), channel_id=1, source_target_pairs={{0,6},{1,7},{2,4},{3,5},{4,2},{5,3},{6,0},{7,1},{8,14},{9,15},{10,... | collective-permute-start | bytes 1179656 | tf_op jit(solution)/shard_map/ppermute | solution.py:95
  (95 other events, 961.9 us)

commit v2 on v1

--- a/solution.py
+++ b/solution.py
@@ -164,15 +164,16 @@
     order = relative_order(grid)
     count, rows, width = mine.shape
     spot = jnp.concatenate([grid.core[None].astype(jnp.int32), order])
-    if any(cut[1] % 8 for cut in cuts):
+    wides = [sum(piece[3] for piece in pieces) for _, pieces in cuts]
+    if any(height % 8 for height, _ in cuts):
         first = jnp.where(grid.core == 0, mine, other)[order]
         second = jnp.where(grid.core == 0, other, mine)[order]
         both = jnp.stack([first, second], axis=1).reshape(2 * count, rows, width)
         outs = []
-        for start, height, blocks in cuts:
-            piece = both[:, start : start + height * blocks]
-            piece = piece.reshape(2 * count, blocks, height, width).transpose(0, 2, 1, 3)
-            outs.append(piece.reshape(2 * count * height, blocks * width))
+        for height, pieces in cuts:
+            ordered = sorted(pieces, key=lambda piece: piece[2])
+            strips = [both[:, p[0] : p[0] + height, p[1] : p[1] + p[3]] for p in ordered]
+            outs.append(jnp.concatenate(strips, axis=2).reshape(2 * count * height, -1))
         return outs
 
     def kernel(spot_ref, mine_ref, other_ref, *out_refs):
@@ -181,12 +182,11 @@
             @pl.when(spot_ref[0] == core)
             def _(core=core):
                 for source, place in ((mine_ref, core), (other_ref, 1 - core)):
-                    for (start, height, blocks), out_ref in zip(cuts, out_refs):
-                        for block in range(blocks):
-                            out_ref[
-                                place * height : (place + 1) * height,
-                                block * width : (block + 1) * width,
-                            ] = source[start + block * height : start + (block + 1) * height, :]
+                    for (height, pieces), out_ref in zip(cuts, out_refs):
+                        for row, column, target, columns in pieces:
+                            out_ref[place * height : (place + 1) * height, target : target + columns] = source[
+                                row : row + height, column : column + columns
+                            ]
 
     return pl.pallas_call(
         kernel,
@@ -198,14 +198,15 @@
                 pl.BlockSpec((None, rows, width), lambda i, spot: (spot[i + 1], 0, 0)),
             ],
             out_specs=[
-                pl.BlockSpec((2 * height, blocks * width), lambda i, spot: (i, 0))
-                for _, height, blocks in cuts
+                pl.BlockSpec((2 * height, wide), lambda i, spot: (i, 0))
+                for (height, _), wide in zip(cuts, wides)
             ],
         ),
         out_shape=[
-            jax.ShapeDtypeStruct((2 * count * height, blocks * width), mine.dtype)
-            for _, height, blocks in cuts
+            jax.ShapeDtypeStruct((2 * count * height, wide), mine.dtype)
+            for (height, _), wide in zip(cuts, wides)
         ],
+        cost_estimate=pl.CostEstimate(flops=0, bytes_accessed=8 * count * rows * width, transcendentals=0),
         name="assemble",
     )(spot, mine, other)
 
@@ -229,44 +230,196 @@
     return total
 
 
-def split_heads(rows):
-    return rows.reshape(rows.shape[0], H, HD).transpose(1, 0, 2)
-
-
-def join_heads(heads):
-    return heads.transpose(1, 0, 2).reshape(heads.shape[1], H * HD)
-
-
-def attention(query, keys, values, key_bias):
-    def attend(operands):
-        query_h, key_h, value_h = operands
-        scores = right_product(query_h, key_h) * 0.125 + key_bias[None, :]
-        largest = jnp.max(scores, axis=-1, keepdims=True)
-        exponent = jnp.exp(scores - largest)
-        totals = jnp.sum(exponent, axis=-1, keepdims=True)
-        context_h = matmul((exponent / totals).astype(BF), value_h)
-        return (context_h.astype(BF), (largest + jnp.log(totals))[..., 0])
-
-    context, log_totals = lax.map(attend, (split_heads(query), split_heads(keys), split_heads(values)))
-    return join_heads(context), log_totals
-
-
-def attention_back(query, keys, values, key_bias, log_totals, grad_context):
-    def attend_back(operands):
-        query_h, key_h, value_h, grad_h, log_h = operands
-        scores = right_product(query_h, key_h) * 0.125 + key_bias[None, :]
-        exact = jnp.exp(scores - log_h[..., None])
-        grad_weights = right_product(grad_h, value_h)
-        grad_value_h = left_product(exact.astype(BF), grad_h)
-        centre_term = jnp.sum(exact * grad_weights, axis=-1, keepdims=True)
-        grad_scores = (exact * (grad_weights - centre_term)).astype(BF)
-        grad_query_h = matmul(grad_scores, key_h) * 0.125
-        grad_key_h = left_product(grad_scores, query_h) * 0.125
-        return (grad_query_h.astype(BF), grad_key_h.astype(BF), grad_value_h.astype(BF))
-
-    heads = tuple(split_heads(a) for a in (query, keys, values, grad_context))
-    grads = lax.map(attend_back, heads + (log_totals,))
-    return tuple(join_heads(a) for a in grads)
+PARTS = 3
+LOG2E = 1.4426950408889634
+SCALE = 0.125 * LOG2E
+
+
+def dot_nt(left, right):
+    return lax.dot_general(left, right, (((1,), (1,)), ((), ())), preferred_element_type=F32)
+
+
+def own_lanes(half, count):
+    lane = lax.broadcasted_iota(jnp.int32, (count, 2 * HD), 1)
+    return (lane // HD) == half, lane == HD * (1 - half)
+
+
+def attention(part, inputs, others, key_bias, context, log_totals, block=256):
+    rows, width = inputs.shape
+    pairs = width // (6 * HD)
+    sources = [inputs] + list(others)
+    count = len(sources)
+    keys = rows * count
+
+    def kernel(q_ref, bias_ref, *refs):
+        k_refs, v_refs = refs[:count], refs[count : 2 * count]
+        o_ref, l_ref, k_own, v_own = refs[-4:]
+
+        @pl.when(pl.program_id(1) == 0)
+        def _():
+            for half in range(2):
+                own, spare = own_lanes(half, rows)
+                zero = jnp.zeros((rows, 2 * HD), BF)
+                for i in range(count):
+                    at = slice(i * rows, (i + 1) * rows)
+                    k_own[half, at, :] = jnp.where(own, k_refs[i][...], jnp.where(spare, bias_ref[at, :], zero))
+                    v_own[half, at, :] = jnp.where(own, v_refs[i][...], jnp.where(spare, zero + 1, zero))
+
+        query = q_ref[...]
+        results = []
+        for half in range(2):
+            own, spare = own_lanes(half, block)
+            zero = jnp.zeros_like(query)
+            query_h = jnp.where(own, query, jnp.where(spare, zero + 1, zero))
+            scores = dot_nt(query_h, k_own[half])
+            largest = jnp.max(scores, axis=1, keepdims=True)
+            weights = jnp.exp2((scores - largest) * SCALE).astype(BF)
+            summed = matmul(weights, v_own[half])
+            totals = summed[:, HD * (1 - half) : HD * (1 - half) + 1]
+            results.append(summed / totals)
+            log_total = jnp.broadcast_to(largest * SCALE + jnp.log2(totals), (block, 2 * HD))
+            l_ref[half : half + 1, :] = jnp.transpose(log_total)[0:1, :]
+        lane = lax.broadcasted_iota(jnp.int32, (block, 2 * HD), 1)
+        o_ref[...] = jnp.where(lane < HD, results[0], results[1]).astype(BF)
+
+    def columns(first):
+        return [pl.BlockSpec((rows, 2 * HD), lambda i, j: (0, i + first)) for _ in range(count)]
+
+    first = part * pairs
+    arguments = [inputs, key_bias] + sources + sources
+    specs = [
+        pl.BlockSpec((block, 2 * HD), lambda i, j: (j, i)),
+        pl.BlockSpec((keys, 2 * HD), lambda i, j: (0, 0)),
+    ]
+    specs = specs + columns(pairs) + columns(2 * pairs)
+    aliases = {}
+    if context is not None:
+        aliases = {len(arguments): 0, len(arguments) + 1: 1}
+        arguments = arguments + [context, log_totals]
+        specs = specs + [pl.BlockSpec(memory_space=pl.ANY)] * 2
+    heads = 2 * pairs
+    return pl.pallas_call(
+        kernel,
+        grid=(pairs, rows // block),
+        in_specs=specs,
+        out_specs=[
+            pl.BlockSpec((block, 2 * HD), lambda i, j: (j, i + first)),
+            pl.BlockSpec((None, 8, block), lambda i, j: (i + first, 0, j)),
+        ],
+        out_shape=[
+            jax.ShapeDtypeStruct((rows, H * HD), BF),
+            jax.ShapeDtypeStruct((H // 2, 8, rows), F32),
+        ],
+        scratch_shapes=[pltpu.VMEM((2, keys, 2 * HD), BF), pltpu.VMEM((2, keys, 2 * HD), BF)],
+        input_output_aliases=aliases,
+        compiler_params=pltpu.CompilerParams(vmem_limit_bytes=40 << 20),
+        cost_estimate=pl.CostEstimate(
+            flops=16 * heads * rows * keys * HD, bytes_accessed=8 * rows * width, transcendentals=heads * rows * keys
+        ),
+        name="attention",
+    )(*arguments)
+
+
+def attention_back(part, inputs, others, key_bias, log_totals, context, grad_context, block=256, chunk=1024):
+    rows, width = inputs.shape
+    pairs = width // (6 * HD)
+    sources = [inputs] + list(others)
+    count = len(sources)
+    keys = rows * count
+    blocks = rows // block
+    chunk = min(chunk, rows)
+    chunks = keys // chunk
+
+    def kernel(q_ref, bias_ref, l_ref, o_ref, g_ref, *refs):
+        k_refs, v_refs = refs[:count], refs[count : 2 * count]
+        out_ref, other_refs = refs[2 * count], refs[2 * count + 1 : 3 * count]
+        k_own, k_turned, v_all, grad_k, grad_v = refs[3 * count :]
+        for i in range(count):
+            at = slice(i * rows, (i + 1) * rows)
+            v_all[at, :] = v_refs[i][...]
+            for half in range(2):
+                own, spare = own_lanes(half, rows)
+                key = k_refs[i][...]
+                zero = jnp.zeros_like(key)
+                k_own[half, at, :] = jnp.where(own, key, jnp.where(spare, bias_ref[at, :], zero))
+                k_turned[half, :, at] = jnp.transpose(jnp.where(own, key, zero))
+        grad_k[...] = jnp.zeros_like(grad_k)
+        grad_v[...] = jnp.zeros_like(grad_v)
+        place = pl.program_id(0)
+
+        @pl.loop(0, blocks)
+        def _(j):
+            at = pl.ds(pl.multiple_of(j * block, block), block)
+            query, grad = q_ref[at, :], g_ref[at, :]
+            turned = jnp.transpose(grad.astype(F32) * o_ref[at, :].astype(F32))
+            asks, plain, grads, centres, logs = [], [], [], [], []
+            for half in range(2):
+                own, spare = own_lanes(half, block)
+                zero = jnp.zeros_like(query)
+                asks.append(jnp.where(own, query, jnp.where(spare, zero + 1, zero)))
+                plain.append(jnp.where(own, query, zero))
+                grads.append(jnp.where(own, grad, zero))
+                centres.append(jnp.sum(turned[HD * half : HD * half + HD], axis=0, keepdims=True))
+                logs.append(l_ref[half : half + 1, at])
+            grad_q = None
+            for c in range(chunks):
+                span = slice(c * chunk, (c + 1) * chunk)
+                weights, slopes = [], []
+                for half in range(2):
+                    scores = dot_nt(k_own[half, span, :], asks[half])
+                    grad_weights = dot_nt(v_all[span, :], grads[half])
+                    exact = jnp.exp2(scores * SCALE - logs[half])
+                    slope = (exact * (grad_weights - centres[half])).astype(BF)
+                    weights.append(exact.astype(BF))
+                    slopes.append(slope)
+                    step = matmul(k_turned[half, :, span], slope)
+                    grad_q = step if grad_q is None else grad_q + step
+                grad_v[span, :] += matmul(weights[0], grads[0]) + matmul(weights[1], grads[1])
+                grad_k[span, :] += matmul(slopes[0], plain[0]) + matmul(slopes[1], plain[1])
+            columns = pl.ds(pl.multiple_of(place * 2 * HD, 2 * HD), 2 * HD)
+            out_ref[at, columns] = (jnp.transpose(grad_q) * 0.125).astype(BF)
+
+        for i in range(count):
+            at = slice(i * rows, (i + 1) * rows)
+            target, shift = (out_ref, pairs) if i == 0 else (other_refs[i - 1], 0)
+            for value, offset, scale in ((grad_k, 0, 0.125), (grad_v, pairs, 1.0)):
+                first_column = pl.multiple_of((place + shift + offset) * 2 * HD, 2 * HD)
+                target[:, pl.ds(first_column, 2 * HD)] = (value[at, :] * scale).astype(BF)
+
+    def column(first):
+        return pl.BlockSpec((rows, 2 * HD), lambda i: (0, i + first))
+
+    first = part * pairs
+    heads = 2 * pairs
+    return pl.pallas_call(
+        kernel,
+        grid=(pairs,),
+        in_specs=[
+            column(0),
+            pl.BlockSpec((keys, 2 * HD), lambda i: (0, 0)),
+            pl.BlockSpec((None, 8, rows), lambda i: (i + first, 0, 0)),
+            column(first),
+            column(first),
+        ]
+        + [column(pairs)] * count
+        + [column(2 * pairs)] * count,
+        out_specs=[pl.BlockSpec((rows, width), lambda i: (0, 0))]
+        + [pl.BlockSpec((rows, 4 * HD * pairs), lambda i: (0, 0))] * (count - 1),
+        out_shape=[jax.ShapeDtypeStruct((rows, width), BF)]
+        + [jax.ShapeDtypeStruct((rows, 4 * HD * pairs), BF)] * (count - 1),
+        scratch_shapes=[
+            pltpu.VMEM((2, keys, 2 * HD), BF),
+            pltpu.VMEM((2, 2 * HD, keys), BF),
+            pltpu.VMEM((keys, 2 * HD), BF),
+            pltpu.VMEM((keys, 2 * HD), F32),
+            pltpu.VMEM((keys, 2 * HD), F32),
+        ],
+        compiler_params=pltpu.CompilerParams(vmem_limit_bytes=48 << 20),
+        cost_estimate=pl.CostEstimate(
+            flops=40 * heads * rows * keys * HD, bytes_accessed=12 * rows * width, transcendentals=heads * rows * keys
+        ),
+        name="attention_back",
+    )(inputs, key_bias, log_totals, context, grad_context, *sources, *sources)
 
 
 def body(
@@ -313,23 +466,20 @@
     vector_size = vector_row.shape[0]
     vector_rows = jnp.zeros((8, width), BF).at[0, :vector_size].set(vector_row)
     early = jnp.concatenate([query_weight, key_weight, value_weight, vector_rows], axis=0)
-    late = jnp.concatenate(
-        [out_weight]
-        + [up_weight[:, i * width : (i + 1) * width] for i in range(wide)]
-        + [down_weight],
-        axis=0,
-    )
-    mine, other = gather_packed(grid, early)
-    into_full, vector_full = assemble(
-        grid, mine, other, ((0, slim, 3), (3 * slim, 8, 1))
-    )
-    late_mine, late_other = gather_packed(grid, late)
-    out_full, up_full, down_full = assemble(
-        grid,
-        late_mine,
-        late_other,
-        ((0, slim, 1), (slim, slim, wide), (slim * (1 + wide), tall, 1)),
-    )
+    ups = [up_weight[:, i * width : (i + 1) * width] for i in range(wide)]
+    late = jnp.concatenate([out_weight] + ups, axis=0)
+    strip = width // PARTS
+    cuts = [
+        (slim, tuple((i * slim, part * strip, i * strip, strip) for i in range(3))) for part in range(PARTS)
+    ]
+    cuts.append((8, ((3 * slim, 0, 0, width),)))
+    *into_full, vector_full = assemble(grid, *gather_packed(grid, early), cuts)
+    cuts = [
+        (slim, ((0, 0, 0, width),)),
+        (slim, tuple((slim * (1 + i), 0, i * width, width) for i in range(wide))),
+    ]
+    out_full, up_full = assemble(grid, *gather_packed(grid, late), cuts)
+    (down_full,) = assemble(grid, *gather_packed(grid, down_weight), [(tall, ((0, 0, 0, width),))])
     vector_table = vector_full.reshape(devices, 8, width)[:, 0, :vector_size]
     small = vector_table[:, : 8 * slim].reshape(devices, 8, slim).transpose(1, 0, 2)
     small = small.reshape(8, width).astype(F32)
@@ -348,16 +498,17 @@
         ]
     ).astype(F32)
 
-    into = matmul(flat_in, into_full)
-    query = (into[:, :width] + query_add).astype(BF)
-    key_value = jnp.concatenate([into[:, width : 2 * width], into[:, 2 * width :] + value_add], axis=1)
-    key_value = key_value.astype(BF)
-    key_value_all = jnp.concatenate(
-        [key_value] + [grid.to_member(key_value, step) for step in range(1, grid.group)], axis=0
-    )
-    keys, values = key_value_all[:, :width], key_value_all[:, width:]
-
-    context, log_totals = attention(query, keys, values, key_bias)
+    key_bias = jnp.broadcast_to(key_bias[:, None], (key_bias.shape[0], 2 * HD)).astype(BF)
+    inputs, others = [], []
+    for part in range(PARTS):
+        at = slice(part * strip, (part + 1) * strip)
+        add = jnp.concatenate([query_add[at], jnp.zeros((strip,), F32), value_add[at]])
+        own = (matmul(flat_in, into_full[part]) + add).astype(BF)
+        inputs.append(own)
+        others.append([grid.to_member(own, step) for step in range(1, grid.group)])
+    context, log_totals = None, None
+    for part in range(PARTS):
+        context, log_totals = attention(part, inputs[part], others[part], key_bias, context, log_totals)
     grad_in = to_sequences(grid, cotangent)
 
     first_sum = flat_in.astype(F32) + matmul(context, out_full) + out_add
@@ -392,47 +543,45 @@
     grad_up_own = scatter_sum(grid, grad_up)
     grad_out_own = scatter_sum(grid, grad_out)
 
-    grad_query_low, grad_keys, grad_values = attention_back(
-        query, keys, values, key_bias, log_totals, grad_context
-    )
-    rows = seqs * length
-    grad_kv = jnp.concatenate([grad_keys, grad_values], axis=1)
-    grad_kv_sum = grad_kv[:rows].astype(F32)
-    for step in range(1, grid.group):
-        piece = grad_kv[step * rows : (step + 1) * rows]
-        grad_kv_sum = grad_kv_sum + grid.to_member(piece, step, back=True).astype(F32)
-    grad_kv_low = grad_kv_sum.astype(BF)
-    grad_into_low = jnp.concatenate([grad_query_low, grad_kv_low], axis=1)
-    grad_query_add = jnp.sum(grad_query_low.astype(F32), axis=0)
-    grad_value_add = jnp.sum(grad_kv_low[:, width:].astype(F32), axis=0)
-    tokens_grad = right_product(grad_into_low, into_full) + grad_residual
+    tokens_grad = grad_residual
+    grad_into_own, query_adds, value_adds = [], [], []
+    for part in range(PARTS):
+        own, *away = attention_back(
+            part, inputs[part], others[part], key_bias, log_totals, context, grad_context
+        )
+        grad_kv = own[:, strip:].astype(F32)
+        for step, piece in enumerate(away, 1):
+            grad_kv = grad_kv + grid.to_member(piece, step, back=True).astype(F32)
+        low = jnp.concatenate([own[:, :strip], grad_kv.astype(BF)], axis=1)
+        query_adds.append(jnp.sum(low[:, :strip].astype(F32), axis=0))
+        value_adds.append(jnp.sum(low[:, 2 * strip :].astype(F32), axis=0))
+        tokens_grad = tokens_grad + right_product(low, into_full[part])
+        grad_into_own.append(scatter_sum(grid, left_product(flat_in, low).astype(BF)))
     tokens_grad = from_sequences(grid, tokens_grad.astype(BF), length).astype(F32)
-    grad_into = left_product(flat_in, grad_into_low).astype(BF)
-    grad_into_own = scatter_sum(grid, grad_into)
-
-    small_grads = jnp.stack(
-        [
-            grad_query_add,
-            grad_value_add,
-            grad_out_add,
-            grad_down_add,
-            grad_gain_one,
-            grad_shift_one,
-            grad_gain_two,
-            grad_shift_two,
-        ]
-    )
-    small_grads = small_grads.reshape(8, devices, slim).transpose(1, 0, 2).reshape(devices, 8 * slim)
-    vector_grads = jnp.concatenate([small_grads, grad_up_add.reshape(devices, tall)], axis=1).astype(BF)
-    vector_own = scatter_sum(grid, vector_grads)[0]
-    vector_outs = [vector_own[i * slim : (i + 1) * slim] for i in range(8)]
-    up_add_own = vector_own[8 * slim :]
+
+    def pack(grads):
+        count = len(grads)
+        table = jnp.stack(grads).reshape(count, devices, slim).transpose(1, 0, 2)
+        return table.reshape(devices, count * slim)
+
+    middle = pack([grad_out_add, grad_down_add, grad_gain_one, grad_shift_one, grad_gain_two, grad_shift_two])
+    middle = jnp.concatenate([middle, grad_up_add.reshape(devices, tall)], axis=1).astype(BF)
+    middle_own = scatter_sum(grid, middle)[0]
+    last = pack([jnp.concatenate(query_adds), jnp.concatenate(value_adds)]).astype(BF)
+    last_own = scatter_sum(grid, last)[0]
+    vector_outs = [last_own[:slim], last_own[slim:]]
+    vector_outs = vector_outs + [middle_own[i * slim : (i + 1) * slim] for i in range(6)]
+    up_add_own = middle_own[6 * slim :]
+    matrix_outs = [
+        jnp.concatenate([own[:, i * strip : (i + 1) * strip] for own in grad_into_own], axis=1)
+        for i in range(3)
+    ]
     return (
         output,
         tokens_grad,
-        grad_into_own[:, :width],
-        grad_into_own[:, width : 2 * width],
-        grad_into_own[:, 2 * width :],
+        matrix_outs[0],
+        matrix_outs[1],
+        matrix_outs[2],
         grad_out_own,
         grad_up_own,
         grad_down_own,

time: 986 us -> 715 us (0.73)
  matrix products: 381 us -> 123 us
  Pallas kernels: 25.3 us -> 160 us
  local copies, waits for them, and re-layouts: 188 us -> 85.9 us
  other arithmetic: 116 us -> 43 us
  starting transfers between devices: 102 us -> 131 us
    pallas_call x0 -> x6, Pallas kernels: none -> 125 us  [the longest x3 76.5 us: attention_back(): pl.pallas_call(kernel, grid=(pairs,), in_specs=[column(0), pl.BlockSpec((...]
    dot_general x40 -> x6, matrix products: 127 us -> 28.4 us  [right_product(): lax.dot_general(left, right, (((1,), (1,)), ((), ())), preferred_element_...]
    dot_general x28 -> x6, matrix products: 166 us -> 70.2 us  [matmul(): return jnp.dot(left, right, preferred_element_type=F32)]
    dot_general x28 -> x6, matrix products: 87.9 us -> 24.8 us  [left_product(): lax.dot_general(left, right, (((0,), (0,)), ((), ())), preferred_element_...]
    while x27 -> x0, local copies, waits for them, and re-layouts: 29.2 us -> none  [the longest x3 16.3 us: attention(): lax.map(attend, (split_heads(query), split_heads(keys), split_heads(value...]
    convert_element_type x13 -> x4, other arithmetic: 32.5 us -> 3.62 us  [the longest x3 3.61 us: body(): low = jnp.concatenate([own[:, :strip], grad_kv.astype(BF)], axis=1)]
    reduce_sum x14 -> x6, other arithmetic: 28.8 us -> 3.36 us  [the longest x3 2.91 us: body(): query_adds.append(jnp.sum(low[:, :strip].astype(F32), axis=0))]
    ppermute x21 -> x33, waiting for transfers between devices: 44.2 us -> 23.7 us  [to_chip(): return lax.ppermute(array_in, 'seq', pairs)]
  transfers between devices with their start and end apart: 63 -> 95, of which waited for: 21 -> 33; matrix products, arithmetic and copies ran while one was open for 38% -> 26% of each run, Pallas kernels for 3% -> 23%
where the time goes in v2:
time: 715 us; the launch traced here: 709 us
  waiting for transfers between devices  163 us (23%)
  Pallas kernels  160 us (22%)
  starting transfers between devices  131 us (18%)
  matrix products  123 us (17%)
  local copies, waits for them, and re-layouts  85.9 us (12%)
  other arithmetic  43 us (6%)
    ppermute x33, waiting for transfers between devices, to_column(): return lax.ppermute(array_in, 'dp', pairs)  95.4 us
    pallas_call x3, Pallas kernels, attention_back(): pl.pallas_call(kernel, grid=(pairs,), in_specs=[column(0), pl.BlockSpec((...  76.5 us
    dot_general x6, matrix products, matmul(): return jnp.dot(left, right, preferred_element_type=F32)  70.2 us
    ppermute x33, starting transfers between devices, to_chip(): return lax.ppermute(array_in, 'seq', pairs)  62 us
    pallas_call x3, Pallas kernels, attention(): pl.pallas_call(kernel, grid=(pairs, rows // block), in_specs=specs, out_s...  49 us
    ppermute x33, starting transfers between devices, to_column(): return lax.ppermute(array_in, 'dp', pairs)  45.3 us
    ppermute x12, waiting for transfers between devices, to_owner(): return lax.ppermute(array_in, 'seq', pairs)  43.5 us
    pallas_call x3, Pallas kernels, assemble(): pl.pallas_call(kernel, grid_spec=pltpu.PrefetchScalarGridSpec(num_scalar_...  34.3 us
  transfers between devices with their start and end apart: 95, of which 33 were waited for; matrix products, arithmetic and copies ran while one was open for 26% of the time, Pallas kernels for 23%

profile of v2, /device:TPU:0, one launch (start us, length us, event | category | flops | bytes accessed | tf_op | source)
XLA Modules:
  0.0 708.6 jit_solution(6284576370621071499)
XLA Ops:
  72.0 20.5 %collective-permute-done.16 = bf16[4,120,768]{2,1,0:T(8,128)(2,1)S(1)} collective-permute-done((bf16[4,120,768]{2,1,0:T(8,128)(2,1)S(1)}, bf16[4,120,768]{2,1,0:T(8,128)(2,1)S(1)}, u32[]{:S(2)}, u32[]{:S(2)}) %collective-permute-start.16) | collective-permute-done | bytes 737312 | tf_op jit(solution)/shard_map/ppermute | solution.py:84
  97.9 12.5 %collective-permute-done.18 = bf16[4,120,768]{2,1,0:T(8,128)(2,1)S(1)} collective-permute-done((bf16[4,120,768]{2,1,0:T(8,128)(2,1)S(1)}, bf16[4,120,768]{2,1,0:T(8,128)(2,1)S(1)}, u32[]{:S(2)}, u32[]{:S(2)}) %collective-permute-start.18) | collective-permute-done | bytes 737312 | tf_op jit(solution)/shard_map/ppermute | solution.py:84
  112.8 16.4 %collective-permute-done.24 = bf16[4,96,768]{2,1,0:T(8,128)(2,1)S(1)} collective-permute-done((bf16[4,96,768]{2,1,0:T(8,128)(2,1)S(1)}, bf16[4,96,768]{2,1,0:T(8,128)(2,1)S(1)}, u32[]{:S(2)}, u32[]{:S(2)}) %collective-permute-start.24) | collective-permute-done | bytes 589856 | tf_op jit(solution)/shard_map/ppermute | solution.py:84
  136.3 11.2 %assemble.3 = (bf16[768,768]{1,0:T(8,128)(2,1)}, bf16[768,768]{1,0:T(8,128)(2,1)}, bf16[768,768]{1,0:T(8,128)(2,1)}, bf16[256,768]{1,0:T(8,128)(2,1)}) custom-call(s32[17]{0:T(128)} %pad_add_fusion.spot_ref, bf16[16,80,768]{2,1,0:T(8,128)(2,1)} %copy-done.26, bf16[16,80,768]{2,1,0:T(8,128)(2,1)} %copy-done.28), custom_call_target="tpu_custom_call" | custom-call | bytes 7864320 | tf_op jit(solution)/shard_map/assemble/pallas_call | solution.py:191
  149.5 8.1 %collective-permute-done.1 = bf16[256,768]{0,1:T(8,128)(2,1)} collective-permute-done((bf16[256,768]{0,1:T(8,128)(2,1)}, bf16[256,768]{0,1:T(8,128)(2,1)}, u32[]{:S(2)}, u32[]{:S(2)}) %collective-permute-start.1) | collective-permute-done | bytes 393248 | tf_op jit(solution)/shard_map/ppermute | solution.py:95
  174.2 8.9 %collective-permute-start.31 = (bf16[256,768]{0,1:T(8,128)(2,1)}, bf16[256,768]{0,1:T(8,128)(2,1)S(1)}, u32[]{:S(2)}, u32[]{:S(2)}) collective-permute-start(bf16[256,768]{0,1:T(8,128)(2,1)} %bitcast.33), channel_id=1, source_target_pairs={{0,4},{1,5},{2,6},{3,7},{4,0},{5,1},{6,2},{7,3},{8,12},{9,13},{10,... | collective-permute-start | bytes 1179656 | tf_op jit(solution)/shard_map/ppermute | solution.py:95
  183.1 11.3 %assemble.5 = bf16[3072,768]{1,0:T(8,128)(2,1)} custom-call(s32[17]{0:T(128)} %pad_add_fusion.spot_ref, bf16[16,96,768]{2,1,0:T(8,128)(2,1)} %constant_dynamic-update-slice_fusion.19.mine_ref, bf16[16,96,768]{2,1,0:T(8,128)(2,1)} %collective-permute-done.26.other_ref), custom_call_target="tpu_custom_call" | custom-call | bytes 9437184 | tf_op jit(solution)/shard_map/assemble/pallas_call | solution.py:191
  195.2 11.8 %assemble.4 = (bf16[768,768]{1,0:T(8,128)(2,1)}, bf16[768,3072]{1,0:T(8,128)(2,1)}) custom-call(s32[17]{0:T(128)} %pad_add_fusion.spot_ref, bf16[16,120,768]{2,1,0:T(8,128)(2,1)} %constant_dynamic-update-slice_fusion.12.mine_ref, bf16[16,120,768]{2,1,0:T(8,128)(2,1)} %collective-permute-done.19.other_ref), custom_call_target="tpu_custom_call" | custom-call | bytes 11796480 | tf_op jit(solution)/shard_map/assemble/pallas_call | solution.py:191
  208.1 16.0 %attention.3 = (bf16[1024,768]{1,0:T(8,128)(2,1)S(1)}, f32[6,8,1024]{2,1,0:T(8,128)S(1)}) custom-call(bf16[1024,768]{1,0:T(8,128)(2,1)S(1)} %add_convert_fusion.2.q_ref.refs_0_.refs_2_, bf16[2048,128]{1,0:T(8,128)(2,1)S(1)} %broadcast_in_dim.65.bias_ref, bf16[1024,768]{1,0:T(8,128)(2,1)S(1)} %add_convert_fusion.2.q_ref.refs_0_.refs_2_, ...), custom_call_target="tpu_custom_call" | custom-call | flops 8589934592 | bytes 6291456 | tf_op jit(solution)/shard_map/attention/pallas_call | solution.py:301
  224.2 17.0 %attention.4 = (bf16[1024,768]{1,0:T(8,128)(2,1)S(1)}, f32[6,8,1024]{2,1,0:T(8,128)S(1)}) custom-call(bf16[1024,768]{1,0:T(8,128)(2,1)} %add_convert_fusion.3.q_ref.refs_0_.refs_2_, bf16[2048,128]{1,0:T(8,128)(2,1)S(1)} %broadcast_in_dim.65.bias_ref, ...), custom_call_target="tpu_custom_call", output_to_operand_aliasing={{0}: (6, {}), {1}: (7, {})} | custom-call | flops 8589934592 | bytes 6291456 | tf_op jit(solution)/shard_map/attention/pallas_call | solution.py:301
  241.2 16.0 %attention.5 = (bf16[1024,768]{1,0:T(8,128)(2,1)S(1)}, f32[6,8,1024]{2,1,0:T(8,128)S(1)}) custom-call(bf16[1024,768]{1,0:T(8,128)(2,1)S(1)} %copy-done.8, bf16[2048,128]{1,0:T(8,128)(2,1)S(1)} %broadcast_in_dim.65.bias_ref, bf16[1024,768]{1,0:T(8,128)(2,1)S(1)} %copy-done.8, ...), custom_call_target="tpu_custom_call", output_to_operand_aliasing={{0}: (6, {}), {1}: (7, {})} | custom-call | flops 8589934592 | bytes 6291456 | tf_op jit(solution)/shard_map/attention/pallas_call | solution.py:301
  261.7 47.8 %fusion.2 = (bf16[1024,3072]{1,0:T(8,128)(2,1)}, f32[1024,3072]{1,0:T(8,128)}) fusion(f32[3072]{0:T(1024)S(1)} %copy-done.51, bf16[768,3072]{1,0:T(8,128)(2,1)S(1)} %bitcast.370, f32[1024,768]{0,1:T(8,128)S(1)} %get-tuple-element.83, f32[768]{0:T(1024)S(1)} %copy-done.54, f32[768]{0:T(1024)S(1)} %mul.226, f32[1024]{0:T(1024)S(1)} %add_rsqrt_fusion.1, ...), kind=kOutput, calls=%fused_computation.4 | convolution fusion | flops 5043388416 | bytes 26765312 | tf_op jit(solution)/shard_map/dot_general | solution.py:19
  309.5 7.5 %fusion.111 = (f32[1024]{0:T(1024)S(1)}, f32[1024,768]{0,1:T(8,128)S(1)}) fusion(f32[768]{0:T(1024)S(1)} %copy-done.55, bf16[1024,3072]{1,0:T(8,128)(2,1)} %get-tuple-element.186, bf16[3072,768]{1,0:T(8,128)(2,1)S(1)} %bitcast.304, f32[768]{0:T(1024)S(1)} %copy-done.54, f32[768]{0:T(1024)S(1)} %mul.226, f32[1024]{0:T(1024)S(1)} %add_rsqrt_fusion.1, ...), kind=kOutput, calls=%fused_computation.361 | convolution fusion | flops 4838915072 | bytes 17323008 | tf_op jit(solution)/shard_map/dot_general | solution.py:19
  332.0 11.8 %fusion.112 = (bf16[3072]{0:T(1024)(128)(2,1)S(1)}, bf16[1024,3072]{1,0:T(8,128)(2,1)S(1)}) fusion(f32[1024,3072]{1,0:T(8,128)} %get-tuple-element.187, f32[3072]{0:T(1024)S(1)} %copy-done.51, bf16[1024,768]{0,1:T(8,128)(2,1)S(1)} %get-tuple-element.79, bf16[3072,768]{1,0:T(8,128)(2,1)S(1)} %bitcast.304), kind=kOutput, calls=%fused_computation.362 | convolution fusion | flops 4869583872 | bytes 25184256 | tf_op jit(solution)/shard_map/dot_general | solution.py:27
  343.8 7.2 %convolution_convert_fusion.1 = bf16[768,3072]{1,0:T(8,128)(2,1)} fusion(bf16[1024,3072]{1,0:T(8,128)(2,1)S(1)} %get-tuple-element.192, f32[1024,768]{0,1:T(8,128)S(1)} %get-tuple-element.83, f32[768]{0:T(1024)S(1)} %copy-done.54, f32[768]{0:T(1024)S(1)} %mul.226, f32[1024]{0:T(1024)S(1)} %add_rsqrt_fusion.1, f32[1024]{0:T(1024)S(1)} %broadcast_multiply_fusion.5), kind=kOutput, calls=%fused_computation.26 | convolution fusion | flops 4838129664 | bytes 14170112 | tf_op jit(solution)/shard_map/dot_general | solution.py:23
  351.0 8.0 %multiply_reduce_fusion.1 = (bf16[768]{0:T(1024)(128)(2,1)S(1)}, f32[1024]{0:T(1024)S(1)}, f32[1024]{0:T(1024)S(1)}, bf16[768]{0:T(1024)(128)(2,1)S(1)}, f32[1024,768]{0,1:T(8,128)S(1)}) fusion(f32[1024,768]{0,1:T(8,128)S(1)} %get-tuple-element.83, f32[1024]{0:T(1024)S(1)} %add_rsqrt_fusion.1, f32[1024]{0:T(1024)S(1)} %broadcast_multiply_fusion.5, ...), kind=kOutput, calls=%fused_computation.32 | convolution fusion | flops 4852281344 | bytes 22066176 | tf_op jit(solution)/shard_map/dot_general | solution.py:27
  368.4 25.5 %attention_back.5 = (bf16[1024,768]{1,0:T(8,128)(2,1)S(1)}, bf16[1024,512]{1,0:T(8,128)(2,1)S(1)}) custom-call(bf16[1024,768]{1,0:T(8,128)(2,1)S(1)} %copy-done.9, bf16[2048,128]{1,0:T(8,128)(2,1)S(1)} %copy-done.3, f32[6,8,1024]{2,1,0:T(8,128)S(1)} %copy-done.17, bf16[1024,768]{1,0:T(8,128)(2,1)} %copy-done.14, ...), custom_call_target="tpu_custom_call" | custom-call | flops 21474836480 | bytes 9437184 | tf_op jit(solution)/shard_map/attention_back/pallas_call | solution.py:394
  395.0 25.2 %attention_back.3 = (bf16[1024,768]{1,0:T(8,128)(2,1)S(1)}, bf16[1024,512]{1,0:T(8,128)(2,1)S(1)}) custom-call(bf16[1024,768]{1,0:T(8,128)(2,1)S(1)} %copy-done.6, bf16[2048,128]{1,0:T(8,128)(2,1)S(1)} %copy-done.4, f32[6,8,1024]{2,1,0:T(8,128)S(1)} %copy-done.17, bf16[1024,768]{1,0:T(8,128)(2,1)} %copy-done.14, ...), custom_call_target="tpu_custom_call" | custom-call | flops 21474836480 | bytes 9437184 | tf_op jit(solution)/shard_map/attention_back/pallas_call | solution.py:394
  422.1 25.8 %attention_back.4 = (bf16[1024,768]{1,0:T(8,128)(2,1)S(1)}, bf16[1024,512]{1,0:T(8,128)(2,1)S(1)}) custom-call(bf16[1024,768]{1,0:T(8,128)(2,1)} %add_convert_fusion.3.q_ref.refs_0_.refs_2_, bf16[2048,128]{1,0:T(8,128)(2,1)S(1)} %copy-done.4, f32[6,8,1024]{2,1,0:T(8,128)S(1)} %copy-done.17, bf16[1024,768]{1,0:T(8,128)(2,1)} %copy-done.14, ...), custom_call_target="tpu_custom_call" | custom-call | flops 21474836480 | bytes 9437184 | tf_op jit(solution)/shard_map/attention_back/pallas_call | solution.py:394
  481.7 10.1 %collective-permute-done.27 = bf16[256,768]{0,1:T(8,128)(2,1)S(1)} collective-permute-done((bf16[256,768]{0,1:T(8,128)(2,1)}, bf16[256,768]{0,1:T(8,128)(2,1)S(1)}, u32[]{:S(2)}, u32[]{:S(2)}) %collective-permute-start.27) | collective-permute-done | bytes 393248 | tf_op jit(solution)/shard_map/ppermute | solution.py:95
  572.4 18.6 %collective-permute-done.37 = bf16[256,768]{0,1:T(8,128)(2,1)} collective-permute-done((bf16[256,768]{0,1:T(8,128)(2,1)S(1)}, bf16[256,768]{0,1:T(8,128)(2,1)}, u32[]{:S(2)}, u32[]{:S(2)}) %collective-permute-start.37) | collective-permute-done | bytes 393248 | tf_op jit(solution)/shard_map/ppermute | solution.py:95
  617.4 7.9 %collective-permute-start.43 = (bf16[24,768]{1,0:T(8,128)(2,1)S(1)}, bf16[24,768]{1,0:T(8,128)(2,1)S(1)}, u32[]{:S(2)}, u32[]{:S(2)}) collective-permute-start(bf16[24,768]{1,0:T(8,128)(2,1)S(1)} %get-tuple-element.135), channel_id=1, source_target_pairs={{0,2},{1,3},{2,0},{3,1},{4,6},{5,7},{6,4},{7,5},{8,10},{9,11},{10,... | collective-permute-start | bytes 110600 | tf_op jit(solution)/shard_map/ppermute | solution.py:80
  671.7 8.6 %collective-permute-done.76 = bf16[384,768]{1,0:T(8,128)(2,1)S(1)} collective-permute-done((bf16[384,768]{1,0:T(8,128)(2,1)S(1)}, bf16[384,768]{1,0:T(8,128)(2,1)S(1)}, u32[]{:S(2)}, u32[]{:S(2)}) %collective-permute-start.76) | collective-permute-done | bytes 589856 | tf_op jit(solution)/shard_map/ppermute | solution.py:84
  682.9 7.2 %collective-permute-done.68 = bf16[96,3072]{1,0:T(8,128)(2,1)S(1)} collective-permute-done((bf16[96,3072]{1,0:T(8,128)(2,1)S(1)}, bf16[96,3072]{1,0:T(8,128)(2,1)S(1)}, u32[]{:S(2)}, u32[]{:S(2)}) %collective-permute-start.68) | collective-permute-done | bytes 589856 | tf_op jit(solution)/shard_map/ppermute | solution.py:84
  (546 shorter events, 345.1 us)
Async XLA Ops:
  13.9 31.1 %collective-permute-start.20 = (bf16[96,768]{1,0:T(8,128)(2,1)}, bf16[96,768]{1,0:T(8,128)(2,1)}, u32[]{:S(2)}, u32[]{:S(2)}) collective-permute-start(bf16[96,768]{1,0:T(8,128)(2,1)} %param.27), channel_id=1, source_target_pairs={{0,2},{1,3},{2,0},{3,1},{4,6},{5,7},{6,4},{7,5},{8,10},{9,11},{10,... | collective-permute-start | bytes 442376 | tf_op jit(solution)/shard_map/ppermute | solution.py:80
  60.5 51.5 %collective-permute-start.23 = (bf16[4,96,768]{2,1,0:T(8,128)(2,1)S(1)}, bf16[4,96,768]{2,1,0:T(8,128)(2,1)S(1)}, u32[]{:S(2)}, u32[]{:S(2)}) collective-permute-start(bf16[4,96,768]{2,1,0:T(8,128)(2,1)S(1)} %pad_maximum_fusion.14), channel_id=1, source_target_pairs={{0,8},{8,0},{16,24},{24,16},{1,9},{9,1},{17,25},{25,17},{2,10},{10... | collective-permute-start | bytes 1769480 | tf_op jit(solution)/shard_map/ppermute | solution.py:84
  64.3 70.6 %collective-permute-start.9 = (bf16[16,80,768]{2,1,0:T(8,128)(2,1)S(1)}, bf16[16,80,768]{2,1,0:T(8,128)(2,1)S(1)}, u32[]{:S(2)}, u32[]{:S(2)}) collective-permute-start(bf16[16,80,768]{2,1,0:T(8,128)(2,1)S(1)} %constant_dynamic-update-slice_fusion.mine_ref), channel_id=1, source_target_pairs={{0,1},{1,0},{2,3},{3,2},{4,5},{5,4},{6,7},{7,6},{8,9},{9,8},{10,11... | collective-permute-start | bytes 5898248 | tf_op jit(solution)/shard_map/ppermute | solution.py:87
  69.5 40.8 %collective-permute-start.18 = (bf16[4,120,768]{2,1,0:T(8,128)(2,1)S(1)}, bf16[4,120,768]{2,1,0:T(8,128)(2,1)S(1)}, u32[]{:S(2)}, u32[]{:S(2)}) collective-permute-start(bf16[4,120,768]{2,1,0:T(8,128)(2,1)S(1)} %pad_maximum_fusion.13), channel_id=1, source_target_pairs={{0,24},{8,16},{16,8},{24,0},{1,25},{9,17},{17,9},{25,1},{2,26},{10... | collective-permute-start | bytes 2211848 | tf_op jit(solution)/shard_map/ppermute | solution.py:84
  92.5 36.8 %collective-permute-start.24 = (bf16[4,96,768]{2,1,0:T(8,128)(2,1)S(1)}, bf16[4,96,768]{2,1,0:T(8,128)(2,1)S(1)}, u32[]{:S(2)}, u32[]{:S(2)}) collective-permute-start(bf16[4,96,768]{2,1,0:T(8,128)(2,1)S(1)} %pad_maximum_fusion.14), channel_id=1, source_target_pairs={{0,16},{8,24},{16,0},{24,8},{1,17},{9,25},{17,1},{25,9},{2,18},{10... | collective-permute-start | bytes 1769480 | tf_op jit(solution)/shard_map/ppermute | solution.py:84
  95.7 36.2 %collective-permute-start.25 = (bf16[4,96,768]{2,1,0:T(8,128)(2,1)S(1)}, bf16[4,96,768]{2,1,0:T(8,128)(2,1)S(1)}, u32[]{:S(2)}, u32[]{:S(2)}) collective-permute-start(bf16[4,96,768]{2,1,0:T(8,128)(2,1)S(1)} %pad_maximum_fusion.14), channel_id=1, source_target_pairs={{0,24},{8,16},{16,8},{24,0},{1,25},{9,17},{17,9},{25,1},{2,26},{10... | collective-permute-start | bytes 1769480 | tf_op jit(solution)/shard_map/ppermute | solution.py:84
  110.3 38.5 %collective-permute-start = (bf16[256,768]{0,1:T(8,128)(2,1)}, bf16[256,768]{0,1:T(8,128)(2,1)}, u32[]{:S(2)}, u32[]{:S(2)}) collective-permute-start(bf16[256,768]{0,1:T(8,128)(2,1)} %bitcast.1), channel_id=1, source_target_pairs={{0,2},{1,3},{2,0},{3,1},{4,6},{5,7},{6,4},{7,5},{8,10},{9,11},{10,... | collective-permute-start | bytes 1179656 | tf_op jit(solution)/shard_map/ppermute | solution.py:95
  111.9 82.5 %collective-permute-start.19 = (bf16[16,120,768]{2,1,0:T(8,128)(2,1)}, bf16[16,120,768]{2,1,0:T(8,128)(2,1)}, u32[]{:S(2)}, u32[]{:S(2)}) collective-permute-start(bf16[16,120,768]{2,1,0:T(8,128)(2,1)} %constant_dynamic-update-slice_fusion.12.mine_ref), channel_id=1, source_target_pairs={{0,1},{1,0},{2,3},{3,2},{4,5},{5,4},{6,7},{7,6},{8,9},{9,8},{10,11... | collective-permute-start | bytes 8847368 | tf_op jit(solution)/shard_map/ppermute | solution.py:87
  136.3 37.9 %collective-permute-start.26 = (bf16[16,96,768]{2,1,0:T(8,128)(2,1)}, bf16[16,96,768]{2,1,0:T(8,128)(2,1)}, u32[]{:S(2)}, u32[]{:S(2)}) collective-permute-start(bf16[16,96,768]{2,1,0:T(8,128)(2,1)} %constant_dynamic-update-slice_fusion.19.mine_ref), channel_id=1, source_target_pairs={{0,1},{1,0},{2,3},{3,2},{4,5},{5,4},{6,7},{7,6},{8,9},{9,8},{10,11... | collective-permute-start | bytes 7077896 | tf_op jit(solution)/shard_map/ppermute | solution.py:87
  148.9 168.6 %collective-permute-start.30 = (bf16[256,768]{0,1:T(8,128)(2,1)}, bf16[256,768]{0,1:T(8,128)(2,1)}, u32[]{:S(2)}, u32[]{:S(2)}) collective-permute-start(bf16[256,768]{0,1:T(8,128)(2,1)} %bitcast.32), channel_id=1, source_target_pairs={{0,2},{1,3},{2,0},{3,1},{4,6},{5,7},{6,4},{7,5},{8,10},{9,11},{10,... | collective-permute-start | bytes 1179656 | tf_op jit(solution)/shard_map/ppermute | solution.py:95
  160.9 46.1 %collective-permute-start.12 = (bf16[1024,768]{1,0:T(8,128)(2,1)S(1)}, bf16[1024,768]{1,0:T(8,128)(2,1)S(1)}, u32[]{:S(2)}, u32[]{:S(2)}) collective-permute-start(bf16[1024,768]{1,0:T(8,128)(2,1)S(1)} %add_convert_fusion.2.q_ref.refs_0_.refs_2_), channel_id=1, source_target_pairs={{0,1},{1,0},{2,3},{3,2},{4,5},{5,4},{6,7},{7,6},{8,9},{9,8},{10,11... | collective-permute-start | bytes 4718600 | tf_op jit(solution)/shard_map/ppermute | solution.py:103
  166.2 57.9 %collective-permute-start.11 = (bf16[1024,768]{1,0:T(8,128)(2,1)}, bf16[1024,768]{1,0:T(8,128)(2,1)}, u32[]{:S(2)}, u32[]{:S(2)}) collective-permute-start(bf16[1024,768]{1,0:T(8,128)(2,1)} %add_convert_fusion.3.q_ref.refs_0_.refs_2_), channel_id=1, source_target_pairs={{0,1},{1,0},{2,3},{3,2},{4,5},{5,4},{6,7},{7,6},{8,9},{9,8},{10,11... | collective-permute-start | bytes 4718600 | tf_op jit(solution)/shard_map/ppermute | solution.py:103
  174.2 143.3 %collective-permute-start.31 = (bf16[256,768]{0,1:T(8,128)(2,1)}, bf16[256,768]{0,1:T(8,128)(2,1)S(1)}, u32[]{:S(2)}, u32[]{:S(2)}) collective-permute-start(bf16[256,768]{0,1:T(8,128)(2,1)} %bitcast.33), channel_id=1, source_target_pairs={{0,4},{1,5},{2,6},{3,7},{4,0},{5,1},{6,2},{7,3},{8,12},{9,13},{10,... | collective-permute-start | bytes 1179656 | tf_op jit(solution)/shard_map/ppermute | solution.py:95
  194.4 123.1 %collective-permute-start.32 = (bf16[256,768]{0,1:T(8,128)(2,1)}, bf16[256,768]{0,1:T(8,128)(2,1)}, u32[]{:S(2)}, u32[]{:S(2)}) collective-permute-start(bf16[256,768]{0,1:T(8,128)(2,1)} %bitcast.351), channel_id=1, source_target_pairs={{0,6},{1,7},{2,4},{3,5},{4,2},{5,3},{6,0},{7,1},{8,14},{9,15},{10,... | collective-permute-start | bytes 1179656 | tf_op jit(solution)/shard_map/ppermute | solution.py:95
  207.0 34.2 %collective-permute-start.10 = (bf16[1024,768]{1,0:T(8,128)(2,1)}, bf16[1024,768]{1,0:T(8,128)(2,1)S(1)}, u32[]{:S(2)}, u32[]{:S(2)}) collective-permute-start(bf16[1024,768]{1,0:T(8,128)(2,1)} %add_convert_fusion.4.q_ref.refs_0_.refs_2_), channel_id=1, source_target_pairs={{0,1},{1,0},{2,3},{3,2},{4,5},{5,4},{6,7},{7,6},{8,9},{9,8},{10,11... | collective-permute-start | bytes 4718600 | tf_op jit(solution)/shard_map/ppermute | solution.py:103
  366.5 91.8 %collective-permute-start.88 = (bf16[16,1,240]{2,1,0:T(2,128)(2,1)S(1)}, bf16[16,1,240]{2,1,0:T(2,128)(2,1)S(1)}, u32[]{:S(2)}, u32[]{:S(2)}) collective-permute-start(bf16[16,1,240]{2,1,0:T(2,128)(2,1)S(1)} %fusion.65), channel_id=1, source_target_pairs={{0,1},{1,0},{2,3},{3,2},{4,5},{5,4},{6,7},{7,6},{8,9},{9,8},{10,11... | collective-permute-start | bytes 23048 | tf_op jit(solution)/shard_map/ppermute | solution.py:87
  450.2 74.3 %collective-permute-start.35 = (bf16[1024,512]{1,0:T(8,128)(2,1)}, bf16[1024,512]{1,0:T(8,128)(2,1)}, u32[]{:S(2)}, u32[]{:S(2)}) collective-permute-start(bf16[1024,512]{1,0:T(8,128)(2,1)} %copy-done.11), channel_id=1, source_target_pairs={{0,1},{1,0},{2,3},{3,2},{4,5},{5,4},{6,7},{7,6},{8,9},{9,8},{10,11... | collective-permute-start | bytes 3145736 | tf_op jit(solution)/shard_map/ppermute | solution.py:103
  457.8 35.9 %collective-permute-start.60 = (bf16[16,24,768]{2,1,0:T(8,128)(2,1)}, bf16[16,24,768]{2,1,0:T(8,128)(2,1)}, u32[]{:S(2)}, u32[]{:S(2)}) collective-permute-start(bf16[16,24,768]{2,1,0:T(8,128)(2,1)} %dynamic-slice_bitcast_fusion.8), channel_id=1, source_target_pairs={{0,1},{1,0},{2,3},{3,2},{4,5},{5,4},{6,7},{7,6},{8,9},{9,8},{10,11... | collective-permute-start | bytes 1769480 | tf_op jit(solution)/shard_map/ppermute | solution.py:87
  479.4 31.4 %collective-permute-start.29 = (bf16[256,768]{0,1:T(8,128)(2,1)}, bf16[256,768]{0,1:T(8,128)(2,1)}, u32[]{:S(2)}, u32[]{:S(2)}) collective-permute-start(bf16[256,768]{0,1:T(8,128)(2,1)} %get-tuple-element.106), channel_id=1, source_target_pairs={{0,6},{1,7},{2,4},{3,5},{4,2},{5,3},{6,0},{7,1},{8,14},{9,15},{10,... | collective-permute-start | bytes 1179656 | tf_op jit(solution)/shard_map/ppermute | solution.py:95
  521.9 126.7 %collective-permute-start.74 = (bf16[16,96,768]{2,1,0:T(8,128)(2,1)}, bf16[16,96,768]{2,1,0:T(8,128)(2,1)}, u32[]{:S(2)}, u32[]{:S(2)}) collective-permute-start(bf16[16,96,768]{2,1,0:T(8,128)(2,1)} %dynamic-slice_bitcast_fusion), channel_id=1, source_target_pairs={{0,1},{1,0},{2,3},{3,2},{4,5},{5,4},{6,7},{7,6},{8,9},{9,8},{10,11... | collective-permute-start | bytes 7077896 | tf_op jit(solution)/shard_map/ppermute | solution.py:87
  536.2 59.8 %collective-permute-start.39 = (bf16[16,24,768]{2,1,0:T(8,128)(2,1)}, bf16[16,24,768]{2,1,0:T(8,128)(2,1)}, u32[]{:S(2)}, u32[]{:S(2)}) collective-permute-start(bf16[16,24,768]{2,1,0:T(8,128)(2,1)} %dynamic-slice_bitcast_fusion.11), channel_id=1, source_target_pairs={{0,1},{1,0},{2,3},{3,2},{4,5},{5,4},{6,7},{7,6},{8,9},{9,8},{10,11... | collective-permute-start | bytes 1769480 | tf_op jit(solution)/shard_map/ppermute | solution.py:87
  570.5 84.4 %collective-permute-start.67 = (bf16[16,24,3072]{2,1,0:T(8,128)(2,1)}, bf16[16,24,3072]{2,1,0:T(8,128)(2,1)}, u32[]{:S(2)}, u32[]{:S(2)}) collective-permute-start(bf16[16,24,3072]{2,1,0:T(8,128)(2,1)} %dynamic-slice_bitcast_fusion.1), channel_id=1, source_target_pairs={{0,1},{1,0},{2,3},{3,2},{4,5},{5,4},{6,7},{7,6},{8,9},{9,8},{10,11... | collective-permute-start | bytes 7077896 | tf_op jit(solution)/shard_map/ppermute | solution.py:87
  657.6 32.6 %collective-permute-start.68 = (bf16[96,3072]{1,0:T(8,128)(2,1)S(1)}, bf16[96,3072]{1,0:T(8,128)(2,1)S(1)}, u32[]{:S(2)}, u32[]{:S(2)}) collective-permute-start(bf16[96,3072]{1,0:T(8,128)(2,1)S(1)} %get-tuple-element.88), channel_id=1, source_target_pairs={{0,8},{8,0},{16,24},{24,16},{1,9},{9,1},{17,25},{25,17},{2,10},{10... | collective-permute-start | bytes 1769480 | tf_op jit(solution)/shard_map/ppermute | solution.py:84
  659.1 37.1 %collective-permute-start.69 = (bf16[96,3072]{1,0:T(8,128)(2,1)S(1)}, bf16[96,3072]{1,0:T(8,128)(2,1)S(1)}, u32[]{:S(2)}, u32[]{:S(2)}) collective-permute-start(bf16[96,3072]{1,0:T(8,128)(2,1)S(1)} %get-tuple-element.90), channel_id=1, source_target_pairs={{0,16},{8,24},{16,0},{24,8},{1,17},{9,25},{17,1},{25,9},{2,18},{10... | collective-permute-start | bytes 1769480 | tf_op jit(solution)/shard_map/ppermute | solution.py:84
  (144 other events, 1800.1 us)

commit v3 on v2

--- a/solution.py
+++ b/solution.py
@@ -108,107 +108,233 @@
 
 
 def to_sequences(grid, array_in):
-    parts = [take_block(array_in, grid.owner)]
+    out = jnp.zeros_like(array_in)
+    out = lax.dynamic_update_index_in_dim(out, take_block(array_in, grid.owner), grid.owner, 0)
     for step in range(1, grid.seqs):
-        target = swap_index(grid.owner, step, grid.seqs)
-        parts.append(grid.to_owner(take_block(array_in, target), step))
-    return jnp.concatenate(parts, axis=0)
+        place = swap_index(grid.owner, step, grid.seqs)
+        got = grid.to_owner(take_block(array_in, place), step)
+        out = lax.dynamic_update_index_in_dim(out, got, place, 0)
+    return out.reshape(-1, array_in.shape[2])
 
 
 def from_sequences(grid, rows, length):
-    blocks = rows.reshape(grid.seqs, length, rows.shape[1])
-    out = jnp.zeros_like(blocks)
-    out = lax.dynamic_update_index_in_dim(out, blocks[0], grid.owner, 0)
-    for step in range(1, grid.seqs):
-        got = grid.to_owner(blocks[step], step, back=True)
-        place = swap_index(grid.owner, step, grid.seqs)
-        out = lax.dynamic_update_index_in_dim(out, got, place, 0)
-    return out
+    return to_sequences(grid, rows.reshape(grid.seqs, length, rows.shape[1])).reshape(grid.seqs, length, -1)
 
 
 def row_positions(grid, length):
     def positions(member):
-        spots = []
-        for step in range(grid.seqs):
-            source = source_index(grid.owner, step, grid.seqs)
-            spots.append((source * grid.group + member) * length + jnp.arange(length, dtype=jnp.int32))
-        return jnp.concatenate(spots)
+        source = jnp.arange(grid.seqs, dtype=jnp.int32)[:, None]
+        return ((source * grid.group + member) * length + jnp.arange(length, dtype=jnp.int32)).reshape(-1)
 
     return positions
 
 
-def gather_packed(grid, shard):
-    parts = [shard] + [grid.to_chip(shard, step) for step in range(1, grid.chips)]
-    chips = jnp.stack(parts)
-    wide = [chips] + [grid.to_column(chips, step) for step in range(1, grid.columns)]
-    mine = jnp.concatenate(wide, axis=0)
-    other = grid.to_core(mine)
-    return mine, other
-
-
-def relative_order(grid):
-    column = jnp.arange(grid.columns, dtype=jnp.int32)[:, None]
-    chip = jnp.arange(grid.chips, dtype=jnp.int32)[None, :]
-    if grid.columns & (grid.columns - 1) == 0:
-        column_step = column ^ grid.column
-    else:
-        column_step = (grid.column - column) % grid.columns
-    if grid.chips & (grid.chips - 1) == 0:
-        chip_step = chip ^ grid.chip
-    else:
-        chip_step = (grid.chip - chip) % grid.chips
-    return (column_step * grid.chips + chip_step).reshape(-1)
-
-
-def assemble(grid, mine, other, cuts):
-    order = relative_order(grid)
-    count, rows, width = mine.shape
-    spot = jnp.concatenate([grid.core[None].astype(jnp.int32), order])
-    wides = [sum(piece[3] for piece in pieces) for _, pieces in cuts]
-    if any(height % 8 for height, _ in cuts):
-        first = jnp.where(grid.core == 0, mine, other)[order]
-        second = jnp.where(grid.core == 0, other, mine)[order]
-        both = jnp.stack([first, second], axis=1).reshape(2 * count, rows, width)
-        outs = []
-        for height, pieces in cuts:
-            ordered = sorted(pieces, key=lambda piece: piece[2])
-            strips = [both[:, p[0] : p[0] + height, p[1] : p[1] + p[3]] for p in ordered]
-            outs.append(jnp.concatenate(strips, axis=2).reshape(2 * count * height, -1))
-        return outs
-
-    def kernel(spot_ref, mine_ref, other_ref, *out_refs):
-        for core in range(2):
-
-            @pl.when(spot_ref[0] == core)
-            def _(core=core):
-                for source, place in ((mine_ref, core), (other_ref, 1 - core)):
-                    for (height, pieces), out_ref in zip(cuts, out_refs):
-                        for row, column, target, columns in pieces:
-                            out_ref[place * height : (place + 1) * height, target : target + columns] = source[
-                                row : row + height, column : column + columns
-                            ]
-
+MESH = pl.DeviceIdType.MESH
+HBM = pl.BlockSpec(memory_space=pl.ANY)
+
+
+def remote(source, target, send, receive, device):
+    return pltpu.make_async_remote_copy(
+        src_ref=source, dst_ref=target, send_sem=send, recv_sem=receive, device_id=device, device_id_type=MESH
+    )
+
+
+def meet(devices):
+    barrier = pltpu.get_barrier_semaphore()
+    for device in devices:
+        pl.semaphore_signal(barrier, inc=1, device_id=device, device_id_type=MESH)
+    pl.semaphore_wait(barrier, len(devices))
+
+
+class Place:
+    def __init__(self, grid):
+        self.columns, self.chips, self.n = grid.columns, grid.chips, grid.n
+        self.seqs, self.group = grid.seqs, grid.group
+        self.column = lax.axis_index("dp")
+        self.spot = lax.axis_index("seq")
+        self.chip = lax.div(self.spot, 2)
+        self.core = lax.rem(self.spot, 2)
+        self.owner = lax.div(self.spot, self.group)
+        self.member = lax.rem(self.spot, self.group)
+
+    def near(self, chip_step):
+        return (self.column, (self.chip ^ chip_step) * 2 + self.core)
+
+    def beside(self, column_step):
+        return (self.column ^ column_step, self.spot)
+
+    def twin(self):
+        return (self.column, self.chip * 2 + (1 - self.core))
+
+    def at_owner(self, step):
+        return (self.column, (self.owner ^ step) * self.group + self.member)
+
+    def at_member(self, step):
+        return (self.column, self.owner * self.group + lax.rem(self.member + step, self.group))
+
+    def index(self, column_step, chip_step, other=False):
+        core = 1 - self.core if other else self.core
+        return ((self.column ^ column_step) * self.chips + (self.chip ^ chip_step)) * 2 + core
+
+    def neighbours(self):
+        chips = [self.near(step) for step in range(1, self.chips)]
+        columns = [self.beside(step) for step in range(1, self.columns)]
+        return chips + columns + [self.twin()]
+
+
+class Gather:
+    def __init__(self, place, arrays, send, receive):
+        self.place, self.arrays, self.send, self.receive = place, arrays, send, receive
+        self.square = place.columns == 4
+        self.sent = []
+
+    def copies(self, kind, column_step, chip_step, device, own=False, where=None):
+        slot = column_step * self.place.chips + chip_step
+        for k, (shard, whole, block) in enumerate(self.arrays):
+            held = block(whole, self.place.index(*(where or (column_step, chip_step))))
+            yield remote(
+                shard if own else held, held, self.send.at[k, kind, slot], self.receive.at[k, kind, slot], device
+            )
+
+    def begin(self, kind, column_step, chip_step, device, own=False, where=None):
+        self.sent.append((kind, column_step, chip_step, own, where))
+        for copy in self.copies(kind, column_step, chip_step, device, own, where):
+            copy.start()
+
+    def to_twin(self, column_step, chip_step, own=False):
+        self.begin(1, column_step, chip_step, self.place.twin(), own=own)
+
+    def outward(self, chip_step):
+        place, own = self.place, chip_step == 0
+        for step in range(1, place.columns):
+            if not (self.square and step == 3):
+                self.begin(0, step, chip_step, place.beside(step), own=own, where=(0, chip_step))
+        self.to_twin(0, chip_step, own=own)
+
+    def start(self):
+        for step in range(1, self.place.chips):
+            self.begin(0, 0, step, self.place.near(step), own=True, where=(0, 0))
+        self.outward(0)
+
+    def arrive(self, column_step, chip_step, other=False):
+        for k, (_, whole, block) in enumerate(self.arrays):
+            held = block(whole, self.place.index(column_step, chip_step, other))
+            kind = 1 if other else 0
+            slot = column_step * self.place.chips + chip_step
+            remote(
+                held, held, self.send.at[k, kind, slot], self.receive.at[k, kind, slot], self.place.twin()
+            ).wait_recv()
+
+    def from_chip(self, chip_step):
+        self.arrive(0, chip_step)
+        self.outward(chip_step)
+
+    def from_columns(self, chip_step):
+        for step in range(1, self.place.columns):
+            if self.square and step == 3:
+                continue
+            self.arrive(step, chip_step)
+            if self.square and step == 1 + chip_step % 2:
+                self.begin(0, 3, chip_step, self.place.beside(3 - step), where=(step, chip_step))
+            self.to_twin(step, chip_step)
+
+    def from_corner(self, chip_step):
+        if self.square:
+            self.arrive(3, chip_step)
+            self.to_twin(3, chip_step)
+
+    def finish(self):
+        place = self.place
+        for column_step in range(place.columns):
+            for chip_step in range(place.chips):
+                self.arrive(column_step, chip_step, other=True)
+        for kind, column_step, chip_step, own, where in self.sent:
+            for copy in self.copies(kind, column_step, chip_step, place.twin(), own, where):
+                copy.wait_send()
+
+
+def gather_semaphores(grid, count):
+    shape = (count, 2, grid.columns * grid.chips)
+    return [pltpu.SemaphoreType.DMA(shape), pltpu.SemaphoreType.DMA(shape)]
+
+
+def through(source, held, target, sem):
+    copy = pltpu.make_async_copy(source, held, sem)
+    copy.start()
+    copy.wait()
+    copy = pltpu.make_async_copy(held, target, sem)
+    copy.start()
+    copy.wait()
+
+
+def start_exchange(grid, tokens, into, vectors):
+    seqs, length, width = tokens.shape
+    devices = grid.columns * grid.n
+    parts, slim, _ = into.shape
+
+    def kernel(
+        tokens_ref, into_ref, vectors_ref, rows_ref, into_all, vectors_all, *scratch
+    ):
+        row_hold, into_hold, vector_hold, hold_sem, send, receive, row_send, row_receive = scratch
+        place = Place(grid)
+        meet(place.neighbours())
+        gather = Gather(
+            place,
+            [
+                (into_ref, into_all, lambda ref, i: ref.at[:, i]),
+                (vectors_ref, vectors_all, lambda ref, i: ref.at[i]),
+            ],
+            send,
+            receive,
+        )
+        gather.start()
+
+        def row_copy(step):
+            return remote(
+                tokens_ref.at[place.owner ^ step],
+                rows_ref.at[place.owner],
+                row_send.at[step],
+                row_receive.at[step],
+                place.at_owner(step),
+            )
+
+        for step in range(1, seqs):
+            row_copy(step).start()
+        me = place.index(0, 0)
+        through(into_ref, into_hold, into_all.at[:, me], hold_sem)
+        through(vectors_ref, vector_hold, vectors_all.at[me], hold_sem)
+        through(tokens_ref.at[place.owner], row_hold, rows_ref.at[place.owner], hold_sem)
+        for step in range(1, place.chips):
+            gather.from_chip(step)
+            gather.from_columns(step - 1)
+        gather.from_columns(place.chips - 1)
+        for step in range(place.chips):
+            gather.from_corner(step)
+        gather.finish()
+        for step in range(1, seqs):
+            landed = rows_ref.at[place.owner ^ step]
+            remote(
+                landed, landed, row_send.at[step], row_receive.at[step], place.at_owner(step)
+            ).wait_recv()
+            row_copy(step).wait_send()
+
+    shapes = [tokens.shape, (parts, devices, slim, width), (devices,) + vectors.shape]
     return pl.pallas_call(
         kernel,
-        grid_spec=pltpu.PrefetchScalarGridSpec(
-            num_scalar_prefetch=1,
-            grid=(count,),
-            in_specs=[
-                pl.BlockSpec((None, rows, width), lambda i, spot: (spot[i + 1], 0, 0)),
-                pl.BlockSpec((None, rows, width), lambda i, spot: (spot[i + 1], 0, 0)),
-            ],
-            out_specs=[
-                pl.BlockSpec((2 * height, wide), lambda i, spot: (i, 0))
-                for (height, _), wide in zip(cuts, wides)
-            ],
-        ),
-        out_shape=[
-            jax.ShapeDtypeStruct((2 * count * height, wide), mine.dtype)
-            for (height, _), wide in zip(cuts, wides)
-        ],
-        cost_estimate=pl.CostEstimate(flops=0, bytes_accessed=8 * count * rows * width, transcendentals=0),
-        name="assemble",
-    )(spot, mine, other)
+        in_specs=[HBM] * 3,
+        out_specs=[HBM] * 3,
+        out_shape=[jax.ShapeDtypeStruct(shape, BF) for shape in shapes],
+        scratch_shapes=[
+            pltpu.VMEM(tokens.shape[1:], BF),
+            pltpu.VMEM(into.shape, BF),
+            pltpu.VMEM(vectors.shape, BF),
+            pltpu.SemaphoreType.DMA(()),
+        ]
+        + gather_semaphores(grid, 2)
+        + [pltpu.SemaphoreType.DMA((seqs,)), pltpu.SemaphoreType.DMA((seqs,))],
+        compiler_params=pltpu.CompilerParams(collective_id=0, has_side_effects=True),
+        name="start_exchange",
+    )(tokens, into, vectors)
 
 
 def scatter_sum(grid, array_in):
@@ -230,7 +356,6 @@
     return total
 
 
-PARTS = 3
 LOG2E = 1.4426950408889634
 SCALE = 0.125 * LOG2E
 
@@ -244,26 +369,86 @@
     return (lane // HD) == half, lane == HD * (1 - half)
 
 
-def attention(part, inputs, others, key_bias, context, log_totals, block=256):
-    rows, width = inputs.shape
-    pairs = width // (6 * HD)
-    sources = [inputs] + list(others)
-    count = len(sources)
+def attention(grid, inputs, key_bias, shards, block=256):
+    rows = inputs.shape[0]
+    width = inputs.shape[1] // 3
+    pairs = width // (2 * HD)
+    count = grid.group
     keys = rows * count
-
-    def kernel(q_ref, bias_ref, *refs):
-        k_refs, v_refs = refs[:count], refs[count : 2 * count]
-        o_ref, l_ref, k_own, v_own = refs[-4:]
-
-        @pl.when(pl.program_id(1) == 0)
+    blocks = rows // block
+    steps = pairs * blocks
+    devices = grid.columns * grid.n
+    late = len(shards)
+
+    def kernel(q_ref, bias_ref, k_ref, v_ref, all_ref, *refs):
+        shard_refs = refs[:late]
+        o_ref, l_ref = refs[late : late + 2]
+        whole_refs = refs[late + 2 : 2 * late + 2]
+        k_own, v_own, far, hold_sem, send, receive, far_send, far_receive = refs[2 * late + 2 : 2 * late + 10]
+        holds = refs[2 * late + 10 :]
+        pair, turn = pl.program_id(0), pl.program_id(1)
+        now = pair * blocks + turn
+        place = Place(grid)
+        gather = Gather(
+            place,
+            [(s, w, lambda ref, i: ref.at[i]) for s, w in zip(shard_refs, whole_refs)],
+            send,
+            receive,
+        )
+
+        def far_copy(step, which, kind):
+            first = pl.multiple_of(which * 2 * HD + (kind + 1) * width, 2 * HD)
+            return remote(
+                all_ref.at[:, pl.ds(first, 2 * HD)],
+                far.at[step - 1, kind, which],
+                far_send.at[step - 1, kind, which],
+                far_receive.at[step - 1, kind, which],
+                place.at_member(step),
+            )
+
+        def first_step():
+            meet(place.neighbours() + [place.at_member(s) for s in range(1, count) if count > 2])
+            for which in range(pairs):
+                for step in range(1, count):
+                    for kind in range(2):
+                        far_copy(step, which, kind).start()
+            gather.start()
+            me = place.index(0, 0)
+            for shard, whole, hold in zip(shard_refs, whole_refs, holds):
+                through(shard, hold, whole.at[me], hold_sem)
+
+        plan = [(0.0, first_step)]
+        for step in range(1, place.chips):
+            plan.append((step * 0.66 / (place.chips - 1), lambda step=step: gather.from_chip(step)))
+            plan.append((0.1 + step * 0.66 / (place.chips - 1), lambda step=step: gather.from_columns(step - 1)))
+
+        def last_step():
+            gather.from_columns(place.chips - 1)
+            for step in range(place.chips):
+                gather.from_corner(step)
+            gather.finish()
+            for step in range(1, count):
+                for which in range(pairs):
+                    for kind in range(2):
+                        far_copy(step, which, kind).wait_send()
+
+        for moment, action in plan:
+            pl.when(now == int(moment * steps))(action)
+
+        @pl.when(turn == 0)
         def _():
+            for step in range(1, count):
+                for kind in range(2):
+                    far_copy(step, pair, kind).wait_recv()
             for half in range(2):
                 own, spare = own_lanes(half, rows)
                 zero = jnp.zeros((rows, 2 * HD), BF)
                 for i in range(count):
                     at = slice(i * rows, (i + 1) * rows)
-                    k_own[half, at, :] = jnp.where(own, k_refs[i][...], jnp.where(spare, bias_ref[at, :], zero))
-                    v_own[half, at, :] = jnp.where(own, v_refs[i][...], jnp.where(spare, zero + 1, zero))
+                    key = k_ref[...] if i == 0 else far[i - 1, 0, pair]
+                    value = v_ref[...] if i == 0 else far[i - 1, 1, pair]
+                    k_own[half, at, :] = jnp.where(own, key, jnp.where(spare, bias_ref[at, :], zero))
+                    v_own[half, at, :] = jnp.where(own, value, jnp.where(spare, zero + 1, zero))
 
         query = q_ref[...]
         results = []
@@ -281,46 +466,53 @@
             l_ref[half : half + 1, :] = jnp.transpose(log_total)[0:1, :]
         lane = lax.broadcasted_iota(jnp.int32, (block, 2 * HD), 1)
         o_ref[...] = jnp.where(lane < HD, results[0], results[1]).astype(BF)
-
-    def columns(first):
-        return [pl.BlockSpec((rows, 2 * HD), lambda i, j: (0, i + first)) for _ in range(count)]
-
-    first = part * pairs
-    arguments = [inputs, key_bias] + sources + sources
-    specs = [
-        pl.BlockSpec((block, 2 * HD), lambda i, j: (j, i)),
-        pl.BlockSpec((keys, 2 * HD), lambda i, j: (0, 0)),
-    ]
-    specs = specs + columns(pairs) + columns(2 * pairs)
-    aliases = {}
-    if context is not None:
-        aliases = {len(arguments): 0, len(arguments) + 1: 1}
-        arguments = arguments + [context, log_totals]
-        specs = specs + [pl.BlockSpec(memory_space=pl.ANY)] * 2
-    heads = 2 * pairs
+        pl.when(now == steps - 1)(last_step)
+
+    def column(first):
+        return pl.BlockSpec((rows, 2 * HD), lambda i, j: (0, i + first))
+
+    far_sems = pltpu.SemaphoreType.DMA((max(count - 1, 1), 2, pairs))
     return pl.pallas_call(
         kernel,
-        grid=(pairs, rows // block),
-        in_specs=specs,
+        grid=(pairs, blocks),
+        in_specs=[
+            pl.BlockSpec((block, 2 * HD), lambda i, j: (j, i)),
+            pl.BlockSpec((keys, 2 * HD), lambda i, j: (0, 0)),
+            column(pairs),
+            column(2 * pairs),
+            HBM,
+        ]
+        + [HBM] * late,
         out_specs=[
-            pl.BlockSpec((block, 2 * HD), lambda i, j: (j, i + first)),
-            pl.BlockSpec((None, 8, block), lambda i, j: (i + first, 0, j)),
-        ],
+            pl.BlockSpec((block, 2 * HD), lambda i, j: (j, i)),
+            pl.BlockSpec((None, 8, block), lambda i, j: (i, 0, j)),
+        ]
+        + [HBM] * late,
         out_shape=[
-            jax.ShapeDtypeStruct((rows, H * HD), BF),
-            jax.ShapeDtypeStruct((H // 2, 8, rows), F32),
-        ],
-        scratch_shapes=[pltpu.VMEM((2, keys, 2 * HD), BF), pltpu.VMEM((2, keys, 2 * HD), BF)],
-        input_output_aliases=aliases,
-        compiler_params=pltpu.CompilerParams(vmem_limit_bytes=40 << 20),
+            jax.ShapeDtypeStruct((rows, width), BF),
+            jax.ShapeDtypeStruct((pairs, 8, rows), F32),
+        ]
+        + [jax.ShapeDtypeStruct((devices,) + shard.shape, BF) for shard in shards],
+        scratch_shapes=[
+            pltpu.VMEM((2, keys, 2 * HD), BF),
+            pltpu.VMEM((2, keys, 2 * HD), BF),
+            pltpu.VMEM((max(count - 1, 1), 2, pairs, rows, 2 * HD), BF),
+            pltpu.SemaphoreType.DMA(()),
+        ]
+        + gather_semaphores(grid, late)
+        + [far_sems, far_sems]
+        + [pltpu.VMEM(shard.shape, BF) for shard in shards],
+        compiler_params=pltpu.CompilerParams(
+            collective_id=1, has_side_effects=True, vmem_limit_bytes=48 << 20
+        ),
         cost_estimate=pl.CostEstimate(
-            flops=16 * heads * rows * keys * HD, bytes_accessed=8 * rows * width, transcendentals=heads * rows * keys
+            flops=16 * H * rows * keys * HD, bytes_accessed=8 * rows * width, transcendentals=H * rows * keys
         ),
         name="attention",
-    )(*arguments)
-
-
-def attention_back(part, inputs, others, key_bias, log_totals, context, grad_context, block=256, chunk=1024):
+    )(inputs, key_bias, inputs, inputs, inputs, *shards)
+
+
+def attention_back(inputs, others, key_bias, log_totals, context, grad_context, block=256, chunk=1024):
     rows, width = inputs.shape
     pairs = width // (6 * HD)
     sources = [inputs] + list(others)
@@ -389,7 +581,7 @@
     def column(first):
         return pl.BlockSpec((rows, 2 * HD), lambda i: (0, i + first))
 
-    first = part * pairs
+    first = 0
     heads = 2 * pairs
     return pl.pallas_call(
         kernel,
@@ -450,8 +642,6 @@
     tall = hidden // devices
     wide = hidden // width
 
-    flat_in = to_sequences(grid, tokens)
-
     vectors = (
         query_bias,
         value_bias,
@@ -464,23 +654,12 @@
     )
     vector_row = jnp.concatenate(vectors + (up_bias,))
     vector_size = vector_row.shape[0]
-    vector_rows = jnp.zeros((8, width), BF).at[0, :vector_size].set(vector_row)
-    early = jnp.concatenate([query_weight, key_weight, value_weight, vector_rows], axis=0)
-    ups = [up_weight[:, i * width : (i + 1) * width] for i in range(wide)]
-    late = jnp.concatenate([out_weight] + ups, axis=0)
-    strip = width // PARTS
-    cuts = [
-        (slim, tuple((i * slim, part * strip, i * strip, strip) for i in range(3))) for part in range(PARTS)
-    ]
-    cuts.append((8, ((3 * slim, 0, 0, width),)))
-    *into_full, vector_full = assemble(grid, *gather_packed(grid, early), cuts)
-    cuts = [
-        (slim, ((0, 0, 0, width),)),
-        (slim, tuple((slim * (1 + i), 0, i * width, width) for i in range(wide))),
-    ]
-    out_full, up_full = assemble(grid, *gather_packed(grid, late), cuts)
-    (down_full,) = assemble(grid, *gather_packed(grid, down_weight), [(tall, ((0, 0, 0, width),))])
-    vector_table = vector_full.reshape(devices, 8, width)[:, 0, :vector_size]
+    vector_rows = jnp.zeros((8, -(-vector_size // 128) * 128), BF).at[0, :vector_size].set(vector_row)
+    into_shard = jnp.stack([query_weight, key_weight, value_weight])
+    flat_in, into_full, vector_full = start_exchange(grid, tokens, into_shard, vector_rows)
+    flat_in = flat_in.reshape(-1, width)
+    into_full = into_full.reshape(3, width, width)
+    vector_table = vector_full[:, 0, :vector_size]
     small = vector_table[:, : 8 * slim].reshape(devices, 8, slim).transpose(1, 0, 2)
     small = small.reshape(8, width).astype(F32)
     query_add, value_add, out_add, down_add, gain_one, shift_one, gain_two, shift_two = (
@@ -499,16 +678,16 @@
     ).astype(F32)
 
     key_bias = jnp.broadcast_to(key_bias[:, None], (key_bias.shape[0], 2 * HD)).astype(BF)
-    inputs, others = [], []
-    for part in range(PARTS):
-        at = slice(part * strip, (part + 1) * strip)
-        add = jnp.concatenate([query_add[at], jnp.zeros((strip,), F32), value_add[at]])
-        own = (matmul(flat_in, into_full[part]) + add).astype(BF)
-        inputs.append(own)
-        others.append([grid.to_member(own, step) for step in range(1, grid.group)])
-    context, log_totals = None, None
-    for part in range(PARTS):
-        context, log_totals = attention(part, inputs[part], others[part], key_bias, context, log_totals)
+    adds = (query_add, jnp.zeros_like(query_add), value_add)
+    inputs = [(matmul(flat_in, into_full[i]) + adds[i]).astype(BF) for i in range(3)]
+    inputs = jnp.concatenate(inputs, axis=1)
+    context, log_totals, out_full, up_full, down_full = attention(
+        grid, inputs, key_bias, (out_weight, up_weight, down_weight)
+    )
+    out_full = out_full.reshape(width, width)
+    up_full = up_full.reshape(width, hidden)
+    down_full = down_full.reshape(hidden, width)
+    others = [grid.to_member(inputs, step) for step in range(1, grid.group)]
     grad_in = to_sequences(grid, cotangent)
 
     first_sum = flat_in.astype(F32) + matmul(context, out_full) + out_add
@@ -543,20 +722,17 @@
     grad_up_own = scatter_sum(grid, grad_up)
     grad_out_own = scatter_sum(grid, grad_out)
 
+    own, *away = attention_back(inputs, others, key_bias, log_totals, context, grad_context)
+    grad_kv = own[:, width:].astype(F32)
+    for step, piece in enumerate(away, 1):
+        grad_kv = grad_kv + grid.to_member(piece, step, back=True).astype(F32)
+    low = jnp.concatenate([own[:, :width], grad_kv.astype(BF)], axis=1)
+    query_adds = jnp.sum(low[:, :width].astype(F32), axis=0)
+    value_adds = jnp.sum(low[:, 2 * width :].astype(F32), axis=0)
     tokens_grad = grad_residual
-    grad_into_own, query_adds, value_adds = [], [], []
-    for part in range(PARTS):
-        own, *away = attention_back(
-            part, inputs[part], others[part], key_bias, log_totals, context, grad_context
-        )
-        grad_kv = own[:, strip:].astype(F32)
-        for step, piece in enumerate(away, 1):
-            grad_kv = grad_kv + grid.to_member(piece, step, back=True).astype(F32)
-        low = jnp.concatenate([own[:, :strip], grad_kv.astype(BF)], axis=1)
-        query_adds.append(jnp.sum(low[:, :strip].astype(F32), axis=0))
-        value_adds.append(jnp.sum(low[:, 2 * strip :].astype(F32), axis=0))
-        tokens_grad = tokens_grad + right_product(low, into_full[part])
-        grad_into_own.append(scatter_sum(grid, left_product(flat_in, low).astype(BF)))
+    for i in range(3):
+        tokens_grad = tokens_grad + right_product(low[:, i * width : (i + 1) * width], into_full[i])
+    grad_into_own = scatter_sum(grid, left_product(flat_in, low).astype(BF))
     tokens_grad = from_sequences(grid, tokens_grad.astype(BF), length).astype(F32)
 
     def pack(grads):
@@ -567,15 +743,12 @@
     middle = pack([grad_out_add, grad_down_add, grad_gain_one, grad_shift_one, grad_gain_two, grad_shift_two])
     middle = jnp.concatenate([middle, grad_up_add.reshape(devices, tall)], axis=1).astype(BF)
     middle_own = scatter_sum(grid, middle)[0]
-    last = pack([jnp.concatenate(query_adds), jnp.concatenate(value_adds)]).astype(BF)
+    last = pack([query_adds, value_adds]).astype(BF)
     last_own = scatter_sum(grid, last)[0]
     vector_outs = [last_own[:slim], last_own[slim:]]
     vector_outs = vector_outs + [middle_own[i * slim : (i + 1) * slim] for i in range(6)]
     up_add_own = middle_own[6 * slim :]
-    matrix_outs = [
-        jnp.concatenate([own[:, i * strip : (i + 1) * strip] for own in grad_into_own], axis=1)
-        for i in range(3)
-    ]
+    matrix_outs = [grad_into_own[:, i * width : (i + 1) * width] for i in range(3)]
     return (
         output,
         tokens_grad,

time: 715 us -> 575 us (0.80)
  starting transfers between devices: 131 us -> 64.8 us
  Pallas kernels: 160 us -> 224 us
  waiting for transfers between devices: 163 us -> 105 us
  local copies, waits for them, and re-layouts: 85.9 us -> 33.5 us
  matrix products: 123 us -> 104 us
    pallas_call x6 -> x2, Pallas kernels: 83.3 us -> 147 us  [the longest x1 75.1 us: attention(): pl.pallas_call(kernel, grid=(pairs, blocks), in_specs=[pl.BlockSpec((bloc...]
    ppermute x33 -> x18, waiting for transfers between devices: 95.4 us -> 44.5 us  [to_column(): return lax.ppermute(array_in, 'dp', pairs)]
    ppermute x33 -> x18, starting transfers between devices: 62 us -> 28.3 us  [to_chip(): return lax.ppermute(array_in, 'seq', pairs)]
    ppermute x33 -> x18, starting transfers between devices: 45.3 us -> 20.8 us  [to_column(): return lax.ppermute(array_in, 'dp', pairs)]
    unnamed x174 -> x141, local copies, waits for them, and re-layouts: 27.8 us -> 3.82 us
    dot_general x6, matrix products: 70.2 us -> 49.4 us  [matmul(): return jnp.dot(left, right, preferred_element_type=F32)]
    ppermute x12 -> x9, waiting for transfers between devices: 43.5 us -> 27.9 us  [to_owner(): return lax.ppermute(array_in, 'seq', pairs)]
    dynamic_slice x10 -> x1, local copies, waits for them, and re-layouts: 10.6 us -> 0.59 us  [take_block(): return lax.dynamic_index_in_dim(array_in, index, 0, keepdims=False)]
  transfers between devices with their start and end apart: 95 -> 53, of which waited for: 33 -> 21; matrix products, arithmetic and copies ran while one was open for 26% -> 27% of each run, Pallas kernels for 23% -> 39%
where the time goes in v3:
time: 575 us; the launch traced here: 570 us
  Pallas kernels  224 us (39%)
  waiting for transfers between devices  105 us (18%)
  matrix products  104 us (18%)
  starting transfers between devices  64.8 us (11%)
  other arithmetic  36.4 us (6%)
  local copies, waits for them, and re-layouts  33.5 us (6%)
    pallas_call x1, Pallas kernels, attention_back(): pl.pallas_call(kernel, grid=(pairs,), in_specs=[column(0), pl.BlockSpec((...  76.9 us
    pallas_call x1, Pallas kernels, attention(): pl.pallas_call(kernel, grid=(pairs, blocks), in_specs=[pl.BlockSpec((bloc...  75.1 us
    pallas_call x1, Pallas kernels, start_exchange(): pl.pallas_call(kernel, in_specs=[HBM] * 3, out_specs=[HBM] * 3, out_shape...  72.1 us
    dot_general x6, matrix products, matmul(): return jnp.dot(left, right, preferred_element_type=F32)  49.4 us
    ppermute x18, waiting for transfers between devices, to_column(): return lax.ppermute(array_in, 'dp', pairs)  44.5 us
    dot_general x6, matrix products, right_product(): lax.dot_general(left, right, (((1,), (1,)), ((), ())), preferred_element_...  32.4 us
    ppermute x18, waiting for transfers between devices, to_chip(): return lax.ppermute(array_in, 'seq', pairs)  32.2 us
    ppermute x18, starting transfers between devices, to_chip(): return lax.ppermute(array_in, 'seq', pairs)  28.3 us
  transfers between devices with their start and end apart: 53, of which 21 were waited for; matrix products, arithmetic and copies ran while one was open for 27% of the time, Pallas kernels for 39%

profile of v3, /device:TPU:0, one launch (start us, length us, event | category | flops | bytes accessed | tf_op | source)
XLA Modules:
  0.0 569.7 jit_solution(17372963209054695623)
XLA Ops:
  11.7 72.1 %start_exchange.1 = (bf16[4,256,768]{2,1,0:T(8,128)(2,1)}, bf16[3,32,24,768]{3,2,1,0:T(8,128)(2,1)}, bf16[32,8,384]{2,1,0:T(8,128)(2,1)}) custom-call(bf16[4,256,768]{2,1,0:T(8,128)(2,1)} %tokens_ref.1, bf16[3,24,768]{2,1,0:T(8,128)(2,1)} %pad_maximum_fusion.1.into_ref, bf16[8,384]{1,0:T(8,128)(2,1)} %scatter.4.vectors_ref), custom_call_target="tpu_custom_call" | custom-call | tf_op jit(solution)/shard_map/start_exchange/pallas_call | solution.py:322
  103.6 75.1 %attention.1 = (bf16[1024,768]{1,0:T(8,128)(2,1)S(1)}, f32[6,8,1024]{2,1,0:T(8,128)S(1)}, bf16[32,24,768]{2,1,0:T(8,128)(2,1)S(1)}, bf16[32,24,3072]{2,1,0:T(8,128)(2,1)}, bf16[32,96,768]{2,1,0:T(8,128)(2,1)}) custom-call(bf16[1024,2304]{1,0:T(8,128)(2,1)} %pad_maximum_fusion.q_ref.k_ref.v_ref.all_ref.refs_0_.refs_2_, ...), custom_call_target="tpu_custom_call" | custom-call | flops 25769803776 | bytes 6291456 | tf_op jit(solution)/shard_map/attention/pallas_call | solution.py:475
  183.1 35.1 %fusion.2 = (bf16[1024,3072]{1,0:T(8,128)(2,1)S(1)}, f32[1024,3072]{1,0:T(8,128)}) fusion(f32[3072]{0:T(1024)S(1)} %reshape.466, bf16[768,3072]{1,0:T(8,128)(2,1)S(1)} %bitcast.322, f32[1024,768]{1,0:T(8,128)S(1)} %get-tuple-element.139, f32[768]{0:T(1024)S(1)} %add.488, f32[768]{0:T(1024)S(1)} %mul.205, f32[1024]{0:T(1024)S(1)} %add_rsqrt_fusion.1, ...), kind=kOutput, calls=%fused_computation.4 | convolution fusion | flops 5043388416 | bytes 26765312 | tf_op jit(solution)/shard_map/dot_general | solution.py:19
  218.3 7.0 %fusion.90 = (f32[1024]{0:T(1024)S(1)}, f32[1024,768]{1,0:T(8,128)}) fusion(f32[768]{0:T(1024)S(1)} %add.494, bf16[1024,3072]{1,0:T(8,128)(2,1)S(1)} %get-tuple-element.140, bf16[3072,768]{1,0:T(8,128)(2,1)S(1)} %bitcast.328, f32[768]{0:T(1024)S(1)} %add.488, f32[768]{0:T(1024)S(1)} %mul.205, f32[1024]{0:T(1024)S(1)} %add_rsqrt_fusion.1, ...), kind=kOutput, calls=%fused_computation.268 | convolution fusion | flops 4838915072 | bytes 17323008 | tf_op jit(solution)/shard_map/dot_general | solution.py:19
  233.4 4.0 multiply_reduce_fusion
  242.4 12.1 %fusion.91 = (bf16[3072]{0:T(1024)(128)(2,1)S(1)}, bf16[1024,3072]{1,0:T(8,128)(2,1)S(1)}) fusion(f32[1024,3072]{1,0:T(8,128)} %get-tuple-element.141, f32[3072]{0:T(1024)S(1)} %reshape.466, bf16[3072,768]{1,0:T(8,128)(2,1)S(1)} %bitcast.331, f32[1024,768]{1,0:T(8,128)S(1)} %get-tuple-element.66), kind=kOutput, calls=%fused_computation.269 | convolution fusion | flops 4870370304 | bytes 26757120 | tf_op jit(solution)/shard_map/dot_general | solution.py:27
  254.5 6.1 %multiply_reduce_fusion.1 = (bf16[768]{0:T(1024)(128)(2,1)S(1)}, f32[1024]{0:T(1024)S(1)}, f32[1024]{0:T(1024)S(1)}, bf16[768]{0:T(1024)(128)(2,1)S(1)}, f32[1024,768]{1,0:T(8,128)S(1)}) fusion(f32[1024,768]{1,0:T(8,128)S(1)} %copy-done.10, f32[1024]{0:T(1024)S(1)} %add_rsqrt_fusion.1, f32[1024]{0:T(1024)S(1)} %broadcast_multiply_fusion.4, ...), kind=kOutput, calls=%fused_computation.41 | convolution fusion | flops 4839698432 | bytes 20469760 | tf_op jit(solution)/shard_map/dot_general | solution.py:27
  266.7 8.0 %convolution_convert_fusion.1 = bf16[768,3072]{1,0:T(8,128)(2,1)} fusion(bf16[1024,3072]{1,0:T(8,128)(2,1)S(1)} %get-tuple-element.146, f32[1024,768]{1,0:T(8,128)S(1)} %copy-done.10, f32[768]{0:T(1024)S(1)} %add.488, f32[768]{0:T(1024)S(1)} %mul.205, f32[1024]{0:T(1024)S(1)} %add_rsqrt_fusion.1, f32[1024]{0:T(1024)S(1)} %broadcast_multiply_fusion.4), kind=kOutput, calls=%fused_computation.27 | convolution fusion | flops 4838129664 | bytes 14170112 | tf_op jit(solution)/shard_map/dot_general | solution.py:23
  274.7 7.3 %convolution_convert_fusion = bf16[3072,768]{1,0:T(8,128)(2,1)} fusion(bf16[1024,3072]{1,0:T(8,128)(2,1)S(1)} %bitcast.333, f32[1024,768]{1,0:T(8,128)S(1)} %get-tuple-element.66), kind=kOutput, calls=%fused_computation.26 | convolution fusion | flops 4834983936 | bytes 14155776 | tf_op jit(solution)/shard_map/dot_general | solution.py:23
  304.5 4.5 collective-permute-done
  312.7 23.3 %collective-permute-done.1 = bf16[256,768]{1,0:T(8,128)(2,1)S(1)} collective-permute-done((bf16[256,768]{1,0:T(8,128)(2,1)S(1)}, bf16[256,768]{1,0:T(8,128)(2,1)S(1)}, u32[]{:S(2)}, u32[]{:S(2)}) %collective-permute-start.1) | collective-permute-done | bytes 393248 | tf_op jit(solution)/shard_map/ppermute | solution.py:95
  338.4 3.8 collective-permute-done.21
  360.9 76.9 %attention_back.1 = (bf16[1024,2304]{1,0:T(8,128)(2,1)}, bf16[1024,1536]{1,0:T(8,128)(2,1)}) custom-call(bf16[1024,2304]{1,0:T(8,128)(2,1)} %pad_maximum_fusion.q_ref.k_ref.v_ref.all_ref.refs_0_.refs_2_, bf16[2048,128]{1,0:T(8,128)(2,1)S(1)} %copy-done.1, f32[6,8,1024]{2,1,0:T(8,128)S(1)} %get-tuple-element.46.l_ref, bf16[1024,768]{1,0:T(8,128)(2,1)S(1)} %copy-done.7, ...), custom_call_target="tpu_custom_call" | custom-call | flops 64424509440 | bytes 28311552 | tf_op jit(solution)/shard_map/attention_back/pallas_call | solution.py:586
  444.2 10.8 %collective-permute-done.28 = bf16[96,3072]{1,0:T(8,128)(2,1)S(1)} collective-permute-done((bf16[96,3072]{1,0:T(8,128)(2,1)S(1)}, bf16[96,3072]{1,0:T(8,128)(2,1)S(1)}, u32[]{:S(2)}, u32[]{:S(2)}) %collective-permute-start.28) | collective-permute-done | bytes 589856 | tf_op jit(solution)/shard_map/ppermute | solution.py:84
  457.3 6.6 %collective-permute-done.27 = bf16[96,3072]{1,0:T(8,128)(2,1)S(1)} collective-permute-done((bf16[96,3072]{1,0:T(8,128)(2,1)S(1)}, bf16[96,3072]{1,0:T(8,128)(2,1)S(1)}, u32[]{:S(2)}, u32[]{:S(2)}) %collective-permute-start.27) | collective-permute-done | bytes 589856 | tf_op jit(solution)/shard_map/ppermute | solution.py:84
  471.2 4.4 collective-permute-done.31
  475.6 5.1 collective-permute-done.30
  483.5 4.7 fusion.85
  494.3 4.1 convolution_convert_fusion.2
  502.4 5.1 add_convert_fusion.1
  516.4 14.2 %collective-permute-done.45 = bf16[1,48]{1,0:T(2,128)(2,1)S(1)} collective-permute-done((bf16[1,48]{1,0:T(2,128)(2,1)S(1)}, bf16[1,48]{1,0:T(2,128)(2,1)S(1)}, u32[]{:S(2)}, u32[]{:S(2)}) %collective-permute-start.45) | collective-permute-done | bytes 128 | tf_op jit(solution)/shard_map/ppermute | solution.py:80
  540.5 10.4 %collective-permute-done.14 = bf16[96,2304]{1,0:T(8,128)(2,1)S(1)} collective-permute-done((bf16[96,2304]{1,0:T(8,128)(2,1)S(1)}, bf16[96,2304]{1,0:T(8,128)(2,1)S(1)}, u32[]{:S(2)}, u32[]{:S(2)}) %collective-permute-start.14) | collective-permute-done | bytes 442400 | tf_op jit(solution)/shard_map/ppermute | solution.py:84
  550.8 5.8 %collective-permute-done.13 = bf16[96,2304]{1,0:T(8,128)(2,1)S(1)} collective-permute-done((bf16[96,2304]{1,0:T(8,128)(2,1)S(1)}, bf16[96,2304]{1,0:T(8,128)(2,1)S(1)}, u32[]{:S(2)}, u32[]{:S(2)}) %collective-permute-start.13) | collective-permute-done | bytes 442400 | tf_op jit(solution)/shard_map/ppermute | solution.py:84
  564.8 3.7 collective-permute-done.16
  (366 shorter events, 156.9 us)
Async XLA Ops:
  4.6 223.5 %collective-permute-start.3 = (bf16[256,768]{1,0:T(8,128)(2,1)}, bf16[256,768]{1,0:T(8,128)(2,1)}, u32[]{:S(2)}, u32[]{:S(2)}) collective-permute-start(bf16[256,768]{1,0:T(8,128)(2,1)} %get-tuple-element.89), channel_id=1, source_target_pairs={{0,2},{1,3},{2,0},{3,1},{4,6},{5,7},{6,4},{7,5},{8,10},{9,11},{10,... | collective-permute-start | bytes 1179656 | tf_op jit(solution)/shard_map/ppermute | solution.py:95
  7.6 222.2 %collective-permute-start.4 = (bf16[256,768]{1,0:T(8,128)(2,1)}, bf16[256,768]{1,0:T(8,128)(2,1)}, u32[]{:S(2)}, u32[]{:S(2)}) collective-permute-start(bf16[256,768]{1,0:T(8,128)(2,1)} %get-tuple-element.91), channel_id=1, source_target_pairs={{0,4},{1,5},{2,6},{3,7},{4,0},{5,1},{6,2},{7,3},{8,12},{9,13},{10,... | collective-permute-start | bytes 1179656 | tf_op jit(solution)/shard_map/ppermute | solution.py:95
  10.2 221.4 %collective-permute-start.5 = (bf16[256,768]{1,0:T(8,128)(2,1)}, bf16[256,768]{1,0:T(8,128)(2,1)}, u32[]{:S(2)}, u32[]{:S(2)}) collective-permute-start(bf16[256,768]{1,0:T(8,128)(2,1)} %get-tuple-element.88), channel_id=1, source_target_pairs={{0,6},{1,7},{2,4},{3,5},{4,2},{5,3},{6,0},{7,1},{8,14},{9,15},{10,... | collective-permute-start | bytes 1179656 | tf_op jit(solution)/shard_map/ppermute | solution.py:95
  100.1 259.6 %collective-permute-start.6 = (bf16[1024,2304]{1,0:T(8,128)(2,1)}, bf16[1024,2304]{1,0:T(8,128)(2,1)}, u32[]{:S(2)}, u32[]{:S(2)}) collective-permute-start(bf16[1024,2304]{1,0:T(8,128)(2,1)} %pad_maximum_fusion.q_ref.k_ref.v_ref.all_ref.refs_0_.refs_2_), channel_id=1, source_target_pairs={{0,1},{1,0},{2,3},{3,2},{4,5},{5,4},{6,7},{7,6},{8,9},{9,8},{10,11... | collective-permute-start | bytes 14155784 | tf_op jit(solution)/shard_map/ppermute | solution.py:103
  288.6 64.4 %collective-permute-start.32 = (bf16[16,96,768]{2,1,0:T(8,128)(2,1)}, bf16[16,96,768]{2,1,0:T(8,128)(2,1)}, u32[]{:S(2)}, u32[]{:S(2)}) collective-permute-start(bf16[16,96,768]{2,1,0:T(8,128)(2,1)} %dynamic-slice_bitcast_fusion), channel_id=1, source_target_pairs={{0,1},{1,0},{2,3},{3,2},{4,5},{5,4},{6,7},{7,6},{8,9},{9,8},{10,11... | collective-permute-start | bytes 7077896 | tf_op jit(solution)/shard_map/ppermute | solution.py:87
  302.8 53.2 %collective-permute-start.25 = (bf16[16,24,3072]{2,1,0:T(8,128)(2,1)S(1)}, bf16[16,24,3072]{2,1,0:T(8,128)(2,1)S(1)}, u32[]{:S(2)}, u32[]{:S(2)}) collective-permute-start(bf16[16,24,3072]{2,1,0:T(8,128)(2,1)S(1)} %copy-done.19), channel_id=1, source_target_pairs={{0,1},{1,0},{2,3},{3,2},{4,5},{5,4},{6,7},{7,6},{8,9},{9,8},{10,11... | collective-permute-start | bytes 7077896 | tf_op jit(solution)/shard_map/ppermute | solution.py:87
  309.1 27.0 %collective-permute-start.1 = (bf16[256,768]{1,0:T(8,128)(2,1)S(1)}, bf16[256,768]{1,0:T(8,128)(2,1)S(1)}, u32[]{:S(2)}, u32[]{:S(2)}) collective-permute-start(bf16[256,768]{1,0:T(8,128)(2,1)S(1)} %get-tuple-element.93), channel_id=1, source_target_pairs={{0,4},{1,5},{2,6},{3,7},{4,0},{5,1},{6,2},{7,3},{8,12},{9,13},{10,... | collective-permute-start | bytes 1179656 | tf_op jit(solution)/shard_map/ppermute | solution.py:95
  311.8 25.5 %collective-permute-start.2 = (bf16[256,768]{1,0:T(8,128)(2,1)S(1)}, bf16[256,768]{1,0:T(8,128)(2,1)S(1)}, u32[]{:S(2)}, u32[]{:S(2)}) collective-permute-start(bf16[256,768]{1,0:T(8,128)(2,1)S(1)} %get-tuple-element.92), channel_id=1, source_target_pairs={{0,6},{1,7},{2,4},{3,5},{4,2},{5,3},{6,0},{7,1},{8,14},{9,15},{10,... | collective-permute-start | bytes 1179656 | tf_op jit(solution)/shard_map/ppermute | solution.py:95
  350.1 87.7 %collective-permute-start.23 = (bf16[24,768]{1,0:T(8,128)(2,1)S(1)}, bf16[24,768]{1,0:T(8,128)(2,1)S(1)}, u32[]{:S(2)}, u32[]{:S(2)}) collective-permute-start(bf16[24,768]{1,0:T(8,128)(2,1)S(1)} %get-tuple-element.113), channel_id=1, source_target_pairs={{0,4},{1,5},{2,6},{3,7},{4,0},{5,1},{6,2},{7,3},{8,12},{9,13},{10,... | collective-permute-start | bytes 110600 | tf_op jit(solution)/shard_map/ppermute | solution.py:80
  353.0 85.8 %collective-permute-start.22 = (bf16[24,768]{1,0:T(8,128)(2,1)S(1)}, bf16[24,768]{1,0:T(8,128)(2,1)S(1)}, u32[]{:S(2)}, u32[]{:S(2)}) collective-permute-start(bf16[24,768]{1,0:T(8,128)(2,1)S(1)} %get-tuple-element.111), channel_id=1, source_target_pairs={{0,2},{1,3},{2,0},{3,1},{4,6},{5,7},{6,4},{7,5},{8,10},{9,11},{10,... | collective-permute-start | bytes 110600 | tf_op jit(solution)/shard_map/ppermute | solution.py:80
  357.3 82.8 %collective-permute-start.35 = (bf16[384,768]{1,0:T(8,128)(2,1)S(1)}, bf16[384,768]{1,0:T(8,128)(2,1)S(1)}, u32[]{:S(2)}, u32[]{:S(2)}) collective-permute-start(bf16[384,768]{1,0:T(8,128)(2,1)S(1)} %get-tuple-element.76), channel_id=1, source_target_pairs={{0,24},{8,16},{16,8},{24,0},{1,25},{9,17},{17,9},{25,1},{2,26},{10... | collective-permute-start | bytes 1769480 | tf_op jit(solution)/shard_map/ppermute | solution.py:84
  358.4 82.9 %collective-permute-start.34 = (bf16[384,768]{1,0:T(8,128)(2,1)S(1)}, bf16[384,768]{1,0:T(8,128)(2,1)S(1)}, u32[]{:S(2)}, u32[]{:S(2)}) collective-permute-start(bf16[384,768]{1,0:T(8,128)(2,1)S(1)} %get-tuple-element.77), channel_id=1, source_target_pairs={{0,16},{8,24},{16,0},{24,8},{1,17},{9,25},{17,1},{25,9},{2,18},{10... | collective-permute-start | bytes 1769480 | tf_op jit(solution)/shard_map/ppermute | solution.py:84
  359.7 82.3 %collective-permute-start.33 = (bf16[384,768]{1,0:T(8,128)(2,1)S(1)}, bf16[384,768]{1,0:T(8,128)(2,1)S(1)}, u32[]{:S(2)}, u32[]{:S(2)}) collective-permute-start(bf16[384,768]{1,0:T(8,128)(2,1)S(1)} %get-tuple-element.75), channel_id=1, source_target_pairs={{0,8},{8,0},{16,24},{24,16},{1,9},{9,1},{17,25},{25,17},{2,10},{10... | collective-permute-start | bytes 1769480 | tf_op jit(solution)/shard_map/ppermute | solution.py:84
  437.8 17.2 %collective-permute-start.28 = (bf16[96,3072]{1,0:T(8,128)(2,1)S(1)}, bf16[96,3072]{1,0:T(8,128)(2,1)S(1)}, u32[]{:S(2)}, u32[]{:S(2)}) collective-permute-start(bf16[96,3072]{1,0:T(8,128)(2,1)S(1)} %get-tuple-element.79), channel_id=1, source_target_pairs={{0,24},{8,16},{16,8},{24,0},{1,25},{9,17},{17,9},{25,1},{2,26},{10... | collective-permute-start | bytes 1769480 | tf_op jit(solution)/shard_map/ppermute | solution.py:84
  438.8 25.1 %collective-permute-start.27 = (bf16[96,3072]{1,0:T(8,128)(2,1)S(1)}, bf16[96,3072]{1,0:T(8,128)(2,1)S(1)}, u32[]{:S(2)}, u32[]{:S(2)}) collective-permute-start(bf16[96,3072]{1,0:T(8,128)(2,1)S(1)} %get-tuple-element.80), channel_id=1, source_target_pairs={{0,16},{8,24},{16,0},{24,8},{1,17},{9,25},{17,1},{25,9},{2,18},{10... | collective-permute-start | bytes 1769480 | tf_op jit(solution)/shard_map/ppermute | solution.py:84
  440.2 25.4 %collective-permute-start.26 = (bf16[96,3072]{1,0:T(8,128)(2,1)S(1)}, bf16[96,3072]{1,0:T(8,128)(2,1)S(1)}, u32[]{:S(2)}, u32[]{:S(2)}) collective-permute-start(bf16[96,3072]{1,0:T(8,128)(2,1)S(1)} %get-tuple-element.78), channel_id=1, source_target_pairs={{0,8},{8,0},{16,24},{24,16},{1,9},{9,1},{17,25},{25,17},{2,10},{10... | collective-permute-start | bytes 1769480 | tf_op jit(solution)/shard_map/ppermute | solution.py:84
  441.3 46.8 %collective-permute-start.7 = (bf16[1024,1536]{1,0:T(8,128)(2,1)}, bf16[1024,1536]{1,0:T(8,128)(2,1)}, u32[]{:S(2)}, u32[]{:S(2)}) collective-permute-start(bf16[1024,1536]{1,0:T(8,128)(2,1)} %get-tuple-element.48), channel_id=1, source_target_pairs={{0,1},{1,0},{2,3},{3,2},{4,5},{5,4},{6,7},{7,6},{8,9},{9,8},{10,11... | collective-permute-start | bytes 9437192 | tf_op jit(solution)/shard_map/ppermute | solution.py:103
  442.4 25.7 %collective-permute-start.38 = (bf16[96,768]{1,0:T(8,128)(2,1)S(1)}, bf16[96,768]{1,0:T(8,128)(2,1)S(1)}, u32[]{:S(2)}, u32[]{:S(2)}) collective-permute-start(bf16[96,768]{1,0:T(8,128)(2,1)S(1)} %get-tuple-element.97), channel_id=1, source_target_pairs={{0,6},{1,7},{2,4},{3,5},{4,2},{5,3},{6,0},{7,1},{8,14},{9,15},{10,... | collective-permute-start | bytes 442376 | tf_op jit(solution)/shard_map/ppermute | solution.py:80
  501.6 33.2 %collective-permute-start.11 = (bf16[16,24,2304]{2,1,0:T(8,128)(2,1)}, bf16[16,24,2304]{2,1,0:T(8,128)(2,1)}, u32[]{:S(2)}, u32[]{:S(2)}) collective-permute-start(bf16[16,24,2304]{2,1,0:T(8,128)(2,1)} %dynamic-slice_bitcast_fusion.2), channel_id=1, source_target_pairs={{0,1},{1,0},{2,3},{3,2},{4,5},{5,4},{6,7},{7,6},{8,9},{9,8},{10,11... | collective-permute-start | bytes 5308424 | tf_op jit(solution)/shard_map/ppermute | solution.py:87
  511.4 28.0 %collective-permute-start.8 = (bf16[256,768]{1,0:T(8,128)(2,1)S(1)}, bf16[256,768]{1,0:T(8,128)(2,1)S(1)}, u32[]{:S(2)}, u32[]{:S(2)}) collective-permute-start(bf16[256,768]{1,0:T(8,128)(2,1)S(1)} %get-tuple-element.86), channel_id=1, source_target_pairs={{0,2},{1,3},{2,0},{3,1},{4,6},{5,7},{6,4},{7,5},{8,10},{9,11},{10,... | collective-permute-start | bytes 1179656 | tf_op jit(solution)/shard_map/ppermute | solution.py:95
  512.1 28.3 %collective-permute-start.9 = (bf16[256,768]{1,0:T(8,128)(2,1)S(1)}, bf16[256,768]{1,0:T(8,128)(2,1)S(1)}, u32[]{:S(2)}, u32[]{:S(2)}) collective-permute-start(bf16[256,768]{1,0:T(8,128)(2,1)S(1)} %get-tuple-element.85), channel_id=1, source_target_pairs={{0,4},{1,5},{2,6},{3,7},{4,0},{5,1},{6,2},{7,3},{8,12},{9,13},{10,... | collective-permute-start | bytes 1179656 | tf_op jit(solution)/shard_map/ppermute | solution.py:95
  532.0 29.4 %collective-permute-start.10 = (bf16[256,768]{1,0:T(8,128)(2,1)S(1)}, bf16[256,768]{1,0:T(8,128)(2,1)S(1)}, u32[]{:S(2)}, u32[]{:S(2)}) collective-permute-start(bf16[256,768]{1,0:T(8,128)(2,1)S(1)} %get-tuple-element.84), channel_id=1, source_target_pairs={{0,6},{1,7},{2,4},{3,5},{4,2},{5,3},{6,0},{7,1},{8,14},{9,15},{10,... | collective-permute-start | bytes 1179656 | tf_op jit(solution)/shard_map/ppermute | solution.py:95
  538.5 18.2 %collective-permute-start.13 = (bf16[96,2304]{1,0:T(8,128)(2,1)S(1)}, bf16[96,2304]{1,0:T(8,128)(2,1)S(1)}, u32[]{:S(2)}, u32[]{:S(2)}) collective-permute-start(bf16[96,2304]{1,0:T(8,128)(2,1)S(1)} %get-tuple-element.83), channel_id=1, source_target_pairs={{0,16},{8,24},{16,0},{24,8},{1,17},{9,25},{17,1},{25,9},{2,18},{10... | collective-permute-start | bytes 1327112 | tf_op jit(solution)/shard_map/ppermute | solution.py:84
  539.4 17.3 %collective-permute-start.12 = (bf16[96,2304]{1,0:T(8,128)(2,1)S(1)}, bf16[96,2304]{1,0:T(8,128)(2,1)S(1)}, u32[]{:S(2)}, u32[]{:S(2)}) collective-permute-start(bf16[96,2304]{1,0:T(8,128)(2,1)S(1)} %get-tuple-element.81), channel_id=1, source_target_pairs={{0,8},{8,0},{16,24},{24,16},{1,9},{9,1},{17,25},{25,17},{2,10},{10... | collective-permute-start | bytes 1327112 | tf_op jit(solution)/shard_map/ppermute | solution.py:84
  (94 other events, 987.4 us)

commit v4 on v3

--- a/solution.py
+++ b/solution.py
@@ -337,23 +337,242 @@
     )(tokens, into, vectors)
 
 
-def scatter_sum(grid, array_in):
-    width = array_in.shape[1]
-    blocks = array_in.reshape(grid.columns * grid.chips, 2, -1, width)
-    keep = lax.dynamic_index_in_dim(blocks, grid.core, 1, keepdims=False)
-    send = lax.dynamic_index_in_dim(blocks, 1 - grid.core, 1, keepdims=False)
-    half = (keep.astype(F32) + grid.to_core(send).astype(F32)).astype(BF)
-    half = half.reshape(grid.columns, -1, width)
-    total = take_block(half, grid.column).astype(F32)
-    for step in range(1, grid.columns):
-        target = swap_index(grid.column, step, grid.columns)
-        total = total + grid.to_column(take_block(half, target), step).astype(F32)
-    part = total.astype(BF).reshape(grid.chips, -1, width)
-    total = take_block(part, grid.chip).astype(F32)
-    for step in range(1, grid.chips):
-        target = swap_index(grid.chip, step, grid.chips)
-        total = total + grid.to_chip(take_block(part, target), step).astype(F32)
-    return total
+class Reduce:
+    def __init__(self, place, arrays, buffers, semaphores):
+        self.place, self.arrays = place, arrays
+        self.halves, self.twins, self.sides, self.deeps = buffers
+        self.load, self.twin_sems, self.side_sems, self.deep_sems = semaphores
+        self.square = place.columns == 4
+        self.every = range(len(arrays))
+        self.sent = []
+
+    def spot(self, column_step, chip_step):
+        return (self.place.column ^ column_step) * self.place.chips + (self.place.chip ^ chip_step)
+
+    def strip(self, column_step):
+        return pl.ds((self.place.column ^ column_step) * self.place.chips, self.place.chips)
+
+    def load_copy(self, k, step):
+        whole = self.arrays[k][0].at[self.strip(step), self.place.core]
+        return pltpu.make_async_copy(whole, self.halves[k].at[self.strip(step)], self.load.at[k, step])
+
+    def twin_copy(self, k, step):
+        place = self.place
+        whole = self.arrays[k][0].at[self.strip(step), 1 - place.core]
+        return remote(
+            whole,
+            self.twins[k].at[self.strip(step)],
+            self.twin_sems[0].at[k, step],
+            self.twin_sems[1].at[k, step],
+            place.twin(),
+        )
+
+    def side_copy(self, k, column_step, chip_step, device):
+        return remote(
+            self.halves[k].at[self.spot(column_step, chip_step)],
+            self.sides[k].at[column_step, chip_step],
+            self.side_sems[0].at[k, column_step, chip_step],
+            self.side_sems[1].at[k, column_step, chip_step],
+            device,
+        )
+
+    def deep_copy(self, k, chip_step):
+        return remote(
+            self.halves[k].at[self.spot(0, chip_step)],
+            self.deeps[k].at[chip_step],
+            self.deep_sems[0].at[k, chip_step],
+            self.deep_sems[1].at[k, chip_step],
+            self.place.near(chip_step),
+        )
+
+    def start(self):
+        order = range(self.place.columns - 1, -1, -1)
+        for step in order:
+            for k in self.every:
+                self.twin_copy(k, step).start()
+                self.load_copy(k, step).start()
+
+    def fold(self, step):
+        for k in self.every:
+            self.load_copy(k, step).wait()
+            self.twin_copy(k, step).wait_recv()
+            half, twin = self.halves[k], self.twins[k]
+            for chip_step in range(self.place.chips):
+                spot = self.spot(step, chip_step)
+                half[spot] = (half[spot].astype(F32) + twin[spot].astype(F32)).astype(BF)
+
+    def corner(self, chip_step):
+        self.sent.append((3, chip_step))
+        for k in self.every:
+            self.side_copy(k, 3, chip_step, self.place.beside(1 + chip_step % 2)).start()
+
+    def side(self, column_step, chip_step):
+        self.sent.append((column_step, chip_step))
+        for k in self.every:
+            self.side_copy(k, column_step, chip_step, self.place.beside(column_step)).start()
+
+    def combine(self, chip_step):
+        for k in self.every:
+            self.side_copy(k, 3, chip_step, self.place.twin()).wait_recv()
+            spot = self.spot(2 - chip_step % 2, chip_step)
+            half = self.halves[k]
+            half[spot] = (half[spot].astype(F32) + self.sides[k][3, chip_step].astype(F32)).astype(BF)
+
+    def merge(self, chip_step):
+        last = 3 if self.square else self.place.columns
+        for k in self.every:
+            spot = self.spot(0, chip_step)
+            total = self.halves[k][spot].astype(F32)
+            for step in range(1, last):
+                self.side_copy(k, step, chip_step, self.place.twin()).wait_recv()
+                total = total + self.sides[k][step, chip_step].astype(F32)
+            self.halves[k][spot] = total.astype(BF)
+
+    def deep(self, chip_step):
+        for k in self.every:
+            self.deep_copy(k, chip_step).start()
+
+    def finish(self):
+        place = self.place
+        for k in self.every:
+            total = self.halves[k][self.spot(0, 0)].astype(F32)
+            for step in range(1, place.chips):
+                self.deep_copy(k, step).wait_recv()
+                total = total + self.deeps[k][step].astype(F32)
+            self.arrays[k][1][...] = total
+            for step in range(1, place.chips):
+                self.deep_copy(k, step).wait_send()
+            for step in range(place.columns):
+                self.twin_copy(k, step).wait_send()
+            for column_step, chip_step in self.sent:
+                self.side_copy(k, column_step, chip_step, place.twin()).wait_send()
+
+    def plan(self):
+        chips, columns = self.place.chips, self.place.columns
+        stages = [(0, self.start)]
+        if not self.square:
+            for step in range(columns):
+                stages.append((1, lambda step=step: self.fold(step)))
+            for step in range(1, columns):
+                for chip_step in range(chips):
+                    stages.append((3, lambda a=step, b=chip_step: self.side(a, b)))
+            for chip_step in range(chips):
+                stages.append((16, lambda b=chip_step: self.merge(b)))
+            for chip_step in range(1, chips):
+                stages.append((17, lambda b=chip_step: self.deep(b)))
+            return stages
+        odd = list(range(1, chips, 2))
+        even = list(range(2, chips, 2))
+
+        def many(moment, call, *steps):
+            for step in steps:
+                stages.append((moment, lambda step=step: call(*step)))
+
+        many(1, self.fold, (3,))
+        many(2, self.corner, *[(b,) for b in even + odd])
+        many(2, self.fold, (1,), (2,))
+        many(3, self.side, *[(1, b) for b in even], *[(2, b) for b in odd])
+        many(4, self.fold, (0,))
+        many(7, self.combine, *[(b,) for b in odd + even])
+        many(8, self.side, *[(1, b) for b in odd], *[(2, b) for b in even])
+        many(8, self.corner, (0,))
+        many(8, self.side, (1, 0))
+        for i, b in enumerate(odd):
+            moment = 11 + (2 * i * 2) // max(len(odd), 1)
+            many(moment, self.merge, (b,))
+            many(moment + 1, self.deep, (b,))
+        many(15, self.combine, (0,))
+        many(15, self.merge, *[(b,) for b in even])
+        many(16, self.side, (2, 0))
+        many(16, self.deep, *[(b,) for b in even])
+        many(20, self.merge, (0,))
+        return stages
+
+
+def reduce_scratch(grid, shapes):
+    columns, chips, count = grid.columns, grid.chips, len(shapes)
+    buffers = []
+    for lead in ((columns * chips,), (columns * chips,), (columns, chips), (chips,)):
+        buffers = buffers + [pltpu.VMEM(lead + tuple(shape), BF) for shape in shapes]
+    dma = pltpu.SemaphoreType.DMA
+    sems = [dma((count, columns))] * 3 + [dma((count, columns, chips))] * 2 + [dma((count, chips))] * 2
+    return buffers + sems
+
+
+def reduce_of(place, wholes, results, scratch):
+    count = len(wholes)
+    groups = [scratch[i * count : (i + 1) * count] for i in range(4)]
+    sems = scratch[4 * count : 4 * count + 7]
+    return Reduce(
+        place, list(zip(wholes, results)), groups, (sems[0], sems[1:3], sems[3:5], sems[5:7])
+    )
+
+
+def by_place(grid, array_in, rows):
+    return array_in.reshape(grid.columns * grid.chips, 2, rows, -1)
+
+
+def row_exchange(place, source, target, send, receive):
+    def copy(step):
+        return remote(
+            source.at[place.owner ^ step],
+            target.at[place.owner],
+            send.at[step],
+            receive.at[step],
+            place.at_owner(step),
+        )
+
+    def finish():
+        for step in range(1, place.seqs):
+            landed = target.at[place.owner ^ step]
+            remote(landed, landed, send.at[step], receive.at[step], place.at_owner(step)).wait_recv()
+            copy(step).wait_send()
+
+    def start():
+        for step in range(1, place.seqs):
+            copy(step).start()
+
+    return start, finish
+
+
+def end_exchange(grid, rows, wholes):
+    shapes = [whole.shape[2:] for whole in wholes]
+    count = len(wholes)
+
+    def kernel(rows_ref, *refs):
+        whole_refs, back_ref, results = refs[:count], refs[count], refs[count + 1 : 2 * count + 1]
+        row_hold, hold_sem, row_send, row_receive = refs[2 * count + 1 : 2 * count + 5]
+        place = Place(grid)
+        meet(place.neighbours())
+        reduce = reduce_of(place, whole_refs, results, refs[2 * count + 5 :])
+        start_rows, finish_rows = row_exchange(place, rows_ref, back_ref, row_send, row_receive)
+        stages = reduce.plan()
+        stages[0][1]()
+        start_rows()
+        through(rows_ref.at[place.owner], row_hold, back_ref.at[place.owner], hold_sem)
+        for _, action in stages[1:]:
+            action()
+        reduce.finish()
+        finish_rows()
+
+    return pl.pallas_call(
+        kernel,
+        in_specs=[HBM] * (count + 1),
+        out_specs=[HBM] + [pl.BlockSpec(memory_space=pltpu.VMEM)] * count,
+        out_shape=[jax.ShapeDtypeStruct(rows.shape, BF)]
+        + [jax.ShapeDtypeStruct(shape, F32) for shape in shapes],
+        scratch_shapes=[
+            pltpu.VMEM(rows.shape[1:], BF),
+            pltpu.SemaphoreType.DMA(()),
+            pltpu.SemaphoreType.DMA((grid.seqs,)),
+            pltpu.SemaphoreType.DMA((grid.seqs,)),
+        ]
+        + reduce_scratch(grid, shapes),
+        compiler_params=pltpu.CompilerParams(
+            collective_id=3, has_side_effects=True, vmem_limit_bytes=40 << 20
+        ),
+        name="end_exchange",
+    )(rows, *wholes)
 
 
 LOG2E = 1.4426950408889634
@@ -512,106 +731,220 @@
     )(inputs, key_bias, inputs, inputs, inputs, *shards)
 
 
-def attention_back(inputs, others, key_bias, log_totals, context, grad_context, block=256, chunk=1024):
-    rows, width = inputs.shape
-    pairs = width // (6 * HD)
-    sources = [inputs] + list(others)
-    count = len(sources)
+def attention_back(grid, inputs, key_bias, log_totals, context, grad_context, wholes, rows_out, block=256, chunk=1024):
+    rows = inputs.shape[0]
+    width = inputs.shape[1] // 3
+    pairs = width // (2 * HD)
+    count = grid.group
     keys = rows * count
     blocks = rows // block
+    steps = pairs * blocks
     chunk = min(chunk, rows)
     chunks = keys // chunk
-
-    def kernel(q_ref, bias_ref, l_ref, o_ref, g_ref, *refs):
-        k_refs, v_refs = refs[:count], refs[count : 2 * count]
-        out_ref, other_refs = refs[2 * count], refs[2 * count + 1 : 3 * count]
-        k_own, k_turned, v_all, grad_k, grad_v = refs[3 * count :]
-        for i in range(count):
-            at = slice(i * rows, (i + 1) * rows)
-            v_all[at, :] = v_refs[i][...]
+    late = len(wholes)
+    shapes = [whole.shape[2:] for whole in wholes]
+    away = max(count - 1, 1)
+
+    def kernel(q_ref, bias_ref, l_ref, o_ref, g_ref, k_ref, v_ref, all_ref, rows_ref, *refs):
+        whole_refs = refs[:late]
+        out_ref, back_ref = refs[late : late + 2]
+        results = refs[late + 2 : 2 * late + 2]
+        rest = refs[2 * late + 2 :]
+        k_own, k_turned, v_all, grad_k, grad_v, far, far_out, far_in, row_hold, hold_sem = rest[:10]
+        far_send, far_receive, out_send, in_receive, row_send, row_receive = rest[10:16]
+        pair, turn = pl.program_id(0), pl.program_id(1)
+        now = pair * blocks + turn
+        place = Place(grid)
+        reduce = reduce_of(place, whole_refs, results, rest[16:])
+        start_rows, finish_rows = row_exchange(place, rows_ref, back_ref, row_send, row_receive)
+
+        def far_copy(step, which, kind):
+            first = pl.multiple_of(which * 2 * HD + (kind + 1) * width, 2 * HD)
+            return remote(
+                all_ref.at[:, pl.ds(first, 2 * HD)],
+                far.at[step - 1, kind, which],
+                far_send.at[step - 1, kind, which],
+                far_receive.at[step - 1, kind, which],
+                place.at_member(step),
+            )
+
+        def back_copy(step, which, kind):
+            return remote(
+                far_out.at[step - 1, kind, which],
+                far_in.at[step - 1, kind, which],
+                out_send.at[step - 1, kind, which],
+                in_receive.at[step - 1, kind, which],
+                place.at_member(count - step),
+            )
+
+        def take_back(which):
+            for kind in range(2):
+                first = pl.multiple_of(which * 2 * HD + (kind + 1) * width, 2 * HD)
+                total = out_ref[:, pl.ds(first, 2 * HD)].astype(F32)
+                for step in range(1, count):
+                    back_copy(step, which, kind).wait_recv()
+                    total = total + far_in[step - 1, kind, which].astype(F32)
+                out_ref[:, pl.ds(first, 2 * HD)] = total.astype(BF)
+
+        def send_back(which):
+            for step in range(1, count):
+                for kind in range(2):
+                    back_copy(step, which, kind).start()
+
+        def first_step():
+            meet(place.neighbours() + [place.at_member(s) for s in range(1, count) if count > 2])
+            for which in range(pairs):
+                for step in range(1, count):
+                    for kind in range(2):
+                        far_copy(step, which, kind).start()
+
+        actions = [(0, first_step)] + reduce.plan()
+        actions.append((0, start_rows))
+        actions.append(
+            (1, lambda: through(rows_ref.at[place.owner], row_hold, back_ref.at[place.owner], hold_sem))
+        )
+        moments = {}
+        for moment, action in actions:
+            moments.setdefault(moment * steps // 24, []).append(action)
+        for moment, group in sorted(moments.items()):
+
+            @pl.when(now == moment)
+            def _(group=group):
+                for action in group:
+                    action()
+
+        @pl.when((turn == 0) & (pair > 0))
+        def _():
+            send_back(pair - 1)
+
+        @pl.when(turn == 0)
+        def _():
+            for step in range(1, count):
+                for kind in range(2):
+                    far_copy(step, pair, kind).wait_recv()
+            for i in range(count):
+                at = slice(i * rows, (i + 1) * rows)
+                v_all[at, :] = v_ref[...] if i == 0 else far[i - 1, 1, pair]
+                key = k_ref[...] if i == 0 else far[i - 1, 0, pair]
+                for half in range(2):
+                    own, spare = own_lanes(half, rows)
+                    zero = jnp.zeros_like(key)
+                    k_own[half, at, :] = jnp.where(own, key, jnp.where(spare, bias_ref[at, :], zero))
+                    k_turned[half, :, at] = jnp.transpose(jnp.where(own, key, zero))
+            grad_k[...] = jnp.zeros_like(grad_k)
+            grad_v[...] = jnp.zeros_like(grad_v)
+
+        query, grad = q_ref[...], g_ref[...]
+        turned = jnp.transpose(grad.astype(F32) * o_ref[...].astype(F32))
+        asks, plain, grads, centres, logs = [], [], [], [], []
+        for half in range(2):
+            own, spare = own_lanes(half, block)
+            zero = jnp.zeros_like(query)
+            asks.append(jnp.where(own, query, jnp.where(spare, zero + 1, zero)))
+            plain.append(jnp.where(own, query, zero))
+            grads.append(jnp.where(own, grad, zero))
+            centres.append(jnp.sum(turned[HD * half : HD * half + HD], axis=0, keepdims=True))
+            logs.append(l_ref[half : half + 1, :])
+        grad_q = None
+        for c in range(chunks):
+            span = slice(c * chunk, (c + 1) * chunk)
+            weights, slopes = [], []
             for half in range(2):
-                own, spare = own_lanes(half, rows)
-                key = k_refs[i][...]
-                zero = jnp.zeros_like(key)
-                k_own[half, at, :] = jnp.where(own, key, jnp.where(spare, bias_ref[at, :], zero))
-                k_turned[half, :, at] = jnp.transpose(jnp.where(own, key, zero))
-        grad_k[...] = jnp.zeros_like(grad_k)
-        grad_v[...] = jnp.zeros_like(grad_v)
-        place = pl.program_id(0)
-
-        @pl.loop(0, blocks)
-        def _(j):
-            at = pl.ds(pl.multiple_of(j * block, block), block)
-            query, grad = q_ref[at, :], g_ref[at, :]
-            turned = jnp.transpose(grad.astype(F32) * o_ref[at, :].astype(F32))
-            asks, plain, grads, centres, logs = [], [], [], [], []
-            for half in range(2):
-                own, spare = own_lanes(half, block)
-                zero = jnp.zeros_like(query)
-                asks.append(jnp.where(own, query, jnp.where(spare, zero + 1, zero)))
-                plain.append(jnp.where(own, query, zero))
-                grads.append(jnp.where(own, grad, zero))
-                centres.append(jnp.sum(turned[HD * half : HD * half + HD], axis=0, keepdims=True))
-                logs.append(l_ref[half : half + 1, at])
-            grad_q = None
-            for c in range(chunks):
-                span = slice(c * chunk, (c + 1) * chunk)
-                weights, slopes = [], []
-                for half in range(2):
-                    scores = dot_nt(k_own[half, span, :], asks[half])
-                    grad_weights = dot_nt(v_all[span, :], grads[half])
-                    exact = jnp.exp2(scores * SCALE - logs[half])
-                    slope = (exact * (grad_weights - centres[half])).astype(BF)
-                    weights.append(exact.astype(BF))
-                    slopes.append(slope)
-                    step = matmul(k_turned[half, :, span], slope)
-                    grad_q = step if grad_q is None else grad_q + step
-                grad_v[span, :] += matmul(weights[0], grads[0]) + matmul(weights[1], grads[1])
-                grad_k[span, :] += matmul(slopes[0], plain[0]) + matmul(slopes[1], plain[1])
-            columns = pl.ds(pl.multiple_of(place * 2 * HD, 2 * HD), 2 * HD)
-            out_ref[at, columns] = (jnp.transpose(grad_q) * 0.125).astype(BF)
-
-        for i in range(count):
-            at = slice(i * rows, (i + 1) * rows)
-            target, shift = (out_ref, pairs) if i == 0 else (other_refs[i - 1], 0)
-            for value, offset, scale in ((grad_k, 0, 0.125), (grad_v, pairs, 1.0)):
-                first_column = pl.multiple_of((place + shift + offset) * 2 * HD, 2 * HD)
-                target[:, pl.ds(first_column, 2 * HD)] = (value[at, :] * scale).astype(BF)
+                scores = dot_nt(k_own[half, span, :], asks[half])
+                grad_weights = dot_nt(v_all[span, :], grads[half])
+                exact = jnp.exp2(scores * SCALE - logs[half])
+                slope = (exact * (grad_weights - centres[half])).astype(BF)
+                weights.append(exact.astype(BF))
+                slopes.append(slope)
+                step = matmul(k_turned[half, :, span], slope)
+                grad_q = step if grad_q is None else grad_q + step
+            grad_v[span, :] += matmul(weights[0], grads[0]) + matmul(weights[1], grads[1])
+            grad_k[span, :] += matmul(slopes[0], plain[0]) + matmul(slopes[1], plain[1])
+        at = pl.ds(pl.multiple_of(turn * block, block), block)
+        out_ref[at, pl.ds(pl.multiple_of(pair * 2 * HD, 2 * HD), 2 * HD)] = (
+            jnp.transpose(grad_q) * 0.125
+        ).astype(BF)
+
+        @pl.when(turn == blocks - 1)
+        def _():
+            for i in range(count):
+                at = slice(i * rows, (i + 1) * rows)
+                for kind, value, scale in ((0, grad_k, 0.125), (1, grad_v, 1.0)):
+                    low = (value[at, :] * scale).astype(BF)
+                    if i == 0:
+                        first = pl.multiple_of(pair * 2 * HD + (kind + 1) * width, 2 * HD)
+                        out_ref[:, pl.ds(first, 2 * HD)] = low
+                    else:
+                        far_out[i - 1, kind, pair] = low
+
+        @pl.when((turn == blocks - 1) & (pair > 0))
+        def _():
+            take_back(pair - 1)
+
+        @pl.when(now == steps - 1)
+        def _():
+            reduce.finish()
+            send_back(pairs - 1)
+            finish_rows()
+            take_back(pairs - 1)
+            for step in range(1, count):
+                for which in range(pairs):
+                    for kind in range(2):
+                        far_copy(step, which, kind).wait_send()
+                        back_copy(step, which, kind).wait_send()
 
     def column(first):
-        return pl.BlockSpec((rows, 2 * HD), lambda i: (0, i + first))
-
-    first = 0
-    heads = 2 * pairs
+        return pl.BlockSpec((rows, 2 * HD), lambda i, j: (0, i + first))
+
+    def tile():
+        return pl.BlockSpec((block, 2 * HD), lambda i, j: (j, i))
+
+    def resident(shape):
+        return pl.BlockSpec(shape, lambda i, j: (0,) * len(shape))
+
+    far_sems = pltpu.SemaphoreType.DMA((away, 2, pairs))
+    far_buffer = pltpu.VMEM((away, 2, pairs, rows, 2 * HD), BF)
     return pl.pallas_call(
         kernel,
-        grid=(pairs,),
+        grid=(pairs, blocks),
         in_specs=[
-            column(0),
-            pl.BlockSpec((keys, 2 * HD), lambda i: (0, 0)),
-            pl.BlockSpec((None, 8, rows), lambda i: (i + first, 0, 0)),
-            column(first),
-            column(first),
+            tile(),
+            resident((keys, 2 * HD)),
+            pl.BlockSpec((None, 8, block), lambda i, j: (i, 0, j)),
+            tile(),
+            tile(),
+            column(pairs),
+            column(2 * pairs),
+            HBM,
+            HBM,
         ]
-        + [column(pairs)] * count
-        + [column(2 * pairs)] * count,
-        out_specs=[pl.BlockSpec((rows, width), lambda i: (0, 0))]
-        + [pl.BlockSpec((rows, 4 * HD * pairs), lambda i: (0, 0))] * (count - 1),
-        out_shape=[jax.ShapeDtypeStruct((rows, width), BF)]
-        + [jax.ShapeDtypeStruct((rows, 4 * HD * pairs), BF)] * (count - 1),
+        + [HBM] * late,
+        out_specs=[resident(inputs.shape), HBM] + [resident(tuple(shape)) for shape in shapes],
+        out_shape=[jax.ShapeDtypeStruct(inputs.shape, BF), jax.ShapeDtypeStruct(rows_out.shape, BF)]
+        + [jax.ShapeDtypeStruct(shape, F32) for shape in shapes],
         scratch_shapes=[
             pltpu.VMEM((2, keys, 2 * HD), BF),
             pltpu.VMEM((2, 2 * HD, keys), BF),
             pltpu.VMEM((keys, 2 * HD), BF),
             pltpu.VMEM((keys, 2 * HD), F32),
             pltpu.VMEM((keys, 2 * HD), F32),
-        ],
-        compiler_params=pltpu.CompilerParams(vmem_limit_bytes=48 << 20),
+            far_buffer,
+            far_buffer,
+            far_buffer,
+            pltpu.VMEM(rows_out.shape[1:], BF),
+            pltpu.SemaphoreType.DMA(()),
+        ]
+        + [far_sems] * 4
+        + [pltpu.SemaphoreType.DMA((grid.seqs,))] * 2
+        + reduce_scratch(grid, shapes),
+        compiler_params=pltpu.CompilerParams(
+            collective_id=2, has_side_effects=True, vmem_limit_bytes=61 << 20
+        ),
         cost_estimate=pl.CostEstimate(
-            flops=40 * heads * rows * keys * HD, bytes_accessed=12 * rows * width, transcendentals=heads * rows * keys
+            flops=40 * H * rows * keys * HD, bytes_accessed=12 * rows * width, transcendentals=H * rows * keys
         ),
         name="attention_back",
-    )(inputs, key_bias, log_totals, context, grad_context, *sources, *sources)
+    )(inputs, key_bias, log_totals, context, grad_context, inputs, inputs, inputs, rows_out, *wholes)
 
 
 def body(
@@ -687,7 +1020,7 @@
     out_full = out_full.reshape(width, width)
     up_full = up_full.reshape(width, hidden)
     down_full = down_full.reshape(hidden, width)
-    others = [grid.to_member(inputs, step) for step in range(1, grid.group)]
+    cotangent = lax.optimization_barrier((cotangent, context))[0]
     grad_in = to_sequences(grid, cotangent)
 
     first_sum = flat_in.astype(F32) + matmul(context, out_full) + out_add
@@ -697,7 +1030,7 @@
     activated = jax.nn.gelu(up_pre, approximate=False).astype(BF)
     second_sum = first_low.astype(F32) + matmul(activated, down_full) + down_add
     second_norm, second_unit, second_factor = normalize(second_sum, gain_two, shift_two)
-    output = from_sequences(grid, (second_norm * live_rows).astype(BF), length)
+    output = (second_norm * live_rows).astype(BF).reshape(seqs, length, width)
 
     grad_output = grad_in.astype(F32) * live_rows
     grad_gain_two = jnp.sum(grad_output * second_unit, axis=0)
@@ -718,36 +1051,43 @@
     grad_out = left_product(context, grad_attend).astype(BF)
     grad_context = right_product(grad_attend, out_full).astype(BF)
 
-    grad_down_own = scatter_sum(grid, grad_down)
-    grad_up_own = scatter_sum(grid, grad_up)
-    grad_out_own = scatter_sum(grid, grad_out)
-
-    own, *away = attention_back(inputs, others, key_bias, log_totals, context, grad_context)
-    grad_kv = own[:, width:].astype(F32)
-    for step, piece in enumerate(away, 1):
-        grad_kv = grad_kv + grid.to_member(piece, step, back=True).astype(F32)
-    low = jnp.concatenate([own[:, :width], grad_kv.astype(BF)], axis=1)
+    def pack(grads, more=()):
+        count = len(grads)
+        table = jnp.stack(grads).reshape(count, devices, slim).transpose(1, 0, 2)
+        table = jnp.concatenate([table.reshape(devices, count * slim), *more], axis=1).astype(BF)
+        size = table.shape[1]
+        table = jnp.pad(table, ((0, 0), (0, -size % 128)))
+        return jnp.broadcast_to(table[:, None, :], (devices, 8, table.shape[1])).reshape(devices * 8, -1)
+
+    middle = pack(
+        [grad_out_add, grad_down_add, grad_gain_one, grad_shift_one, grad_gain_two, grad_shift_two],
+        (grad_up_add.reshape(devices, tall),),
+    )
+    wholes = [
+        by_place(grid, grad_up, slim),
+        by_place(grid, grad_down, tall),
+        by_place(grid, grad_out, slim),
+        by_place(grid, middle, 8),
+    ]
+    low, output, grad_up_own, grad_down_own, grad_out_own, middle_own = attention_back(
+        grid, inputs, key_bias, log_totals, context, grad_context, wholes, output
+    )
     query_adds = jnp.sum(low[:, :width].astype(F32), axis=0)
     value_adds = jnp.sum(low[:, 2 * width :].astype(F32), axis=0)
     tokens_grad = grad_residual
     for i in range(3):
         tokens_grad = tokens_grad + right_product(low[:, i * width : (i + 1) * width], into_full[i])
-    grad_into_own = scatter_sum(grid, left_product(flat_in, low).astype(BF))
-    tokens_grad = from_sequences(grid, tokens_grad.astype(BF), length).astype(F32)
-
-    def pack(grads):
-        count = len(grads)
-        table = jnp.stack(grads).reshape(count, devices, slim).transpose(1, 0, 2)
-        return table.reshape(devices, count * slim)
-
-    middle = pack([grad_out_add, grad_down_add, grad_gain_one, grad_shift_one, grad_gain_two, grad_shift_two])
-    middle = jnp.concatenate([middle, grad_up_add.reshape(devices, tall)], axis=1).astype(BF)
-    middle_own = scatter_sum(grid, middle)[0]
-    last = pack([query_adds, value_adds]).astype(BF)
-    last_own = scatter_sum(grid, last)[0]
-    vector_outs = [last_own[:slim], last_own[slim:]]
+    wholes = [
+        by_place(grid, left_product(flat_in, low).astype(BF), slim),
+        by_place(grid, pack([query_adds, value_adds]), 8),
+    ]
+    tokens_grad = tokens_grad.astype(BF).reshape(seqs, length, width)
+    tokens_grad, grad_into_own, last_own = end_exchange(grid, tokens_grad, wholes)
+    tokens_grad = tokens_grad.astype(F32)
+    middle_own, last_own = middle_own[0], last_own[0]
+    vector_outs = [last_own[:slim], last_own[slim : 2 * slim]]
     vector_outs = vector_outs + [middle_own[i * slim : (i + 1) * slim] for i in range(6)]
-    up_add_own = middle_own[6 * slim :]
+    up_add_own = middle_own[6 * slim : 6 * slim + tall]
     matrix_outs = [grad_into_own[:, i * width : (i + 1) * width] for i in range(3)]
     return (
         output,

time: 575 us -> 464 us (0.81)
  waiting for transfers between devices: 105 us -> 0.01 us
  starting transfers between devices: 64.8 us -> 4.87 us
  Pallas kernels: 224 us -> 267 us
  matrix products: 104 us -> 117 us
  other arithmetic: 36.4 us -> 26.4 us
  local copies, waits for them, and re-layouts: 33.5 us -> 42.3 us
    ppermute x44 -> x0, waiting for transfers between devices: 76.8 us -> none  [the longest x18 44.5 us: to_column(): return lax.ppermute(array_in, 'dp', pairs)]
    pallas_call x1 -> x2, Pallas kernels: 76.9 us -> 148 us  [the longest x1 99.8 us: attention_back(): pl.pallas_call(kernel, grid=(pairs, blocks), in_specs=[tile(), resident((...]
    ppermute x44 -> x0, starting transfers between devices: 51.2 us -> none  [the longest x18 28.3 us: to_chip(): return lax.ppermute(array_in, 'seq', pairs)]
    ppermute x9 -> x3, waiting for transfers between devices: 27.9 us -> 0.01 us  [to_owner(): return lax.ppermute(array_in, 'seq', pairs)]
    pallas_call x1, Pallas kernels: 72.1 us -> 44.9 us  [start_exchange(): pl.pallas_call(kernel, in_specs=[HBM] * 3, out_specs=[HBM] * 3, out_shape...]
    convert_element_type x15 -> x2, other arithmetic: 11.8 us -> 2.65 us  [the longest x1 1.93 us: body(): tokens_grad = tokens_grad.astype(F32)]
    ppermute x9 -> x3, starting transfers between devices: 13.6 us -> 4.87 us  [to_owner(): return lax.ppermute(array_in, 'seq', pairs)]
    dot_general x6, matrix products: 49.4 us -> 57.3 us  [matmul(): return jnp.dot(left, right, preferred_element_type=F32)]
  transfers between devices with their start and end apart: 53 -> 3, of which waited for: 21 -> 0; matrix products, arithmetic and copies ran while one was open for 27% -> 13% of each run, Pallas kernels for 39% -> 0%
where the time goes in v4:
time: 464 us; the launch traced here: 459 us
  Pallas kernels  267 us (58%)
  matrix products  117 us (25%)
  local copies, waits for them, and re-layouts  42.3 us (9%)
  other arithmetic  26.4 us (6%)
  starting transfers between devices  4.87 us (1%)
    pallas_call x1, Pallas kernels, attention_back(): pl.pallas_call(kernel, grid=(pairs, blocks), in_specs=[tile(), resident((...  99.8 us
    pallas_call x1, Pallas kernels, attention(): pl.pallas_call(kernel, grid=(pairs, blocks), in_specs=[pl.BlockSpec((bloc...  73.5 us
    dot_general x6, matrix products, matmul(): return jnp.dot(left, right, preferred_element_type=F32)  57.3 us
    pallas_call x1, Pallas kernels, end_exchange(): pl.pallas_call(kernel, in_specs=[HBM] * (count + 1), out_specs=[HBM] + [p...  48.5 us
    pallas_call x1, Pallas kernels, start_exchange(): pl.pallas_call(kernel, in_specs=[HBM] * 3, out_specs=[HBM] * 3, out_shape...  44.9 us
    dot_general x6, matrix products, right_product(): lax.dot_general(left, right, (((1,), (1,)), ((), ())), preferred_element_...  34.7 us
    dot_general x4, matrix products, left_product(): lax.dot_general(left, right, (((0,), (0,)), ((), ())), preferred_element_...  24.5 us
  transfers between devices with their start and end apart: 3, of which 0 were waited for; matrix products, arithmetic and copies ran while one was open for 13% of the time, Pallas kernels for 0%

profile of v4, /device:TPU:0, one launch (start us, length us, event | category | flops | bytes accessed | tf_op | source)
XLA Modules:
  0.0 458.5 jit_solution(2562345062409372442)
XLA Ops:
  0.7 6.1 %concatenate.20 = bf16[288]{0:T(512)(128)(2,1)S(1)} concatenate(bf16[24]{0:T(256)(128)(2,1)} %param.28, bf16[24]{0:T(256)(128)(2,1)} %param.29, bf16[24]{0:T(256)(128)(2,1)} %param.30, bf16[24]{0:T(256)(128)(2,1)} %param.32, bf16[24]{0:T(256)(128)(2,1)} %param.33, bf16[24]{0:T(256)(128)(2,1)} %param.34, bf16[24]{0:T(256)(128)(2,1)} %param.35, bf16[24]{0:T(256)(128)(2,1)} %param.36, ...), dimensions={0} | concatenate | bytes 1152 | tf_op jit(solution)/shard_map/concatenate | solution.py:988
  8.9 44.9 %start_exchange.1 = (bf16[4,256,768]{2,1,0:T(8,128)(2,1)}, bf16[3,32,24,768]{3,2,1,0:T(8,128)(2,1)}, bf16[32,8,384]{2,1,0:T(8,128)(2,1)}) custom-call(bf16[4,256,768]{2,1,0:T(8,128)(2,1)} %tokens_ref.1, bf16[3,24,768]{2,1,0:T(8,128)(2,1)} %pad_maximum_fusion.1.into_ref, bf16[8,384]{1,0:T(8,128)(2,1)} %scatter.4.vectors_ref), custom_call_target="tpu_custom_call" | custom-call | tf_op jit(solution)/shard_map/start_exchange/pallas_call | solution.py:322
  60.0 2.6 slice_reduce_fusion.2
  69.0 2.9 convolution_convert_fusion.4
  74.9 2.9 pad_maximum_fusion.q_ref.k_ref.v_ref.all_ref
  78.1 73.5 %attention.1 = (bf16[1024,768]{1,0:T(8,128)(2,1)S(1)}, f32[6,8,1024]{2,1,0:T(8,128)S(1)}, bf16[32,24,768]{2,1,0:T(8,128)(2,1)S(1)}, bf16[32,24,3072]{2,1,0:T(8,128)(2,1)}, bf16[32,96,768]{2,1,0:T(8,128)(2,1)}) custom-call(bf16[1024,2304]{1,0:T(8,128)(2,1)} %pad_maximum_fusion.q_ref.k_ref.v_ref.all_ref, bf16[2048,128]{1,0:T(8,128)(2,1)S(1)} %broadcast_in_dim.35.bias_ref, ...), custom_call_target="tpu_custom_call" | custom-call | flops 25769803776 | bytes 6291456 | tf_op jit(solution)/shard_map/attention/pallas_call | solution.py:694
  153.6 2.5 dynamic-slice_bitcast_fusion
  156.6 4.5 collective-permute-start.1
  164.3 3.0 fusion.35
  170.6 37.1 %fusion.2 = (bf16[1024,3072]{1,0:T(8,128)(2,1)S(1)}, f32[1024,3072]{1,0:T(8,128)}) fusion(f32[3072]{0:T(1024)S(1)} %reshape.317, bf16[768,3072]{1,0:T(8,128)(2,1)} %bitcast.134, f32[1024,768]{1,0:T(8,128)} %copy-done.8, f32[768]{0:T(1024)S(1)} %add.256, f32[768]{0:T(1024)S(1)} %mul.205, f32[1024]{0:T(1024)S(1)} %add_rsqrt_fusion.1, ...), kind=kOutput, calls=%fused_computation.4 | convolution fusion | flops 5043388416 | bytes 26765312 | tf_op jit(solution)/shard_map/dot_general | solution.py:19
  207.8 11.5 %fusion.36 = (f32[1024]{0:T(1024)S(1)}, f32[1024,768]{1,0:T(8,128)}) fusion(f32[768]{0:T(1024)S(1)} %add.262, bf16[1024,3072]{1,0:T(8,128)(2,1)S(1)} %get-tuple-element.110, bf16[3072,768]{1,0:T(8,128)(2,1)} %bitcast.138, f32[768]{0:T(1024)S(1)} %add.256, f32[768]{0:T(1024)S(1)} %mul.205, f32[1024]{0:T(1024)S(1)} %add_rsqrt_fusion.1, ...), kind=kOutput, calls=%fused_computation.133 | convolution fusion | flops 4838915072 | bytes 17323008 | tf_op jit(solution)/shard_map/dot_general | solution.py:19
  225.4 4.0 multiply_reduce_fusion
  231.7 2.6 convert_reduce_fusion.1
  234.3 12.3 %fusion.37 = (bf16[3072]{0:T(1024)(128)(2,1)S(1)}, bf16[1024,3072]{1,0:T(8,128)(2,1)S(1)}) fusion(f32[1024,3072]{1,0:T(8,128)} %get-tuple-element.111, f32[3072]{0:T(1024)S(1)} %reshape.317, bf16[3072,768]{1,0:T(8,128)(2,1)S(1)} %bitcast.141, f32[1024,768]{1,0:T(8,128)S(1)} %get-tuple-element.84), kind=kOutput, calls=%fused_computation.134 | convolution fusion | flops 4870370304 | bytes 26757120 | tf_op jit(solution)/shard_map/dot_general | solution.py:27
  246.7 6.1 %multiply_reduce_fusion.1 = (bf16[768]{0:T(1024)(128)(2,1)S(1)}, f32[1024]{0:T(1024)S(1)}, f32[1024]{0:T(1024)S(1)}, bf16[768]{0:T(1024)(128)(2,1)S(1)}, f32[1024,768]{1,0:T(8,128)S(1)}) fusion(f32[1024,768]{1,0:T(8,128)S(1)} %copy-done.10, f32[1024]{0:T(1024)S(1)} %add_rsqrt_fusion.1, f32[1024]{0:T(1024)S(1)} %broadcast_multiply_fusion.4, ...), kind=kOutput, calls=%fused_computation.32 | convolution fusion | flops 4839698432 | bytes 20469760 | tf_op jit(solution)/shard_map/dot_general | solution.py:27
  252.8 8.1 %convolution_convert_fusion.1 = bf16[768,3072]{1,0:T(8,128)(2,1)} fusion(bf16[1024,3072]{1,0:T(8,128)(2,1)S(1)} %get-tuple-element.116, f32[1024,768]{1,0:T(8,128)S(1)} %copy-done.10, f32[768]{0:T(1024)S(1)} %add.256, f32[768]{0:T(1024)S(1)} %mul.205, f32[1024]{0:T(1024)S(1)} %add_rsqrt_fusion.1, f32[1024]{0:T(1024)S(1)} %broadcast_multiply_fusion.4), kind=kOutput, calls=%fused_computation.26 | convolution fusion | flops 4838129664 | bytes 14170112 | tf_op jit(solution)/shard_map/dot_general | solution.py:23
  260.8 9.8 %convolution_convert_fusion = bf16[3072,768]{1,0:T(8,128)(2,1)} fusion(bf16[1024,3072]{1,0:T(8,128)(2,1)} %copy-done.33, f32[1024,768]{1,0:T(8,128)S(1)} %get-tuple-element.84), kind=kOutput, calls=%fused_computation.25 | convolution fusion | flops 4834983936 | bytes 14155776 | tf_op jit(solution)/shard_map/dot_general | solution.py:23
  272.0 2.6 convolution_convert_fusion.3.g_ref
  278.8 99.8 %attention_back.1 = (bf16[1024,2304]{1,0:T(8,128)(2,1)}, bf16[4,256,768]{2,1,0:T(8,128)(2,1)}, f32[24,3072]{1,0:T(8,128)}, f32[96,768]{1,0:T(8,128)}, f32[24,768]{1,0:T(8,128)}, /*index=5*/f32[8,256]{1,0:T(8,128)}) custom-call(bf16[1024,2304]{1,0:T(8,128)(2,1)} %pad_maximum_fusion.q_ref.k_ref.v_ref.all_ref, bf16[2048,128]{1,0:T(8,128)(2,1)} %copy-done, ...), custom_call_target="tpu_custom_call" | custom-call | flops 64424509440 | bytes 9437184 | tf_op jit(solution)/shard_map/attention_back/pallas_call | solution.py:907
  378.6 4.6 %fusion.17 = f32[1024,768]{1,0:T(8,128)} fusion(bf16[768,768]{1,0:T(8,128)(2,1)S(1)} %bitcast.113, bf16[1024,2304]{1,0:T(8,128)(2,1)} %get-tuple-element.57), kind=kOutput, calls=%fused_computation.55 | convolution fusion | flops 1207959552 | bytes 5898240 | tf_op jit(solution)/shard_map/dot_general | solution.py:27
  383.3 3.1 fusion.20
  386.4 4.1 convolution_convert_fusion.2
  397.3 6.0 %add_convert_fusion = bf16[1024,768]{1,0:T(8,128)(2,1)S(1)} fusion(f32[1024,768]{1,0:T(8,128)} %fusion.17, f32[1024,768]{1,0:T(8,128)} %copy-done.11, f32[1024,768]{1,0:T(8,128)} %fusion.20, bf16[768,768]{1,0:T(8,128)(2,1)} %bitcast.108, bf16[1024,2304]{1,0:T(8,128)(2,1)} %get-tuple-element.57), kind=kOutput, calls=%fused_computation.30 | convolution fusion | flops 1211105280 | bytes 13762560 | tf_op jit(solution)/shard_map/dot_general | solution.py:27
  403.4 48.5 %end_exchange.1 = (bf16[4,256,768]{2,1,0:T(8,128)(2,1)S(1)}, f32[24,2304]{1,0:T(8,128)S(1)}, f32[8,128]{1,0:T(8,128)S(1)}) custom-call(bf16[4,256,768]{2,1,0:T(8,128)(2,1)S(1)} %bitcast.103, bf16[16,2,24,2304]{3,2,1,0:T(8,128)(2,1)S(1)} %bitcast.104, bf16[16,2,8,128]{3,2,1,0:T(8,128)(2,1)S(1)} %broadcast_in_dim.73.refs_1_), custom_call_target="tpu_custom_call" | custom-call | tf_op jit(solution)/shard_map/end_exchange/pallas_call | solution.py:558
  (167 shorter events, 53.7 us)
Async XLA Ops:
  56.0 15.9 %copy-start.17 = (bf16[1,32,24,768]{3,2,1,0:T(8,128)(2,1)}, bf16[1,32,24,768]{3,2,1,0:T(8,128)(2,1)S(1)}, u32[]{:S(2)}) copy-start(bf16[1,32,24,768]{3,2,1,0:T(8,128)(2,1)S(1)} %get-tuple-element.89) | copy-start | bytes 3538948
  56.0 15.9 %copy-start.12 = (bf16[1,32,24,768]{3,2,1,0:T(8,128)(2,1)}, bf16[1,32,24,768]{3,2,1,0:T(8,128)(2,1)S(1)}, u32[]{:S(2)}) copy-start(bf16[1,32,24,768]{3,2,1,0:T(8,128)(2,1)S(1)} %get-tuple-element.88) | copy-start | bytes 3538948
  56.0 17.4 %copy-start.15 = (bf16[1,32,24,768]{3,2,1,0:T(8,128)(2,1)}, bf16[1,32,24,768]{3,2,1,0:T(8,128)(2,1)S(1)}, u32[]{:S(2)}) copy-start(bf16[1,32,24,768]{3,2,1,0:T(8,128)(2,1)S(1)} %get-tuple-element.87) | copy-start | bytes 3538948
  74.8 3.2 copy-start.1
  78.1 73.5 %copy-start = (bf16[2048,128]{1,0:T(8,128)(2,1)}, bf16[2048,128]{1,0:T(8,128)(2,1)S(1)}, u32[]{:S(2)}) copy-start(bf16[2048,128]{1,0:T(8,128)(2,1)S(1)} %broadcast_in_dim.35.bias_ref) | copy-start | bytes 1572868
  152.3 15.0 %copy-start.4 = (bf16[1024,768]{1,0:T(8,128)(2,1)}, bf16[1024,768]{1,0:T(8,128)(2,1)S(1)}, u32[]{:S(2)}) copy-start(bf16[1024,768]{1,0:T(8,128)(2,1)S(1)} %get-tuple-element.51.o_ref) | copy-start | bytes 4718596
  156.2 65.9 %collective-permute-start = (bf16[256,768]{1,0:T(8,128)(2,1)}, bf16[256,768]{1,0:T(8,128)(2,1)}, u32[]{:S(2)}, u32[]{:S(2)}) collective-permute-start(bf16[256,768]{1,0:T(8,128)(2,1)} %get-tuple-element.93), channel_id=1, source_target_pairs={{0,2},{1,3},{2,0},{3,1},{4,6},{5,7},{6,4},{7,5},{8,10},{9,11},{10,... | collective-permute-start | bytes 1179656 | tf_op jit(solution)/shard_map/ppermute | solution.py:95
  156.6 67.3 %collective-permute-start.1 = (bf16[256,768]{1,0:T(8,128)(2,1)}, bf16[256,768]{1,0:T(8,128)(2,1)S(1)}, u32[]{:S(2)}, u32[]{:S(2)}) collective-permute-start(bf16[256,768]{1,0:T(8,128)(2,1)} %get-tuple-element.92), channel_id=1, source_target_pairs={{0,4},{1,5},{2,6},{3,7},{4,0},{5,1},{6,2},{7,3},{8,12},{9,13},{10,... | collective-permute-start | bytes 1179656 | tf_op jit(solution)/shard_map/ppermute | solution.py:95
  161.0 63.6 %collective-permute-start.2 = (bf16[256,768]{1,0:T(8,128)(2,1)}, bf16[256,768]{1,0:T(8,128)(2,1)S(1)}, u32[]{:S(2)}, u32[]{:S(2)}) collective-permute-start(bf16[256,768]{1,0:T(8,128)(2,1)} %get-tuple-element.91), channel_id=1, source_target_pairs={{0,6},{1,7},{2,4},{3,5},{4,2},{5,3},{6,0},{7,1},{8,14},{9,15},{10,... | collective-permute-start | bytes 1179656 | tf_op jit(solution)/shard_map/ppermute | solution.py:95
  170.6 37.1 %copy-start.9 = (f32[1024,768]{1,0:T(8,128)S(1)}, f32[1024,768]{1,0:T(8,128)}, u32[]{:S(2)}) copy-start(f32[1024,768]{1,0:T(8,128)} %copy-done.8) | copy-start | bytes 9437188
  207.7 11.6 %copy-start.33 = (bf16[1024,3072]{1,0:T(8,128)(2,1)}, bf16[1024,3072]{1,0:T(8,128)(2,1)S(1)}, u32[]{:S(2)}) copy-start(bf16[1024,3072]{1,0:T(8,128)(2,1)S(1)} %get-tuple-element.110) | copy-start | bytes 18874372
  207.7 11.6 %copy-start.23 = (f32[32,24]{1,0:T(8,128)S(1)}, f32[32,24]{1,0:T(8,128)}, u32[]{:S(2)}) copy-start(f32[32,24]{1,0:T(8,128)} %get-tuple-element.76) | copy-start | bytes 9220
  219.5 5.9 %copy-start.7 = (f32[1024,768]{1,0:T(8,128)S(1)}, f32[1024,768]{1,0:T(8,128)}, u32[]{:S(2)}) copy-start(f32[1024,768]{1,0:T(8,128)} %get-tuple-element.113) | copy-start | bytes 9437188
  225.4 8.9 %slice-start.2 = ((s8[4718592]{0:T(1024)(128)(4,1)}), s8[4194304]{0:T(1024)(128)(4,1)S(1)}, s32[]{:S(2)}) async-start(s8[4718592]{0:T(1024)(128)(4,1)} %bitcast.139), calls=%async_computation.2 | async-start | bytes 8388608
  229.4 4.9 %slice-start.3 = ((s8[4718592]{0:T(1024)(128)(4,1)}), s8[524288]{0:T(1024)(128)(4,1)S(1)}, s32[]{:S(2)}) async-start(s8[4718592]{0:T(1024)(128)(4,1)} %bitcast.139), calls=%async_computation.3 | async-start | bytes 1048576
  231.6 15.0 %slice-start = ((s8[4718592]{0:T(1024)(128)(4,1)}), s8[4194304]{0:T(1024)(128)(4,1)S(1)}, s32[]{:S(2)}) async-start(s8[4718592]{0:T(1024)(128)(4,1)} %bitcast.135), calls=%async_computation | async-start | bytes 8388608
  234.3 12.4 %copy-start.10 = (f32[1024,768]{1,0:T(8,128)S(1)}, f32[1024,768]{1,0:T(8,128)}, u32[]{:S(2)}) copy-start(f32[1024,768]{1,0:T(8,128)} %copy-done.8) | copy-start | bytes 9437188
  234.3 12.4 %slice-start.1 = ((s8[4718592]{0:T(1024)(128)(4,1)}), s8[524288]{0:T(1024)(128)(4,1)S(1)}, s32[]{:S(2)}) async-start(s8[4718592]{0:T(1024)(128)(4,1)} %bitcast.135), calls=%async_computation.1 | async-start | bytes 1048576
  278.8 99.8 %copy-start.18 = (bf16[1,32,24,768]{3,2,1,0:T(8,128)(2,1)S(1)}, bf16[1,32,24,768]{3,2,1,0:T(8,128)(2,1)}, u32[]{:S(2)}) copy-start(bf16[1,32,24,768]{3,2,1,0:T(8,128)(2,1)} %copy-done.17) | copy-start | bytes 3538948
  378.6 4.7 %copy-start.13 = (bf16[1024,2304]{1,0:T(8,128)(2,1)S(1)}, bf16[1024,2304]{1,0:T(8,128)(2,1)}, u32[]{:S(2)}) copy-start(bf16[1024,2304]{1,0:T(8,128)(2,1)} %get-tuple-element.57) | copy-start | bytes 14155780
  378.6 4.7 %copy-start.16 = (bf16[1,32,24,768]{3,2,1,0:T(8,128)(2,1)S(1)}, bf16[1,32,24,768]{3,2,1,0:T(8,128)(2,1)}, u32[]{:S(2)}) copy-start(bf16[1,32,24,768]{3,2,1,0:T(8,128)(2,1)} %copy-done.15) | copy-start | bytes 3538948
  451.9 4.4 copy-start.22
  451.9 5.0 %copy-start.20 = (f32[24,3072]{1,0:T(8,128)S(1)}, f32[24,3072]{1,0:T(8,128)}, u32[]{:S(2)}) copy-start(f32[24,3072]{1,0:T(8,128)} %get-tuple-element.142) | copy-start | bytes 884740
  453.8 3.8 copy-start.19
  (17 other events, 40.1 us)

commit v5 on v4

--- a/solution.py
+++ b/solution.py
@@ -40,12 +40,6 @@
         grad_unit
         - jnp.mean(grad_unit, axis=-1, keepdims=True)
         - unit_rows * jnp.mean(grad_unit * unit_rows, axis=-1, keepdims=True)
-    )
-
-
-def gelu_slope(inputs):
-    return 0.5 * (1.0 + lax.erf(inputs * ROOT_HALF)) + inputs * INV_ROOT_TWO_PI * jnp.exp(
-        -0.5 * inputs * inputs
     )
 
 
@@ -121,14 +115,6 @@
     return to_sequences(grid, rows.reshape(grid.seqs, length, rows.shape[1])).reshape(grid.seqs, length, -1)
 
 
-def row_positions(grid, length):
-    def positions(member):
-        source = jnp.arange(grid.seqs, dtype=jnp.int32)[:, None]
-        return ((source * grid.group + member) * length + jnp.arange(length, dtype=jnp.int32)).reshape(-1)
-
-    return positions
-
-
 MESH = pl.DeviceIdType.MESH
 HBM = pl.BlockSpec(memory_space=pl.ANY)
 
@@ -267,23 +253,40 @@
     copy.wait()
 
 
-def start_exchange(grid, tokens, into, vectors):
+def start_exchange(grid, tokens, into, vectors, lengths, vector_widths):
     seqs, length, width = tokens.shape
     devices = grid.columns * grid.n
-    parts, slim, _ = into.shape
-
-    def kernel(
-        tokens_ref, into_ref, vectors_ref, rows_ref, into_all, vectors_all, *scratch
-    ):
-        row_hold, into_hold, vector_hold, hold_sem, send, receive, row_send, row_receive = scratch
+    slim = into[0].shape[0]
+    parts = len(into)
+    rows = seqs * length
+    tile = vectors.shape
+
+    def spread(table, size):
+        lane = lax.broadcasted_iota(jnp.int32, (128, devices * size), 1).astype(F32)
+        row = lax.broadcasted_iota(jnp.int32, (128, devices * size), 0).astype(F32)
+        within = lane - size * jnp.floor((lane + 0.5) * (1.0 / size))
+        return matmul(table, (row == within).astype(BF))
+
+    def own_block(count, size):
+        lane = lax.broadcasted_iota(jnp.int32, (count, devices * size), 1).astype(F32)
+        return jnp.floor((lane + 0.5) * (1.0 / size))
+
+    def kernel(tokens_ref, query_ref, key_ref, value_ref, vectors_ref, lengths_ref, rows_ref, into_all, vectors_all, *rest):
+        into_refs = (query_ref, key_ref, value_ref)
+        bias_ref, live_ref = rest[:2]
+        vector_refs = rest[2 : 2 + len(vector_widths)]
+        scratch = rest[2 + len(vector_widths) :]
+        row_hold, into_hold, vector_hold, table_hold, hold_sem, send, receive, row_send, row_receive = scratch
         place = Place(grid)
         meet(place.neighbours())
+
+        def part(k):
+            return lambda ref, i: ref.at[i, :, pl.ds(k * width, width)]
+
         gather = Gather(
             place,
-            [
-                (into_ref, into_all, lambda ref, i: ref.at[:, i]),
-                (vectors_ref, vectors_all, lambda ref, i: ref.at[i]),
-            ],
+            [(into_refs[k], into_all, part(k)) for k in range(parts)]
+            + [(vectors_ref, vectors_all, lambda ref, i: ref.at[i])],
             send,
             receive,
         )
@@ -301,9 +304,23 @@
         for step in range(1, seqs):
             row_copy(step).start()
         me = place.index(0, 0)
-        through(into_ref, into_hold, into_all.at[:, me], hold_sem)
+        for k in range(parts):
+            through(into_refs[k], into_hold, part(k)(into_all, me), hold_sem)
         through(vectors_ref, vector_hold, vectors_all.at[me], hold_sem)
         through(tokens_ref.at[place.owner], row_hold, rows_ref.at[place.owner], hold_sem)
+
+        my_length = lengths_ref[place.owner]
+        for step in range(place.group):
+            member = lax.rem(place.member - step + place.group, place.group)
+            for source in range(seqs):
+                first = (source * place.group + member) * length
+                at = slice(step * rows + source * length, step * rows + (source + 1) * length)
+                here = lax.broadcasted_iota(jnp.int32, (length, 2 * HD), 0) + first
+                bias_ref[at, :] = jnp.where(here < my_length, 0.0, -1e30).astype(BF)
+                if step == 0:
+                    here = lax.broadcasted_iota(jnp.int32, (length, 1), 0) + first
+                    live_ref[at, :] = jnp.where(here < my_length, 1.0, 0.0).astype(F32)
+
         for step in range(1, place.chips):
             gather.from_chip(step)
             gather.from_columns(step - 1)
@@ -311,6 +328,16 @@
         for step in range(place.chips):
             gather.from_corner(step)
         gather.finish()
+        copy = pltpu.make_async_copy(vectors_all, table_hold, hold_sem)
+        copy.start()
+        copy.wait()
+        table = table_hold[...].astype(F32)
+        kind = lax.broadcasted_iota(jnp.int32, table.shape, 1)
+        source = lax.broadcasted_iota(jnp.int32, (devices, 1), 0).astype(F32)
+        for k, size in enumerate(vector_widths):
+            own = jnp.sum(jnp.where(kind == k, table, 0.0), axis=1).astype(BF)
+            apart = jnp.where(own_block(devices, size) == source, spread(own, size), 0.0)
+            vector_refs[k][...] = jnp.sum(apart, axis=0, keepdims=True)
         for step in range(1, seqs):
             landed = rows_ref.at[place.owner ^ step]
             remote(
@@ -318,23 +345,27 @@
             ).wait_recv()
             row_copy(step).wait_send()
 
-    shapes = [tokens.shape, (parts, devices, slim, width), (devices,) + vectors.shape]
+    vmem = pl.BlockSpec(memory_space=pltpu.VMEM)
+    shapes = [tokens.shape, (devices, slim, parts * width), (devices,) + tile]
     return pl.pallas_call(
         kernel,
-        in_specs=[HBM] * 3,
-        out_specs=[HBM] * 3,
-        out_shape=[jax.ShapeDtypeStruct(shape, BF) for shape in shapes],
+        in_specs=[HBM] * (parts + 2) + [pl.BlockSpec(memory_space=pltpu.SMEM)],
+        out_specs=[HBM] * 3 + [vmem] * (2 + len(vector_widths)),
+        out_shape=[jax.ShapeDtypeStruct(shape, BF) for shape in shapes]
+        + [jax.ShapeDtypeStruct((grid.group * rows, 2 * HD), BF), jax.ShapeDtypeStruct((rows, 1), F32)]
+        + [jax.ShapeDtypeStruct((1, devices * size), F32) for size in vector_widths],
         scratch_shapes=[
             pltpu.VMEM(tokens.shape[1:], BF),
-            pltpu.VMEM(into.shape, BF),
-            pltpu.VMEM(vectors.shape, BF),
+            pltpu.VMEM(into[0].shape, BF),
+            pltpu.VMEM(tile, BF),
+            pltpu.VMEM((devices,) + tile, BF),
             pltpu.SemaphoreType.DMA(()),
         ]
-        + gather_semaphores(grid, 2)
+        + gather_semaphores(grid, parts + 1)
         + [pltpu.SemaphoreType.DMA((seqs,)), pltpu.SemaphoreType.DMA((seqs,))],
         compiler_params=pltpu.CompilerParams(collective_id=0, has_side_effects=True),
         name="start_exchange",
-    )(tokens, into, vectors)
+    )(tokens, *into, vectors, lengths)
 
 
 class Reduce:
@@ -985,35 +1016,26 @@
         second_gain,
         second_shift,
     )
-    vector_row = jnp.concatenate(vectors + (up_bias,))
-    vector_size = vector_row.shape[0]
-    vector_rows = jnp.zeros((8, -(-vector_size // 128) * 128), BF).at[0, :vector_size].set(vector_row)
-    into_shard = jnp.stack([query_weight, key_weight, value_weight])
-    flat_in, into_full, vector_full = start_exchange(grid, tokens, into_shard, vector_rows)
+    vectors = vectors + (up_bias,)
+    lines = -(-len(vectors) // 16) * 16
+    tile = jnp.zeros((lines, 128), BF)
+    for i, vector in enumerate(vectors):
+        size = vector.shape[0]
+        tile = tile + jnp.pad(vector[None, :], ((i, lines - 1 - i), (0, 128 - size)))
+    flat_in, into_full, _, key_bias, live_rows, *whole_vectors = start_exchange(
+        grid,
+        tokens,
+        (query_weight, key_weight, value_weight),
+        tile,
+        lengths,
+        tuple(vector.shape[0] for vector in vectors),
+    )
     flat_in = flat_in.reshape(-1, width)
-    into_full = into_full.reshape(3, width, width)
-    vector_table = vector_full[:, 0, :vector_size]
-    small = vector_table[:, : 8 * slim].reshape(devices, 8, slim).transpose(1, 0, 2)
-    small = small.reshape(8, width).astype(F32)
-    query_add, value_add, out_add, down_add, gain_one, shift_one, gain_two, shift_two = (
-        small[i] for i in range(8)
-    )
-    up_add = vector_table[:, 8 * slim :].reshape(hidden).astype(F32)
-
-    positions = row_positions(grid, length)
-    my_length = take_block(lengths, grid.owner)
-    live_rows = (positions(grid.member) < my_length).astype(F32)[:, None]
-    key_bias = jnp.concatenate(
-        [
-            jnp.where(positions((grid.member - step) % grid.group) < my_length, 0.0, -1e30)
-            for step in range(grid.group)
-        ]
-    ).astype(F32)
-
-    key_bias = jnp.broadcast_to(key_bias[:, None], (key_bias.shape[0], 2 * HD)).astype(BF)
-    adds = (query_add, jnp.zeros_like(query_add), value_add)
-    inputs = [(matmul(flat_in, into_full[i]) + adds[i]).astype(BF) for i in range(3)]
-    inputs = jnp.concatenate(inputs, axis=1)
+    into_full = into_full.reshape(width, 3 * width)
+    query_add, value_add, out_add, down_add, gain_one, shift_one, gain_two, shift_two, up_add = whole_vectors
+
+    into_add = jnp.concatenate([query_add, jnp.zeros_like(query_add), value_add], axis=1)
+    inputs = (matmul(flat_in, into_full) + into_add).astype(BF)
     context, log_totals, out_full, up_full, down_full = attention(
         grid, inputs, key_bias, (out_weight, up_weight, down_weight)
     )
@@ -1027,7 +1049,9 @@
     first_norm, first_unit, first_factor = normalize(first_sum, gain_one, shift_one)
     first_low = first_norm.astype(BF)
     up_pre = matmul(first_low, up_full) + up_add
-    activated = jax.nn.gelu(up_pre, approximate=False).astype(BF)
+    below = 0.5 * (1.0 + lax.erf(up_pre * ROOT_HALF))
+    slope = (below + up_pre * INV_ROOT_TWO_PI * jnp.exp(-0.5 * up_pre * up_pre)).astype(BF)
+    activated, slope = lax.optimization_barrier(((up_pre * below).astype(BF), slope))
     second_sum = first_low.astype(F32) + matmul(activated, down_full) + down_add
     second_norm, second_unit, second_factor = normalize(second_sum, gain_two, shift_two)
     output = (second_norm * live_rows).astype(BF).reshape(seqs, length, width)
@@ -1039,7 +1063,7 @@
     grad_branch = grad_second.astype(BF)
     grad_down_add = jnp.sum(grad_branch.astype(F32), axis=0)
     grad_down = left_product(activated, grad_branch).astype(BF)
-    grad_up_low = (right_product(grad_branch, down_full) * gelu_slope(up_pre)).astype(BF)
+    grad_up_low = (right_product(grad_branch, down_full) * slope.astype(F32)).astype(BF)
     grad_up_add = jnp.sum(grad_up_low.astype(F32), axis=0)
     grad_up = left_product(first_low, grad_up_low).astype(BF)
     grad_first = right_product(grad_up_low, up_full) + grad_second
@@ -1074,9 +1098,7 @@
     )
     query_adds = jnp.sum(low[:, :width].astype(F32), axis=0)
     value_adds = jnp.sum(low[:, 2 * width :].astype(F32), axis=0)
-    tokens_grad = grad_residual
-    for i in range(3):
-        tokens_grad = tokens_grad + right_product(low[:, i * width : (i + 1) * width], into_full[i])
+    tokens_grad = right_product(low, into_full) + grad_residual
     wholes = [
         by_place(grid, left_product(flat_in, low).astype(BF), slim),
         by_place(grid, pack([query_adds, value_adds]), 8),

time: 464 us -> 418 us (0.901)
  matrix products: 117 us -> 93 us
  local copies, waits for them, and re-layouts: 42.3 us -> 24.7 us
  other arithmetic: 26.4 us -> 19.1 us
    dot_general x6 -> x4, matrix products: 57.3 us -> 37.1 us  [matmul(): return jnp.dot(left, right, preferred_element_type=F32)]
    concatenate x1, local copies, waits for them, and re-layouts: 6.1 us -> 0.01 us  [body(): jnp.concatenate([query_add, jnp.zeros_like(query_add), value_add], axis=1)]
    slice x3 -> x0, local copies, waits for them, and re-layouts: 5.95 us -> none  [the longest x1 2.56 us: body(): small[i]]
    dot_general x6 -> x4, matrix products: 34.7 us -> 29.4 us  [right_product(): lax.dot_general(left, right, (((1,), (1,)), ((), ())), preferred_element_...]
  transfers between devices with their start and end apart: 3 -> 3, of which waited for: 0 -> 0; matrix products, arithmetic and copies ran while one was open for 13% -> 9% of each run, Pallas kernels for 0% -> 0%
where the time goes in v5:
time: 418 us; the launch traced here: 413 us
  Pallas kernels  270 us (65%)
  matrix products  93 us (22%)
  local copies, waits for them, and re-layouts  24.7 us (6%)
  other arithmetic  19.1 us (5%)
  starting transfers between devices  4.9 us (1%)
    pallas_call x1, Pallas kernels, attention_back(): pl.pallas_call(kernel, grid=(pairs, blocks), in_specs=[tile(), resident((...  99.7 us
    pallas_call x1, Pallas kernels, attention(): pl.pallas_call(kernel, grid=(pairs, blocks), in_specs=[pl.BlockSpec((bloc...  73.7 us
    pallas_call x1, Pallas kernels, end_exchange(): pl.pallas_call(kernel, in_specs=[HBM] * (count + 1), out_specs=[HBM] + [p...  48.4 us
    pallas_call x1, Pallas kernels, start_exchange(): pl.pallas_call(kernel, in_specs=[HBM] * (parts + 2) + [pl.BlockSpec(memor...  47.6 us
    dot_general x4, matrix products, matmul(): return jnp.dot(left, right, preferred_element_type=F32)  37.1 us
    dot_general x4, matrix products, right_product(): lax.dot_general(left, right, (((1,), (1,)), ((), ())), preferred_element_...  29.4 us
    dot_general x4, matrix products, left_product(): lax.dot_general(left, right, (((0,), (0,)), ((), ())), preferred_element_...  26.5 us
  transfers between devices with their start and end apart: 3, of which 0 were waited for; matrix products, arithmetic and copies ran while one was open for 9% of the time, Pallas kernels for 0%

profile of v5, /device:TPU:0, one launch (start us, length us, event | category | flops | bytes accessed | tf_op | source)
XLA Modules:
  0.0 412.9 jit_solution(17184790966095890781)
XLA Ops:
  2.1 47.6 %start_exchange.1 = (bf16[4,256,768]{2,1,0:T(8,128)(2,1)}, bf16[32,24,2304]{2,1,0:T(8,128)(2,1)}, bf16[32,16,128]{2,1,0:T(8,128)(2,1)}, bf16[2048,128]{1,0:T(8,1...) custom-call(bf16[4,256,768]{2,1,0:T(8,128)(2,1)} %tokens_ref.1, ...), custom_call_target="tpu_custom_call" | custom-call | tf_op jit(solution)/shard_map/start_exchange/pallas_call | solution.py:350
  50.5 8.5 %add_convert_fusion.q_ref.k_ref.v_ref.all_ref = bf16[1024,2304]{1,0:T(8,128)(2,1)} fusion(bf16[1024,768]{1,0:T(8,128)(2,1)} %bitcast.110, bf16[768,2304]{1,0:T(8,128)(2,1)} %bitcast.108, f32[2304]{0:T(1024)S(1)} %fusion.10), kind=kOutput, calls=%fused_computation.8 | convolution fusion | flops 3628597248 | bytes 9839616 | tf_op jit(solution)/shard_map/dot_general | solution.py:19
  59.1 73.7 %attention.1 = (bf16[1024,768]{1,0:T(8,128)(2,1)S(1)}, f32[6,8,1024]{2,1,0:T(8,128)S(1)}, bf16[32,24,768]{2,1,0:T(8,128)(2,1)S(1)}, bf16[32,24,3072]{2,1,0:T(8,128)(2,1)}, bf16[32,96,768]{2,1,0:T(8,128)(2,1)}) custom-call(bf16[1024,2304]{1,0:T(8,128)(2,1)} %add_convert_fusion.q_ref.k_ref.v_ref.all_ref, bf16[2048,128]{1,0:T(8,128)(2,1)S(1)} %copy-done.1, ...), custom_call_target="tpu_custom_call" | custom-call | flops 25769803776 | bytes 6291456 | tf_op jit(solution)/shard_map/attention/pallas_call | solution.py:725
  134.8 2.5 dynamic-slice_bitcast_fusion
  137.7 4.5 %collective-permute-start.1 = (bf16[256,768]{1,0:T(8,128)(2,1)}, bf16[256,768]{1,0:T(8,128)(2,1)}, u32[]{:S(2)}, u32[]{:S(2)}) collective-permute-start(bf16[256,768]{1,0:T(8,128)(2,1)} %get-tuple-element.95), channel_id=1, source_target_pairs={{0,4},{1,5},{2,6},{3,7},{4,0},{5,1},{6,2},{7,3},{8,12},{9,13},{10,... | collective-permute-start | bytes 1179656 | tf_op jit(solution)/shard_map/ppermute | solution.py:89
  142.3 2.9 fusion.16
  147.6 15.2 %fusion.3 = (bf16[1024,3072]{1,0:T(8,128)(2,1)}, bf16[1024,3072]{1,0:T(8,128)(2,1)}) fusion(f32[3072]{0:T(1024)S(1)} %bitcast.113, bf16[768,3072]{1,0:T(8,128)(2,1)} %bitcast.114, f32[1024,768]{1,0:T(8,128)} %copy-done.8, f32[768]{0:T(1024)S(1)} %reduce.10, f32[768]{0:T(1024)S(1)} %reduce.9, f32[1024]{0:T(1024)S(1)} %add_rsqrt_fusion.1, ...), kind=kOutput, calls=%fused_computation.4 | convolution fusion | flops 4873519104 | bytes 20473856 | tf_op jit(solution)/shard_map/dot_general | solution.py:19
  163.0 10.4 %fusion.17 = (f32[1024]{0:T(1024)S(1)}, f32[1024,768]{1,0:T(8,128)}) fusion(f32[768]{0:T(1024)S(1)} %reduce.11, bf16[1024,3072]{1,0:T(8,128)(2,1)} %get-tuple-element.60, bf16[3072,768]{1,0:T(8,128)(2,1)} %bitcast.118, f32[768]{0:T(1024)S(1)} %reduce.10, f32[768]{0:T(1024)S(1)} %reduce.9, f32[1024]{0:T(1024)S(1)} %add_rsqrt_fusion.1, ...), kind=kOutput, calls=%fused_computation.85 | convolution fusion | flops 4838915072 | bytes 17323008 | tf_op jit(solution)/shard_map/dot_general | solution.py:19
  173.5 2.5 multiply_reduce_fusion.5
  176.0 1.8 bitcast_dynamic-update-slice_fusion.2
  181.4 4.2 %multiply_reduce_fusion = (bf16[768]{0:T(1024)(128)(2,1)S(1)}, f32[1024]{0:T(1024)S(1)}, bf16[1024,768]{1,0:T(8,128)(2,1)}) fusion(bf16[4,256,768]{2,1,0:T(8,128)(2,1)} %bitcast_dynamic-update-slice_fusion, f32[1024,768]{1,0:T(8,128)S(1)} %copy-done.7, f32[1024]{0:T(1024)S(1)} %reduce.12, f32[1024]{0:T(1024)S(1)} %add_rsqrt_fusion, ...), kind=kLoop, calls=%fused_computation.14 | loop fusion | flops 10221824 | bytes 6315520 | tf_op jit(solution)/shard_map/reduce_sum | solution.py:1060
  185.6 2.2 fusion.5
  187.8 2.6 convert_reduce_fusion.1
  190.5 9.1 %fusion.18 = (bf16[3072]{0:T(1024)(128)(2,1)S(1)}, bf16[1024,3072]{1,0:T(8,128)(2,1)}) fusion(bf16[1024,3072]{1,0:T(8,128)(2,1)} %get-tuple-element.66, bf16[3072,768]{1,0:T(8,128)(2,1)S(1)} %bitcast.121, f32[1024,768]{1,0:T(8,128)S(1)} %get-tuple-element.88), kind=kOutput, calls=%fused_computation.86 | convolution fusion | flops 4845204480 | bytes 20453376 | tf_op jit(solution)/shard_map/dot_general | solution.py:27
  199.6 8.3 %multiply_reduce_fusion.1 = (bf16[768]{0:T(1024)(128)(2,1)S(1)}, f32[1024]{0:T(1024)S(1)}, f32[1024]{0:T(1024)S(1)}, bf16[768]{0:T(1024)(128)(2,1)S(1)}, f32[1024,768]{1,0:T(8,128)S(1)}) fusion(f32[1024,768]{1,0:T(8,128)S(1)} %copy-done.9, f32[1024]{0:T(1024)S(1)} %add_rsqrt_fusion.1, f32[1024]{0:T(1024)S(1)} %broadcast_multiply_fusion.4, ...), kind=kOutput, calls=%fused_computation.15 | convolution fusion | flops 4839698432 | bytes 20469760 | tf_op jit(solution)/shard_map/dot_general | solution.py:27
  207.9 10.0 %convolution_convert_fusion.1 = bf16[768,3072]{1,0:T(8,128)(2,1)} fusion(bf16[1024,3072]{1,0:T(8,128)(2,1)} %get-tuple-element.115, f32[1024,768]{1,0:T(8,128)S(1)} %copy-done.9, f32[768]{0:T(1024)S(1)} %reduce.10, f32[768]{0:T(1024)S(1)} %reduce.9, f32[1024]{0:T(1024)S(1)} %add_rsqrt_fusion.1, f32[1024]{0:T(1024)S(1)} %broadcast_multiply_fusion.4), kind=kOutput, calls=%fused_computation.10 | convolution fusion | flops 4838129664 | bytes 14170112 | tf_op jit(solution)/shard_map/dot_general | solution.py:23
  217.9 9.8 %convolution_convert_fusion = bf16[3072,768]{1,0:T(8,128)(2,1)} fusion(bf16[1024,3072]{1,0:T(8,128)(2,1)} %get-tuple-element.60, f32[1024,768]{1,0:T(8,128)S(1)} %get-tuple-element.88), kind=kOutput, calls=%fused_computation.9 | convolution fusion | flops 4834983936 | bytes 14155776 | tf_op jit(solution)/shard_map/dot_general | solution.py:23
  229.0 2.6 convolution_convert_fusion.3.g_ref
  231.7 2.5 convolution_convert_fusion.4
  235.9 99.7 %attention_back.1 = (bf16[1024,2304]{1,0:T(8,128)(2,1)}, bf16[4,256,768]{2,1,0:T(8,128)(2,1)}, f32[24,3072]{1,0:T(8,128)}, f32[96,768]{1,0:T(8,128)}, f32[24,768]{1,0:T(8,128)}, /*index=5*/f32[8,256]{1,0:T(8,128)}) custom-call(bf16[1024,2304]{1,0:T(8,128)(2,1)} %add_convert_fusion.q_ref.k_ref.v_ref.all_ref, bf16[2048,128]{1,0:T(8,128)(2,1)} %get-tuple-element.51.bias_ref, ...), custom_call_target="tpu_custom_call" | custom-call | flops 64424509440 | bytes 9437184 | tf_op jit(solution)/shard_map/attention_back/pallas_call | solution.py:938
  335.6 9.4 %add_convert_fusion.1 = bf16[1024,768]{1,0:T(8,128)(2,1)} fusion(f32[1024,768]{1,0:T(8,128)} %copy-done.10, bf16[1024,2304]{1,0:T(8,128)(2,1)} %get-tuple-element.69, bf16[768,2304]{1,0:T(8,128)(2,1)} %bitcast.109), kind=kOutput, calls=%fused_computation.13 | convolution fusion | flops 3625451520 | bytes 12976128 | tf_op jit(solution)/shard_map/dot_general | solution.py:27
  345.1 4.2 %convolution_convert_fusion.2 = bf16[768,2304]{1,0:T(8,128)(2,1)S(1)} fusion(bf16[1024,768]{1,0:T(8,128)(2,1)S(1)} %bitcast.112, bf16[1024,2304]{1,0:T(8,128)(2,1)S(1)} %copy-done.11), kind=kOutput, calls=%fused_computation.11 | convolution fusion | flops 3625648128 | bytes 9830400 | tf_op jit(solution)/shard_map/dot_general | solution.py:23
  357.6 48.4 %end_exchange.1 = (bf16[4,256,768]{2,1,0:T(8,128)(2,1)S(1)}, f32[24,2304]{1,0:T(8,128)S(1)}, f32[8,128]{1,0:T(8,128)S(1)}) custom-call(bf16[4,256,768]{2,1,0:T(8,128)(2,1)S(1)} %bitcast.90, bf16[16,2,24,2304]{3,2,1,0:T(8,128)(2,1)S(1)} %bitcast.89, bf16[16,2,8,128]{3,2,1,0:T(8,128)(2,1)S(1)} %broadcast_in_dim.85.refs_1_), custom_call_target="tpu_custom_call" | custom-call | tf_op jit(solution)/shard_map/end_exchange/pallas_call | solution.py:589
  406.0 1.9 convert_element_type.136
  (124 shorter events, 26.4 us)
Async XLA Ops:
  50.5 8.6 %copy-start.1 = (bf16[2048,128]{1,0:T(8,128)(2,1)S(1)}, bf16[2048,128]{1,0:T(8,128)(2,1)}, u32[]{:S(2)}) copy-start(bf16[2048,128]{1,0:T(8,128)(2,1)} %get-tuple-element.51.bias_ref) | copy-start | bytes 1572868
  50.5 8.6 %copy-start.2 = (bf16[24,3072]{1,0:T(8,128)(2,1)S(1)}, bf16[24,3072]{1,0:T(8,128)(2,1)}, u32[]{:S(2)}) copy-start(bf16[24,3072]{1,0:T(8,128)(2,1)} %refs_1_.1) | copy-start | bytes 442372
  50.5 8.6 %copy-start.3 = (bf16[96,768]{1,0:T(8,128)(2,1)S(1)}, bf16[96,768]{1,0:T(8,128)(2,1)}, u32[]{:S(2)}) copy-start(bf16[96,768]{1,0:T(8,128)(2,1)} %refs_2_.1) | copy-start | bytes 442372
  50.5 8.6 %copy-start.4 = (bf16[24,768]{1,0:T(8,128)(2,1)S(1)}, bf16[24,768]{1,0:T(8,128)(2,1)}, u32[]{:S(2)}) copy-start(bf16[24,768]{1,0:T(8,128)(2,1)} %refs_0_.1) | copy-start | bytes 110596
  133.5 98.2 %copy-start.5 = (bf16[1024,768]{1,0:T(8,128)(2,1)}, bf16[1024,768]{1,0:T(8,128)(2,1)S(1)}, u32[]{:S(2)}) copy-start(bf16[1024,768]{1,0:T(8,128)(2,1)S(1)} %get-tuple-element.53.o_ref) | copy-start | bytes 4718596
  133.5 8.8 %copy-start.22 = (f32[1,768]{1,0:T(1,128)S(1)}, f32[1,768]{1,0:T(1,128)}, u32[]{:S(2)}) copy-start(f32[1,768]{1,0:T(1,128)} %get-tuple-element.55) | copy-start | bytes 9220
  137.4 38.6 %collective-permute-start = (bf16[256,768]{1,0:T(8,128)(2,1)}, bf16[256,768]{1,0:T(8,128)(2,1)}, u32[]{:S(2)}, u32[]{:S(2)}) collective-permute-start(bf16[256,768]{1,0:T(8,128)(2,1)} %get-tuple-element.96), channel_id=1, source_target_pairs={{0,2},{1,3},{2,0},{3,1},{4,6},{5,7},{6,4},{7,5},{8,10},{9,11},{10,... | collective-permute-start | bytes 1179656 | tf_op jit(solution)/shard_map/ppermute | solution.py:89
  137.7 40.0 %collective-permute-start.1 = (bf16[256,768]{1,0:T(8,128)(2,1)}, bf16[256,768]{1,0:T(8,128)(2,1)}, u32[]{:S(2)}, u32[]{:S(2)}) collective-permute-start(bf16[256,768]{1,0:T(8,128)(2,1)} %get-tuple-element.95), channel_id=1, source_target_pairs={{0,4},{1,5},{2,6},{3,7},{4,0},{5,1},{6,2},{7,3},{8,12},{9,13},{10,... | collective-permute-start | bytes 1179656 | tf_op jit(solution)/shard_map/ppermute | solution.py:89
  142.3 37.3 %collective-permute-start.2 = (bf16[256,768]{1,0:T(8,128)(2,1)}, bf16[256,768]{1,0:T(8,128)(2,1)}, u32[]{:S(2)}, u32[]{:S(2)}) collective-permute-start(bf16[256,768]{1,0:T(8,128)(2,1)} %get-tuple-element.94), channel_id=1, source_target_pairs={{0,6},{1,7},{2,4},{3,5},{4,2},{5,3},{6,0},{7,1},{8,14},{9,15},{10,... | collective-permute-start | bytes 1179656 | tf_op jit(solution)/shard_map/ppermute | solution.py:89
  147.5 15.2 %copy-start.13 = (f32[1024,1]{1,0:T(8,128)S(1)}, f32[1024,1]{1,0:T(8,128)}, u32[]{:S(2)}) copy-start(f32[1024,1]{1,0:T(8,128)} %get-tuple-element.64) | copy-start | bytes 12292
  163.0 10.4 %copy-start.18 = (f32[1,768]{1,0:T(1,128)S(1)}, f32[1,768]{1,0:T(1,128)}, u32[]{:S(2)}) copy-start(f32[1,768]{1,0:T(1,128)} %get-tuple-element.65) | copy-start | bytes 9220
  163.0 10.4 %copy-start.17 = (f32[1,768]{1,0:T(1,128)S(1)}, f32[1,768]{1,0:T(1,128)}, u32[]{:S(2)}) copy-start(f32[1,768]{1,0:T(1,128)} %get-tuple-element.67) | copy-start | bytes 9220
  173.5 7.9 %copy-start.7 = (f32[1024,768]{1,0:T(8,128)S(1)}, f32[1024,768]{1,0:T(8,128)}, u32[]{:S(2)}) copy-start(f32[1024,768]{1,0:T(8,128)} %get-tuple-element.112) | copy-start | bytes 9437188
  181.4 9.1 %slice-start.2 = ((s8[4718592]{0:T(1024)(128)(4,1)}), s8[4194304]{0:T(1024)(128)(4,1)S(1)}, s32[]{:S(2)}) async-start(s8[4718592]{0:T(1024)(128)(4,1)} %bitcast.119), calls=%async_computation.2 | async-start | bytes 8388608
  185.6 4.9 %slice-start.3 = ((s8[4718592]{0:T(1024)(128)(4,1)}), s8[524288]{0:T(1024)(128)(4,1)S(1)}, s32[]{:S(2)}) async-start(s8[4718592]{0:T(1024)(128)(4,1)} %bitcast.119), calls=%async_computation.3 | async-start | bytes 1048576
  187.8 11.8 %slice-start = ((s8[4718592]{0:T(1024)(128)(4,1)}), s8[4194304]{0:T(1024)(128)(4,1)S(1)}, s32[]{:S(2)}) async-start(s8[4718592]{0:T(1024)(128)(4,1)} %bitcast.115), calls=%async_computation | async-start | bytes 8388608
  190.5 9.1 %copy-start.9 = (f32[1024,768]{1,0:T(8,128)S(1)}, f32[1024,768]{1,0:T(8,128)}, u32[]{:S(2)}) copy-start(f32[1024,768]{1,0:T(8,128)} %copy-done.8) | copy-start | bytes 9437188
  190.5 9.1 %slice-start.1 = ((s8[4718592]{0:T(1024)(128)(4,1)}), s8[524288]{0:T(1024)(128)(4,1)S(1)}, s32[]{:S(2)}) async-start(s8[4718592]{0:T(1024)(128)(4,1)} %bitcast.115), calls=%async_computation.1 | async-start | bytes 1048576
  335.6 9.5 %copy-start.11 = (bf16[1024,2304]{1,0:T(8,128)(2,1)S(1)}, bf16[1024,2304]{1,0:T(8,128)(2,1)}, u32[]{:S(2)}) copy-start(bf16[1024,2304]{1,0:T(8,128)(2,1)} %get-tuple-element.69) | copy-start | bytes 14155780
  335.6 9.4 %copy-start.23 = (bf16[4,256,768]{2,1,0:T(8,128)(2,1)S(1)}, bf16[4,256,768]{2,1,0:T(8,128)(2,1)}, u32[]{:S(2)}) copy-start(bf16[4,256,768]{2,1,0:T(8,128)(2,1)} %get-tuple-element.47) | copy-start | bytes 4718596
  406.0 3.2 copy-start.12
  406.0 4.4 %copy-start.16 = (f32[24,768]{1,0:T(8,128)S(1)}, f32[24,768]{1,0:T(8,128)}, u32[]{:S(2)}) copy-start(f32[24,768]{1,0:T(8,128)} %get-tuple-element.140) | copy-start | bytes 221188
  406.0 5.0 %copy-start.15 = (f32[24,3072]{1,0:T(8,128)S(1)}, f32[24,3072]{1,0:T(8,128)}, u32[]{:S(2)}) copy-start(f32[24,3072]{1,0:T(8,128)} %get-tuple-element.141) | copy-start | bytes 884740
  408.0 3.8 copy-start.14
  (8 other events, 15.3 us)

commit v6 on v5

--- a/solution.py
+++ b/solution.py
@@ -41,18 +41,6 @@
         - jnp.mean(grad_unit, axis=-1, keepdims=True)
         - unit_rows * jnp.mean(grad_unit * unit_rows, axis=-1, keepdims=True)
     )
-
-
-def swap_index(place, step, count):
-    if count & (count - 1) == 0:
-        return place ^ step
-    return (place + step) % count
-
-
-def source_index(place, step, count):
-    if count & (count - 1) == 0:
-        return place ^ step
-    return (place - step) % count
 
 
 class Grid:
@@ -69,51 +57,6 @@
         self.owner = place // self.group
         self.member = place % self.group
 
-    def to_chip(self, array_in, step):
-        pairs = [(s, swap_index(s // 2, step, self.chips) * 2 + s % 2) for s in range(self.n)]
-        return lax.ppermute(array_in, "seq", pairs)
-
-    def to_column(self, array_in, step):
-        pairs = [(s, swap_index(s, step, self.columns)) for s in range(self.columns)]
-        return lax.ppermute(array_in, "dp", pairs)
-
-    def to_core(self, array_in):
-        return lax.ppermute(array_in, "seq", [(s, s ^ 1) for s in range(self.n)])
-
-    def to_owner(self, array_in, step, back=False):
-        move = source_index if back else swap_index
-        pairs = [
-            (s, move(s // self.group, step, self.seqs) * self.group + s % self.group)
-            for s in range(self.n)
-        ]
-        return lax.ppermute(array_in, "seq", pairs)
-
-    def to_member(self, array_in, step, back=False):
-        shift = -step if back else step
-        pairs = [
-            (s, (s // self.group) * self.group + (s % self.group + shift) % self.group)
-            for s in range(self.n)
-        ]
-        return lax.ppermute(array_in, "seq", pairs)
-
-
-def take_block(array_in, index):
-    return lax.dynamic_index_in_dim(array_in, index, 0, keepdims=False)
-
-
-def to_sequences(grid, array_in):
-    out = jnp.zeros_like(array_in)
-    out = lax.dynamic_update_index_in_dim(out, take_block(array_in, grid.owner), grid.owner, 0)
-    for step in range(1, grid.seqs):
-        place = swap_index(grid.owner, step, grid.seqs)
-        got = grid.to_owner(take_block(array_in, place), step)
-        out = lax.dynamic_update_index_in_dim(out, got, place, 0)
-    return out.reshape(-1, array_in.shape[2])
-
-
-def from_sequences(grid, rows, length):
-    return to_sequences(grid, rows.reshape(grid.seqs, length, rows.shape[1])).reshape(grid.seqs, length, -1)
-
 
 MESH = pl.DeviceIdType.MESH
 HBM = pl.BlockSpec(memory_space=pl.ANY)
@@ -197,9 +140,12 @@
                 self.begin(0, step, chip_step, place.beside(step), own=own, where=(0, chip_step))
         self.to_twin(0, chip_step, own=own)
 
+    def to_chip(self, step):
+        self.begin(0, 0, step, self.place.near(step), own=True, where=(0, 0))
+
     def start(self):
         for step in range(1, self.place.chips):
-            self.begin(0, 0, step, self.place.near(step), own=True, where=(0, 0))
+            self.to_chip(step)
         self.outward(0)
 
     def arrive(self, column_step, chip_step, other=False):
@@ -494,29 +440,37 @@
             return stages
         odd = list(range(1, chips, 2))
         even = list(range(2, chips, 2))
-
-        def many(moment, call, *steps):
-            for step in steps:
-                stages.append((moment, lambda step=step: call(*step)))
-
-        many(1, self.fold, (3,))
-        many(2, self.corner, *[(b,) for b in even + odd])
-        many(2, self.fold, (1,), (2,))
-        many(3, self.side, *[(1, b) for b in even], *[(2, b) for b in odd])
-        many(4, self.fold, (0,))
-        many(7, self.combine, *[(b,) for b in odd + even])
-        many(8, self.side, *[(1, b) for b in odd], *[(2, b) for b in even])
-        many(8, self.corner, (0,))
-        many(8, self.side, (1, 0))
-        for i, b in enumerate(odd):
-            moment = 11 + (2 * i * 2) // max(len(odd), 1)
-            many(moment, self.merge, (b,))
-            many(moment + 1, self.deep, (b,))
-        many(15, self.combine, (0,))
-        many(15, self.merge, *[(b,) for b in even])
-        many(16, self.side, (2, 0))
-        many(16, self.deep, *[(b,) for b in even])
-        many(20, self.merge, (0,))
+        first = [("corner", b) for b in even] + [(1, b) for b in even] + [(1, b) for b in odd] + [("corner", 0), (1, 0)]
+        second = [("corner", b) for b in odd] + [(2, b) for b in odd] + [(2, b) for b in even] + [(2, 0)]
+        slots = max(len(first), len(second))
+        pace = 14.4 / slots
+        mixed = [("fold", 3, 1.9), ("fold", 1, 3.9), ("fold", 2, 3.9), ("fold", 0, 6)]
+        corners, last_side = {}, {}
+        for link, orders in ((1, first), (2, second)):
+            for i, (kind, b) in enumerate(orders):
+                if kind == "corner":
+                    corners[b] = 2 + pace * i
+                    mixed.append(("corner", b, corners[b]))
+        for link, orders in ((1, first), (2, second)):
+            for i, (kind, b) in enumerate(orders):
+                if kind == "corner":
+                    continue
+                moment = 2 + pace * i
+                if link == 2 - b % 2:
+                    moment = max(moment, corners[b] + pace + 1.6)
+                    mixed.append(("combine", b, moment - 1))
+                mixed.append((("side", link), b, moment))
+                last_side[b] = max(last_side.get(b, 0), moment)
+        for b, moment in last_side.items():
+            mixed.append(("merge", b, moment + pace + 0.6))
+            if b:
+                mixed.append(("deep", b, moment + pace + 1.6))
+        mixed.sort(key=lambda item: item[2])
+        for kind, b, moment in mixed:
+            if isinstance(kind, tuple):
+                stages.append((moment, lambda a=kind[1], b=b: self.side(a, b)))
+            else:
+                stages.append((moment, lambda kind=kind, b=b: getattr(self, kind)(b)))
         return stages
 
 
@@ -619,7 +573,7 @@
     return (lane // HD) == half, lane == HD * (1 - half)
 
 
-def attention(grid, inputs, key_bias, shards, block=256):
+def attention(grid, inputs, key_bias, shards, rows_in, block=256):
     rows = inputs.shape[0]
     width = inputs.shape[1] // 3
     pairs = width // (2 * HD)
@@ -630,12 +584,13 @@
     devices = grid.columns * grid.n
     late = len(shards)
 
-    def kernel(q_ref, bias_ref, k_ref, v_ref, all_ref, *refs):
+    def kernel(bias_ref, own_ref, all_ref, rows_ref, *refs):
         shard_refs = refs[:late]
-        o_ref, l_ref = refs[late : late + 2]
-        whole_refs = refs[late + 2 : 2 * late + 2]
-        k_own, v_own, far, hold_sem, send, receive, far_send, far_receive = refs[2 * late + 2 : 2 * late + 10]
-        holds = refs[2 * late + 10 :]
+        o_ref, l_ref, block_ref = refs[late : late + 3]
+        whole_refs = refs[late + 3 : 2 * late + 3]
+        rest = refs[2 * late + 3 :]
+        k_own, v_own, far, hold_sem, send, receive, far_send, far_receive, row_send, row_receive = rest[:10]
+        holds = rest[10:]
         pair, turn = pl.program_id(0), pl.program_id(1)
         now = pair * blocks + turn
         place = Place(grid)
@@ -646,6 +601,9 @@
             receive,
         )
 
+        def part(kind):
+            return own_ref[:, pl.ds(pl.multiple_of(kind * width + pair * 2 * HD, 2 * HD), 2 * HD)]
+
         def far_copy(step, which, kind):
             first = pl.multiple_of(which * 2 * HD + (kind + 1) * width, 2 * HD)
             return remote(
@@ -658,32 +616,65 @@
 
         def first_step():
             meet(place.neighbours() + [place.at_member(s) for s in range(1, count) if count > 2])
-            for which in range(pairs):
-                for step in range(1, count):
-                    for kind in range(2):
-                        far_copy(step, which, kind).start()
+            start_far(0)
             gather.start()
-            me = place.index(0, 0)
-            for shard, whole, hold in zip(shard_refs, whole_refs, holds):
-                through(shard, hold, whole.at[me], hold_sem)
-
-        plan = [(0.0, first_step)]
-        for step in range(1, place.chips):
-            plan.append((step * 0.66 / (place.chips - 1), lambda step=step: gather.from_chip(step)))
-            plan.append((0.1 + step * 0.66 / (place.chips - 1), lambda step=step: gather.from_columns(step - 1)))
+            for k in range(late + 1):
+                own_copy(k, 0).start()
+            for which in range(1, pairs):
+                start_far(which)
+
+        def start_far(which):
+            for step in range(1, count):
+                for kind in range(2):
+                    far_copy(step, which, kind).start()
+
+        start_rows, finish_rows = row_exchange(place, rows_ref, block_ref, row_send, row_receive)
+
+        def own_copy(k, way):
+            if k == late:
+                source, target = rows_ref.at[place.owner], block_ref.at[place.owner]
+            else:
+                source, target = shard_refs[k], whole_refs[k].at[place.index(0, 0)]
+            if way == 0:
+                return pltpu.make_async_copy(source, holds[k], hold_sem.at[k, 0])
+            return pltpu.make_async_copy(holds[k], target, hold_sem.at[k, 1])
+
+        def own_onward():
+            for k in range(late + 1):
+                own_copy(k, 0).wait()
+                own_copy(k, 1).start()
+
+        chips = place.chips
+        pace = 8 / max(chips - 2, 1)
+        plan = [(0, first_step), (1, own_onward), (8, lambda: gather.from_chip(1)), (8, lambda: gather.from_columns(0))]
+        plan.append((10, start_rows))
+        for step in range(2, chips):
+            moment = 12 + pace * (step - 2)
+            plan.append((moment - 0.01 * (step > 2), lambda step=step: gather.from_chip(step)))
+            plan.append((moment, lambda step=step: gather.from_columns(step - 1)))
+        plan.append((20, lambda: gather.from_columns(chips - 1)))
+        moments = {}
+        for moment, action in plan:
+            moments.setdefault(min(int(moment * steps / 24), steps - 1), []).append(action)
 
         def last_step():
-            gather.from_columns(place.chips - 1)
-            for step in range(place.chips):
+            for step in range(chips):
                 gather.from_corner(step)
             gather.finish()
+            for k in range(late + 1):
+                own_copy(k, 1).wait()
+            finish_rows()
             for step in range(1, count):
                 for which in range(pairs):
                     for kind in range(2):
                         far_copy(step, which, kind).wait_send()
 
-        for moment, action in plan:
-            pl.when(now == int(moment * steps))(action)
+        for moment, group in sorted(moments.items()):
+
+            @pl.when(now == moment)
+            def _(group=group):
+                for action in group:
+                    action()
 
         @pl.when(turn == 0)
         def _():
@@ -695,12 +686,14 @@
                 zero = jnp.zeros((rows, 2 * HD), BF)
                 for i in range(count):
                     at = slice(i * rows, (i + 1) * rows)
-                    key = k_ref[...] if i == 0 else far[i - 1, 0, pair]
-                    value = v_ref[...] if i == 0 else far[i - 1, 1, pair]
+                    key = part(1) if i == 0 else far[i - 1, 0, pair]
+                    value = part(2) if i == 0 else far[i - 1, 1, pair]
                     k_own[half, at, :] = jnp.where(own, key, jnp.where(spare, bias_ref[at, :], zero))
                     v_own[half, at, :] = jnp.where(own, value, jnp.where(spare, zero + 1, zero))
 
-        query = q_ref[...]
+        at = pl.ds(pl.multiple_of(turn * block, block), block)
+        lanes = pl.ds(pl.multiple_of(pair * 2 * HD, 2 * HD), 2 * HD)
+        query = own_ref[at, lanes]
         results = []
         for half in range(2):
             own, spare = own_lanes(half, block)
@@ -713,45 +706,48 @@
             totals = summed[:, HD * (1 - half) : HD * (1 - half) + 1]
             results.append(summed / totals)
             log_total = jnp.broadcast_to(largest * SCALE + jnp.log2(totals), (block, 2 * HD))
-            l_ref[half : half + 1, :] = jnp.transpose(log_total)[0:1, :]
+            l_ref[pair, half : half + 1, at] = jnp.transpose(log_total)[0:1, :]
         lane = lax.broadcasted_iota(jnp.int32, (block, 2 * HD), 1)
-        o_ref[...] = jnp.where(lane < HD, results[0], results[1]).astype(BF)
+        o_ref[at, lanes] = jnp.where(lane < HD, results[0], results[1]).astype(BF)
         pl.when(now == steps - 1)(last_step)
 
-    def column(first):
-        return pl.BlockSpec((rows, 2 * HD), lambda i, j: (0, i + first))
+    def resident(shape):
+        return pl.BlockSpec(shape, lambda i, j: (0,) * len(shape))
 
     far_sems = pltpu.SemaphoreType.DMA((max(count - 1, 1), 2, pairs))
     return pl.pallas_call(
         kernel,
         grid=(pairs, blocks),
         in_specs=[
-            pl.BlockSpec((block, 2 * HD), lambda i, j: (j, i)),
-            pl.BlockSpec((keys, 2 * HD), lambda i, j: (0, 0)),
-            column(pairs),
-            column(2 * pairs),
+            resident((keys, 2 * HD)),
+            resident(inputs.shape),
+            HBM,
             HBM,
         ]
         + [HBM] * late,
         out_specs=[
-            pl.BlockSpec((block, 2 * HD), lambda i, j: (j, i)),
-            pl.BlockSpec((None, 8, block), lambda i, j: (i, 0, j)),
+            resident((rows, width)),
+            resident((pairs, 8, rows)),
+            HBM,
         ]
         + [HBM] * late,
         out_shape=[
             jax.ShapeDtypeStruct((rows, width), BF),
             jax.ShapeDtypeStruct((pairs, 8, rows), F32),
+            jax.ShapeDtypeStruct(rows_in.shape, BF),
         ]
         + [jax.ShapeDtypeStruct((devices,) + shard.shape, BF) for shard in shards],
         scratch_shapes=[
             pltpu.VMEM((2, keys, 2 * HD), BF),
             pltpu.VMEM((2, keys, 2 * HD), BF),
             pltpu.VMEM((max(count - 1, 1), 2, pairs, rows, 2 * HD), BF),
-            pltpu.SemaphoreType.DMA(()),
+            pltpu.SemaphoreType.DMA((late + 1, 2)),
         ]
         + gather_semaphores(grid, late)
         + [far_sems, far_sems]
-        + [pltpu.VMEM(shard.shape, BF) for shard in shards],
+        + [pltpu.SemaphoreType.DMA((grid.seqs,))] * 2
+        + [pltpu.VMEM(shard.shape, BF) for shard in shards]
+        + [pltpu.VMEM(rows_in.shape[1:], BF)],
         compiler_params=pltpu.CompilerParams(
             collective_id=1, has_side_effects=True, vmem_limit_bytes=48 << 20
         ),
@@ -759,7 +755,7 @@
             flops=16 * H * rows * keys * HD, bytes_accessed=8 * rows * width, transcendentals=H * rows * keys
         ),
         name="attention",
-    )(inputs, key_bias, inputs, inputs, inputs, *shards)
+    )(key_bias, inputs, inputs, rows_in, *shards)
 
 
 def attention_back(grid, inputs, key_bias, log_totals, context, grad_context, wholes, rows_out, block=256, chunk=1024):
@@ -824,19 +820,30 @@
 
         def first_step():
             meet(place.neighbours() + [place.at_member(s) for s in range(1, count) if count > 2])
-            for which in range(pairs):
-                for step in range(1, count):
-                    for kind in range(2):
-                        far_copy(step, which, kind).start()
-
-        actions = [(0, first_step)] + reduce.plan()
-        actions.append((0, start_rows))
-        actions.append(
-            (1, lambda: through(rows_ref.at[place.owner], row_hold, back_ref.at[place.owner], hold_sem))
-        )
+            start_far(0)
+
+        def start_far(which):
+            for step in range(1, count):
+                for kind in range(2):
+                    far_copy(step, which, kind).start()
+
+        def more_far():
+            start_rows()
+            own_in.start()
+            for which in range(1, pairs):
+                start_far(which)
+
+        def own_onward():
+            own_in.wait()
+            own_out.start()
+
+        own_in = pltpu.make_async_copy(rows_ref.at[place.owner], row_hold, hold_sem.at[0])
+        own_out = pltpu.make_async_copy(row_hold, back_ref.at[place.owner], hold_sem.at[1])
+        stages = reduce.plan()
+        actions = [(0, first_step), stages[0], (0, more_far), (1, own_onward)] + stages[1:]
         moments = {}
         for moment, action in actions:
-            moments.setdefault(moment * steps // 24, []).append(action)
+            moments.setdefault(min(int(moment * steps / 24), steps - 1), []).append(action)
         for moment, group in sorted(moments.items()):
 
             @pl.when(now == moment)
@@ -914,9 +921,10 @@
 
         @pl.when(now == steps - 1)
         def _():
+            send_back(pairs - 1)
             reduce.finish()
-            send_back(pairs - 1)
             finish_rows()
+            own_out.wait()
             take_back(pairs - 1)
             for step in range(1, count):
                 for which in range(pairs):
@@ -963,7 +971,7 @@
             far_buffer,
             far_buffer,
             pltpu.VMEM(rows_out.shape[1:], BF),
-            pltpu.SemaphoreType.DMA(()),
+            pltpu.SemaphoreType.DMA((2,)),
         ]
         + [far_sems] * 4
         + [pltpu.SemaphoreType.DMA((grid.seqs,))] * 2
@@ -1036,14 +1044,13 @@
 
     into_add = jnp.concatenate([query_add, jnp.zeros_like(query_add), value_add], axis=1)
     inputs = (matmul(flat_in, into_full) + into_add).astype(BF)
-    context, log_totals, out_full, up_full, down_full = attention(
-        grid, inputs, key_bias, (out_weight, up_weight, down_weight)
+    context, log_totals, grad_in, out_full, up_full, down_full = attention(
+        grid, inputs, key_bias, (out_weight, up_weight, down_weight), cotangent
     )
     out_full = out_full.reshape(width, width)
     up_full = up_full.reshape(width, hidden)
     down_full = down_full.reshape(hidden, width)
-    cotangent = lax.optimization_barrier((cotangent, context))[0]
-    grad_in = to_sequences(grid, cotangent)
+    grad_in = grad_in.reshape(-1, width)
 
     first_sum = flat_in.astype(F32) + matmul(context, out_full) + out_add
     first_norm, first_unit, first_factor = normalize(first_sum, gain_one, shift_one)

time: 418 us -> 402 us (0.962)
  local copies, waits for them, and re-layouts: 24.7 us -> 15 us
  starting transfers between devices: 4.9 us -> 0 us
    dynamic_update_slice x3 -> x0, local copies, waits for them, and re-layouts: 5.34 us -> none  [to_sequences(): out = lax.dynamic_update_index_in_dim(out, got, place, 0)]
    ppermute x3 -> x0, starting transfers between devices: 4.9 us -> none  [to_owner(): return lax.ppermute(array_in, 'seq', pairs)]
  transfers between devices with their start and end apart: 3 -> 0, of which waited for: 0 -> 0; matrix products, arithmetic and copies ran while one was open for 9% -> 0% of each run, Pallas kernels for 0% -> 0%
where the time goes in v6:
time: 402 us; the launch traced here: 397 us
  Pallas kernels  266 us (66%)
  matrix products  93.1 us (23%)
  other arithmetic  20.9 us (5%)
  local copies, waits for them, and re-layouts  15 us (4%)
    pallas_call x1, Pallas kernels, attention_back(): pl.pallas_call(kernel, grid=(pairs, blocks), in_specs=[tile(), resident((...  96.7 us
    pallas_call x1, Pallas kernels, attention(): pl.pallas_call(kernel, grid=(pairs, blocks), in_specs=[resident((keys, 2...  73.2 us
    pallas_call x1, Pallas kernels, end_exchange(): pl.pallas_call(kernel, in_specs=[HBM] * (count + 1), out_specs=[HBM] + [p...  48.6 us
    pallas_call x1, Pallas kernels, start_exchange(): pl.pallas_call(kernel, in_specs=[HBM] * (parts + 2) + [pl.BlockSpec(memor...  47.6 us
    dot_general x4, matrix products, matmul(): return jnp.dot(left, right, preferred_element_type=F32)  39.8 us
    dot_general x4, matrix products, right_product(): lax.dot_general(left, right, (((1,), (1,)), ((), ())), preferred_element_...  28.7 us
    dot_general x4, matrix products, left_product(): lax.dot_general(left, right, (((0,), (0,)), ((), ())), preferred_element_...  24.6 us

profile of v6, /device:TPU:0, one launch (start us, length us, event | category | flops | bytes accessed | tf_op | source)
XLA Modules:
  0.0 396.5 jit_solution(13748487799387424640)
XLA Ops:
  2.1 47.6 %start_exchange.1 = (bf16[4,256,768]{2,1,0:T(8,128)(2,1)}, bf16[32,24,2304]{2,1,0:T(8,128)(2,1)}, bf16[32,16,128]{2,1,0:T(8,128)(2,1)}, bf16[2048,128]{1,0:T(8,1...) custom-call(bf16[4,256,768]{2,1,0:T(8,128)(2,1)} %tokens_ref.1, ...), custom_call_target="tpu_custom_call" | custom-call | tf_op jit(solution)/shard_map/start_exchange/pallas_call | solution.py:296
  50.5 8.5 %add_convert_fusion.own_ref.all_ref.q_ref.k_ref.v_ref = bf16[1024,2304]{1,0:T(8,128)(2,1)} fusion(bf16[1024,768]{1,0:T(8,128)(2,1)} %bitcast.98, bf16[768,2304]{1,0:T(8,128)(2,1)} %bitcast.96, f32[2304]{0:T(1024)S(1)} %fusion.10), kind=kOutput, calls=%fused_computation.8 | convolution fusion | flops 3628597248 | bytes 9839616 | tf_op jit(solution)/shard_map/dot_general | solution.py:19
  59.0 73.2 %attention.1 = (bf16[1024,768]{1,0:T(8,128)(2,1)S(1)}, f32[6,8,1024]{2,1,0:T(8,128)S(1)}, bf16[4,256,768]{2,1,0:T(8,128)(2,1)S(1)}, bf16[32,24,768]{2,1,0:T(8,12...) custom-call(bf16[2048,128]{1,0:T(8,128)(2,1)S(1)} %copy-done.1, ...), custom_call_target="tpu_custom_call" | custom-call | flops 25769803776 | bytes 6291456 | tf_op jit(solution)/shard_map/attention/pallas_call | solution.py:718
  134.0 5.0 %fusion.16 = (f32[1024]{0:T(1024)S(1)}, f32[1024,768]{1,0:T(8,128)}) fusion(f32[768]{0:T(1024)S(1)} %reduce.8, bf16[1024,768]{1,0:T(8,128)(2,1)} %copy-done.5, bf16[768,768]{1,0:T(8,128)(2,1)S(1)} %bitcast.79, bf16[1024,768]{1,0:T(8,128)(2,1)} %bitcast.99), kind=kOutput, calls=%fused_computation.77 | convolution fusion | flops 1211104256 | bytes 7478272 | tf_op jit(solution)/shard_map/dot_general | solution.py:19
  139.0 2.4 multiply_reduce_fusion.6
  141.5 14.6 %fusion.3 = (bf16[1024,3072]{1,0:T(8,128)(2,1)}, bf16[1024,3072]{1,0:T(8,128)(2,1)S(1)}) fusion(f32[3072]{0:T(1024)S(1)} %bitcast.101, bf16[768,3072]{1,0:T(8,128)(2,1)} %bitcast.102, f32[1024,768]{1,0:T(8,128)} %get-tuple-element.106, f32[768]{0:T(1024)S(1)} %reduce.10, f32[768]{0:T(1024)S(1)} %reduce.9, f32[1024]{0:T(1024)S(1)} %add_rsqrt_fusion.1, ...), kind=kOutput, calls=%fused_computation.4 | convolution fusion | flops 4873519104 | bytes 20473856 | tf_op jit(solution)/shard_map/dot_general | solution.py:19
  156.2 11.7 %fusion.17 = (f32[1024]{0:T(1024)S(1)}, f32[1024,768]{1,0:T(8,128)}) fusion(f32[768]{0:T(1024)S(1)} %reduce.11, bf16[1024,3072]{1,0:T(8,128)(2,1)S(1)} %get-tuple-element.60, bf16[3072,768]{1,0:T(8,128)(2,1)} %bitcast.106, f32[768]{0:T(1024)S(1)} %reduce.10, f32[768]{0:T(1024)S(1)} %reduce.9, f32[1024]{0:T(1024)S(1)} %add_rsqrt_fusion.1, ...), kind=kOutput, calls=%fused_computation.78 | convolution fusion | flops 4838915072 | bytes 17323008 | tf_op jit(solution)/shard_map/dot_general | solution.py:19
  168.1 2.4 multiply_reduce_fusion.5
  170.5 4.3 %multiply_reduce_fusion = (bf16[768]{0:T(1024)(128)(2,1)S(1)}, f32[1024]{0:T(1024)S(1)}, bf16[1024,768]{1,0:T(8,128)(2,1)}) fusion(bf16[4,256,768]{2,1,0:T(8,128)(2,1)S(1)} %get-tuple-element.63, f32[1024,768]{1,0:T(8,128)} %get-tuple-element.108, f32[1024]{0:T(1024)S(1)} %reduce.12, f32[1024]{0:T(1024)S(1)} %add_rsqrt_fusion, ...), kind=kLoop, calls=%fused_computation.14 | loop fusion | flops 10221824 | bytes 6315520 | tf_op jit(solution)/shard_map/reduce_sum | solution.py:1067
  175.7 2.9 convert_reduce_fusion.1
  178.6 8.7 %fusion.18 = (bf16[3072]{0:T(1024)(128)(2,1)S(1)}, bf16[1024,3072]{1,0:T(8,128)(2,1)S(1)}) fusion(bf16[1024,3072]{1,0:T(8,128)(2,1)} %get-tuple-element.66, bf16[3072,768]{1,0:T(8,128)(2,1)} %bitcast.107, f32[1024,768]{1,0:T(8,128)S(1)} %get-tuple-element.88), kind=kOutput, calls=%fused_computation.79 | convolution fusion | flops 4845204480 | bytes 20453376 | tf_op jit(solution)/shard_map/dot_general | solution.py:27
  187.3 7.9 %multiply_reduce_fusion.1 = (bf16[768]{0:T(1024)(128)(2,1)S(1)}, f32[1024]{0:T(1024)S(1)}, f32[1024]{0:T(1024)S(1)}, bf16[768]{0:T(1024)(128)(2,1)S(1)}, f32[1024,768]{1,0:T(8,128)S(1)}) fusion(f32[1024,768]{1,0:T(8,128)} %get-tuple-element.106, f32[1024]{0:T(1024)S(1)} %add_rsqrt_fusion.1, f32[1024]{0:T(1024)S(1)} %broadcast_multiply_fusion.4, ...), kind=kOutput, calls=%fused_computation.15 | convolution fusion | flops 4839698432 | bytes 20469760 | tf_op jit(solution)/shard_map/dot_general | solution.py:27
  195.3 2.5 convert_reduce_fusion
  197.8 2.6 convolution_convert_fusion.3.g_ref
  200.4 10.7 %convolution_convert_fusion.1 = bf16[768,3072]{1,0:T(8,128)(2,1)} fusion(bf16[1024,3072]{1,0:T(8,128)(2,1)S(1)} %get-tuple-element.111, f32[1024,768]{1,0:T(8,128)} %get-tuple-element.106, f32[768]{0:T(1024)S(1)} %reduce.10, f32[768]{0:T(1024)S(1)} %reduce.9, f32[1024]{0:T(1024)S(1)} %add_rsqrt_fusion.1, f32[1024]{0:T(1024)S(1)} %broadcast_multiply_fusion.4), kind=kOutput, calls=%fused_computation.10 | convolution fusion | flops 4838129664 | bytes 14170112 | tf_op jit(solution)/shard_map/dot_general | solution.py:23
  211.1 7.0 %convolution_convert_fusion = bf16[3072,768]{1,0:T(8,128)(2,1)} fusion(bf16[1024,3072]{1,0:T(8,128)(2,1)S(1)} %bitcast.112, f32[1024,768]{1,0:T(8,128)S(1)} %get-tuple-element.88), kind=kOutput, calls=%fused_computation.9 | convolution fusion | flops 4834983936 | bytes 14155776 | tf_op jit(solution)/shard_map/dot_general | solution.py:23
  218.2 2.5 convolution_convert_fusion.4
  222.4 96.7 %attention_back.1 = (bf16[1024,2304]{1,0:T(8,128)(2,1)}, bf16[4,256,768]{2,1,0:T(8,128)(2,1)}, f32[24,3072]{1,0:T(8,128)}, f32[96,768]{1,0:T(8,128)}, f32[24,768]{1,0:T(8,128)}, /*index=5*/f32[8,256]{1,0:T(8,128)}) custom-call(bf16[1024,2304]{1,0:T(8,128)(2,1)} %add_convert_fusion.own_ref.all_ref.q_ref.k_ref.v_ref, ...), custom_call_target="tpu_custom_call" | custom-call | flops 64424509440 | bytes 9437184 | tf_op jit(solution)/shard_map/attention_back/pallas_call | solution.py:946
  319.1 9.4 %add_convert_fusion.1 = bf16[1024,768]{1,0:T(8,128)(2,1)} fusion(f32[1024,768]{1,0:T(8,128)} %copy-done.8, bf16[1024,2304]{1,0:T(8,128)(2,1)} %get-tuple-element.69, bf16[768,2304]{1,0:T(8,128)(2,1)} %bitcast.97), kind=kOutput, calls=%fused_computation.13 | convolution fusion | flops 3625451520 | bytes 12976128 | tf_op jit(solution)/shard_map/dot_general | solution.py:27
  328.5 4.4 %convolution_convert_fusion.2 = bf16[768,2304]{1,0:T(8,128)(2,1)S(1)} fusion(bf16[1024,768]{1,0:T(8,128)(2,1)S(1)} %bitcast.100, bf16[1024,2304]{1,0:T(8,128)(2,1)S(1)} %copy-done.9), kind=kOutput, calls=%fused_computation.11 | convolution fusion | flops 3625648128 | bytes 9830400 | tf_op jit(solution)/shard_map/dot_general | solution.py:23
  337.1 1.4 copy-done
  338.5 48.6 %end_exchange.1 = (bf16[4,256,768]{2,1,0:T(8,128)(2,1)S(1)}, f32[24,2304]{1,0:T(8,128)S(1)}, f32[8,128]{1,0:T(8,128)S(1)}) custom-call(bf16[4,256,768]{2,1,0:T(8,128)(2,1)S(1)} %bitcast.78, bf16[16,2,24,2304]{3,2,1,0:T(8,128)(2,1)S(1)} %bitcast.77, bf16[16,2,8,128]{3,2,1,0:T(8,128)(2,1)S(1)} %broadcast_in_dim.67.refs_1_), custom_call_target="tpu_custom_call" | custom-call | tf_op jit(solution)/shard_map/end_exchange/pallas_call | solution.py:543
  387.1 1.9 convert_element_type.136
  390.3 1.5 slice_bitcast_fusion
  (111 shorter events, 16.6 us)
Async XLA Ops:
  50.4 8.5 %copy-start.1 = (bf16[2048,128]{1,0:T(8,128)(2,1)S(1)}, bf16[2048,128]{1,0:T(8,128)(2,1)}, u32[]{:S(2)}) copy-start(bf16[2048,128]{1,0:T(8,128)(2,1)} %get-tuple-element.51.bias_ref) | copy-start | bytes 1572868
  50.4 8.5 %copy-start.2 = (bf16[24,3072]{1,0:T(8,128)(2,1)S(1)}, bf16[24,3072]{1,0:T(8,128)(2,1)}, u32[]{:S(2)}) copy-start(bf16[24,3072]{1,0:T(8,128)(2,1)} %refs_1_.1) | copy-start | bytes 442372
  50.4 8.5 %copy-start.3 = (bf16[96,768]{1,0:T(8,128)(2,1)S(1)}, bf16[96,768]{1,0:T(8,128)(2,1)}, u32[]{:S(2)}) copy-start(bf16[96,768]{1,0:T(8,128)(2,1)} %refs_2_.1) | copy-start | bytes 442372
  50.5 8.5 %copy-start.4 = (bf16[24,768]{1,0:T(8,128)(2,1)S(1)}, bf16[24,768]{1,0:T(8,128)(2,1)}, u32[]{:S(2)}) copy-start(bf16[24,768]{1,0:T(8,128)(2,1)} %refs_0_.1) | copy-start | bytes 110596
  59.0 75.0 %copy-start.20 = (f32[1,768]{1,0:T(1,128)S(1)}, f32[1,768]{1,0:T(1,128)}, u32[]{:S(2)}) copy-start(f32[1,768]{1,0:T(1,128)} %get-tuple-element.55) | copy-start | bytes 9220
  139.0 2.4 copy-start.18
  139.0 2.5 copy-start.17
  139.0 2.5 copy-start.22
  156.2 11.7 %copy-start.23 = (bf16[1024,3072]{1,0:T(8,128)(2,1)}, bf16[1024,3072]{1,0:T(8,128)(2,1)S(1)}, u32[]{:S(2)}) copy-start(bf16[1024,3072]{1,0:T(8,128)(2,1)S(1)} %get-tuple-element.60) | copy-start | bytes 18874372
  156.2 11.7 %copy-start.11 = (f32[1024,1]{1,0:T(8,128)S(1)}, f32[1024,1]{1,0:T(8,128)}, u32[]{:S(2)}) copy-start(f32[1024,1]{1,0:T(8,128)} %get-tuple-element.64) | copy-start | bytes 12292
  167.9 2.6 copy-start.16
  167.9 2.6 copy-start.15
  175.7 11.6 %slice-start = ((s8[4718592]{0:T(1024)(128)(4,1)}), s8[4194304]{0:T(1024)(128)(4,1)S(1)}, s32[]{:S(2)}) async-start(s8[4718592]{0:T(1024)(128)(4,1)} %bitcast.103), calls=%async_computation | async-start | bytes 8388608
  178.6 8.8 %slice-start.1 = ((s8[4718592]{0:T(1024)(128)(4,1)}), s8[524288]{0:T(1024)(128)(4,1)S(1)}, s32[]{:S(2)}) async-start(s8[4718592]{0:T(1024)(128)(4,1)} %bitcast.103), calls=%async_computation.1 | async-start | bytes 1048576
  197.8 20.3 %copy-start.8 = (f32[1024,768]{1,0:T(8,128)}, f32[1024,768]{1,0:T(8,128)S(1)}, u32[]{:S(2)}) copy-start(f32[1024,768]{1,0:T(8,128)S(1)} %get-tuple-element.90) | copy-start | bytes 9437188
  197.8 13.3 %slice-start.2 = ((s8[6291456]{0:T(1024)(128)(4,1)}), s8[4194304]{0:T(1024)(128)(4,1)S(1)}, s32[]{:S(2)}) async-start(s8[6291456]{0:T(1024)(128)(4,1)} %bitcast.111), calls=%async_computation.2 | async-start | bytes 8388608
  200.4 10.7 %slice-start.3 = ((s8[6291456]{0:T(1024)(128)(4,1)}), s8[2097152]{0:T(1024)(128)(4,1)S(1)}, s32[]{:S(2)}) async-start(s8[6291456]{0:T(1024)(128)(4,1)} %bitcast.111), calls=%async_computation.3 | async-start | bytes 4194304
  211.1 7.0 %copy-start.6 = (bf16[1024,768]{1,0:T(8,128)(2,1)S(1)}, bf16[1024,768]{1,0:T(8,128)(2,1)}, u32[]{:S(2)}) copy-start(bf16[1024,768]{1,0:T(8,128)(2,1)} %copy-done.5) | copy-start | bytes 4718596
  319.1 9.5 %copy-start.9 = (bf16[1024,2304]{1,0:T(8,128)(2,1)S(1)}, bf16[1024,2304]{1,0:T(8,128)(2,1)}, u32[]{:S(2)}) copy-start(bf16[1024,2304]{1,0:T(8,128)(2,1)} %get-tuple-element.69) | copy-start | bytes 14155780
  319.1 9.4 %copy-start.21 = (bf16[4,256,768]{2,1,0:T(8,128)(2,1)S(1)}, bf16[4,256,768]{2,1,0:T(8,128)(2,1)}, u32[]{:S(2)}) copy-start(bf16[4,256,768]{2,1,0:T(8,128)(2,1)} %get-tuple-element.47) | copy-start | bytes 4718596
  387.1 6.0 %copy-start.10 = (bf16[4,256,768]{2,1,0:T(8,128)(2,1)S(1)}, bf16[4,256,768]{2,1,0:T(8,128)(2,1)}, u32[]{:S(2)}) copy-start(bf16[4,256,768]{2,1,0:T(8,128)(2,1)} %get-tuple-element.131) | copy-start | bytes 4718596
  387.1 7.1 %copy-start.14 = (f32[24,768]{1,0:T(8,128)S(1)}, f32[24,768]{1,0:T(8,128)}, u32[]{:S(2)}) copy-start(f32[24,768]{1,0:T(8,128)} %get-tuple-element.136) | copy-start | bytes 221188
  387.1 7.7 %copy-start.13 = (f32[24,3072]{1,0:T(8,128)S(1)}, f32[24,3072]{1,0:T(8,128)}, u32[]{:S(2)}) copy-start(f32[24,3072]{1,0:T(8,128)} %get-tuple-element.137) | copy-start | bytes 884740
  389.0 6.5 %copy-start.12 = (f32[96,768]{1,0:T(8,128)S(1)}, f32[96,768]{1,0:T(8,128)}, u32[]{:S(2)}) copy-start(f32[96,768]{1,0:T(8,128)} %get-tuple-element.138) | copy-start | bytes 884740
  (4 other events, 5.6 us)

commit v7 on v6

--- a/solution.py
+++ b/solution.py
@@ -376,7 +376,7 @@
             half, twin = self.halves[k], self.twins[k]
             for chip_step in range(self.place.chips):
                 spot = self.spot(step, chip_step)
-                half[spot] = (half[spot].astype(F32) + twin[spot].astype(F32)).astype(BF)
+                half[spot] = half[spot] + twin[spot]
 
     def corner(self, chip_step):
         self.sent.append((3, chip_step))
@@ -393,7 +393,7 @@
             self.side_copy(k, 3, chip_step, self.place.twin()).wait_recv()
             spot = self.spot(2 - chip_step % 2, chip_step)
             half = self.halves[k]
-            half[spot] = (half[spot].astype(F32) + self.sides[k][3, chip_step].astype(F32)).astype(BF)
+            half[spot] = half[spot] + self.sides[k][3, chip_step]
 
     def merge(self, chip_step):
         last = 3 if self.square else self.place.columns
@@ -758,16 +758,15 @@
     )(key_bias, inputs, inputs, rows_in, *shards)
 
 
-def attention_back(grid, inputs, key_bias, log_totals, context, grad_context, wholes, rows_out, block=256, chunk=1024):
+def attention_back(grid, inputs, key_bias, log_totals, context, grad_context, wholes, rows_out, block=1024, chunk=512):
     rows = inputs.shape[0]
     width = inputs.shape[1] // 3
     pairs = width // (2 * HD)
     count = grid.group
     keys = rows * count
-    blocks = rows // block
-    steps = pairs * blocks
-    chunk = min(chunk, rows)
-    chunks = keys // chunk
+    block, chunk = min(block, rows), min(chunk, rows)
+    blocks, chunks = rows // block, keys // chunk
+    steps = pairs * blocks * chunks
     late = len(wholes)
     shapes = [whole.shape[2:] for whole in wholes]
     away = max(count - 1, 1)
@@ -777,12 +776,12 @@
         out_ref, back_ref = refs[late : late + 2]
         results = refs[late + 2 : 2 * late + 2]
         rest = refs[2 * late + 2 :]
-        k_own, k_turned, v_all, grad_k, grad_v, far, far_out, far_in, row_hold, hold_sem = rest[:10]
-        far_send, far_receive, out_send, in_receive, row_send, row_receive = rest[10:16]
+        k_own, k_turned, v_all, grad_k, grad_v, grad_q, far, far_out, far_in, row_hold, hold_sem = rest[:11]
+        far_send, far_receive, out_send, in_receive, row_send, row_receive = rest[11:17]
         pair, turn = pl.program_id(0), pl.program_id(1)
         now = pair * blocks + turn
         place = Place(grid)
-        reduce = reduce_of(place, whole_refs, results, rest[16:])
+        reduce = reduce_of(place, whole_refs, results, rest[17:])
         start_rows, finish_rows = row_exchange(place, rows_ref, back_ref, row_send, row_receive)
 
         def far_copy(step, which, kind):
@@ -844,12 +843,17 @@
         moments = {}
         for moment, action in actions:
             moments.setdefault(min(int(moment * steps / 24), steps - 1), []).append(action)
-        for moment, group in sorted(moments.items()):
-
-            @pl.when(now == moment)
-            def _(group=group):
-                for action in group:
-                    action()
+
+        def act(here, some):
+            for moment, group in sorted(moments.items()):
+                if some(moment):
+
+                    @pl.when(here == moment)
+                    def _(group=group):
+                        for action in group:
+                            action()
+
+        act(now * chunks, lambda moment: moment == 0)
 
         @pl.when((turn == 0) & (pair > 0))
         def _():
@@ -883,9 +887,12 @@
             grads.append(jnp.where(own, grad, zero))
             centres.append(jnp.sum(turned[HD * half : HD * half + HD], axis=0, keepdims=True))
             logs.append(l_ref[half : half + 1, :])
-        grad_q = None
-        for c in range(chunks):
-            span = slice(c * chunk, (c + 1) * chunk)
+        grad_q[...] = jnp.zeros_like(grad_q)
+
+        @pl.loop(0, chunks)
+        def _(c):
+            act(now * chunks + c, lambda moment: moment > 0)
+            span = pl.ds(pl.multiple_of(c * chunk, chunk), chunk)
             weights, slopes = [], []
             for half in range(2):
                 scores = dot_nt(k_own[half, span, :], asks[half])
@@ -894,13 +901,12 @@
                 slope = (exact * (grad_weights - centres[half])).astype(BF)
                 weights.append(exact.astype(BF))
                 slopes.append(slope)
-                step = matmul(k_turned[half, :, span], slope)
-                grad_q = step if grad_q is None else grad_q + step
+                grad_q[...] += matmul(k_turned[half, :, span], slope)
             grad_v[span, :] += matmul(weights[0], grads[0]) + matmul(weights[1], grads[1])
             grad_k[span, :] += matmul(slopes[0], plain[0]) + matmul(slopes[1], plain[1])
         at = pl.ds(pl.multiple_of(turn * block, block), block)
         out_ref[at, pl.ds(pl.multiple_of(pair * 2 * HD, 2 * HD), 2 * HD)] = (
-            jnp.transpose(grad_q) * 0.125
+            jnp.transpose(grad_q[...]) * 0.125
         ).astype(BF)
 
         @pl.when(turn == blocks - 1)
@@ -919,7 +925,7 @@
         def _():
             take_back(pair - 1)
 
-        @pl.when(now == steps - 1)
+        @pl.when(now == pairs * blocks - 1)
         def _():
             send_back(pairs - 1)
             reduce.finish()
@@ -967,6 +973,7 @@
             pltpu.VMEM((keys, 2 * HD), BF),
             pltpu.VMEM((keys, 2 * HD), F32),
             pltpu.VMEM((keys, 2 * HD), F32),
+            pltpu.VMEM((2 * HD, block), F32),
             far_buffer,
             far_buffer,
             far_buffer,

time: 402 us -> 399 us (level)
  no operation moved by 1% of the time
where the time goes in v7:
time: 399 us; the launch traced here: 394 us
  Pallas kernels  263 us (66%)
  matrix products  93.1 us (23%)
  other arithmetic  20.9 us (5%)
  local copies, waits for them, and re-layouts  15 us (4%)
    pallas_call x1, Pallas kernels, attention_back(): pl.pallas_call(kernel, grid=(pairs, blocks), in_specs=[tile(), resident((...  93.9 us
    pallas_call x1, Pallas kernels, attention(): pl.pallas_call(kernel, grid=(pairs, blocks), in_specs=[resident((keys, 2...  73.2 us
    pallas_call x1, Pallas kernels, end_exchange(): pl.pallas_call(kernel, in_specs=[HBM] * (count + 1), out_specs=[HBM] + [p...  48.6 us
    pallas_call x1, Pallas kernels, start_exchange(): pl.pallas_call(kernel, in_specs=[HBM] * (parts + 2) + [pl.BlockSpec(memor...  47.6 us
    dot_general x4, matrix products, matmul(): return jnp.dot(left, right, preferred_element_type=F32)  39.8 us
    dot_general x4, matrix products, right_product(): lax.dot_general(left, right, (((1,), (1,)), ((), ())), preferred_element_...  28.7 us
    dot_general x4, matrix products, left_product(): lax.dot_general(left, right, (((0,), (0,)), ((), ())), preferred_element_...  24.7 us

profile of v7, /device:TPU:0, one launch (start us, length us, event | category | flops | bytes accessed | tf_op | source)
XLA Modules:
  0.0 393.8 jit_solution(11772162094747477338)
XLA Ops:
  2.1 47.6 %start_exchange.1 = (bf16[4,256,768]{2,1,0:T(8,128)(2,1)}, bf16[32,24,2304]{2,1,0:T(8,128)(2,1)}, bf16[32,16,128]{2,1,0:T(8,128)(2,1)}, bf16[2048,128]{1,0:T(8,1...) custom-call(bf16[4,256,768]{2,1,0:T(8,128)(2,1)} %tokens_ref.1, ...), custom_call_target="tpu_custom_call" | custom-call | tf_op jit(solution)/shard_map/start_exchange/pallas_call | solution.py:296
  50.5 8.5 %add_convert_fusion.own_ref.all_ref.q_ref.k_ref.v_ref = bf16[1024,2304]{1,0:T(8,128)(2,1)} fusion(bf16[1024,768]{1,0:T(8,128)(2,1)} %bitcast.98, bf16[768,2304]{1,0:T(8,128)(2,1)} %bitcast.96, f32[2304]{0:T(1024)S(1)} %fusion.10), kind=kOutput, calls=%fused_computation.8 | convolution fusion | flops 3628597248 | bytes 9839616 | tf_op jit(solution)/shard_map/dot_general | solution.py:19
  59.0 73.2 %attention.1 = (bf16[1024,768]{1,0:T(8,128)(2,1)S(1)}, f32[6,8,1024]{2,1,0:T(8,128)S(1)}, bf16[4,256,768]{2,1,0:T(8,128)(2,1)S(1)}, bf16[32,24,768]{2,1,0:T(8,12...) custom-call(bf16[2048,128]{1,0:T(8,128)(2,1)S(1)} %copy-done.1, ...), custom_call_target="tpu_custom_call" | custom-call | flops 25769803776 | bytes 6291456 | tf_op jit(solution)/shard_map/attention/pallas_call | solution.py:718
  134.0 5.0 %fusion.16 = (f32[1024]{0:T(1024)S(1)}, f32[1024,768]{1,0:T(8,128)}) fusion(f32[768]{0:T(1024)S(1)} %reduce.8, bf16[1024,768]{1,0:T(8,128)(2,1)} %copy-done.5, bf16[768,768]{1,0:T(8,128)(2,1)S(1)} %bitcast.79, bf16[1024,768]{1,0:T(8,128)(2,1)} %bitcast.99), kind=kOutput, calls=%fused_computation.77 | convolution fusion | flops 1211104256 | bytes 7478272 | tf_op jit(solution)/shard_map/dot_general | solution.py:19
  139.0 2.4 multiply_reduce_fusion.6
  141.5 14.6 %fusion.3 = (bf16[1024,3072]{1,0:T(8,128)(2,1)}, bf16[1024,3072]{1,0:T(8,128)(2,1)S(1)}) fusion(f32[3072]{0:T(1024)S(1)} %bitcast.101, bf16[768,3072]{1,0:T(8,128)(2,1)} %bitcast.102, f32[1024,768]{1,0:T(8,128)} %get-tuple-element.106, f32[768]{0:T(1024)S(1)} %reduce.10, f32[768]{0:T(1024)S(1)} %reduce.9, f32[1024]{0:T(1024)S(1)} %add_rsqrt_fusion.1, ...), kind=kOutput, calls=%fused_computation.4 | convolution fusion | flops 4873519104 | bytes 20473856 | tf_op jit(solution)/shard_map/dot_general | solution.py:19
  156.2 11.7 %fusion.17 = (f32[1024]{0:T(1024)S(1)}, f32[1024,768]{1,0:T(8,128)}) fusion(f32[768]{0:T(1024)S(1)} %reduce.11, bf16[1024,3072]{1,0:T(8,128)(2,1)S(1)} %get-tuple-element.60, bf16[3072,768]{1,0:T(8,128)(2,1)} %bitcast.106, f32[768]{0:T(1024)S(1)} %reduce.10, f32[768]{0:T(1024)S(1)} %reduce.9, f32[1024]{0:T(1024)S(1)} %add_rsqrt_fusion.1, ...), kind=kOutput, calls=%fused_computation.78 | convolution fusion | flops 4838915072 | bytes 17323008 | tf_op jit(solution)/shard_map/dot_general | solution.py:19
  168.1 2.4 multiply_reduce_fusion.5
  170.5 4.3 %multiply_reduce_fusion = (bf16[768]{0:T(1024)(128)(2,1)S(1)}, f32[1024]{0:T(1024)S(1)}, bf16[1024,768]{1,0:T(8,128)(2,1)}) fusion(bf16[4,256,768]{2,1,0:T(8,128)(2,1)S(1)} %get-tuple-element.63, f32[1024,768]{1,0:T(8,128)} %get-tuple-element.108, f32[1024]{0:T(1024)S(1)} %reduce.12, f32[1024]{0:T(1024)S(1)} %add_rsqrt_fusion, ...), kind=kLoop, calls=%fused_computation.14 | loop fusion | flops 10221824 | bytes 6315520 | tf_op jit(solution)/shard_map/reduce_sum | solution.py:1074
  175.7 2.9 convert_reduce_fusion.1
  178.6 8.7 %fusion.18 = (bf16[3072]{0:T(1024)(128)(2,1)S(1)}, bf16[1024,3072]{1,0:T(8,128)(2,1)S(1)}) fusion(bf16[1024,3072]{1,0:T(8,128)(2,1)} %get-tuple-element.66, bf16[3072,768]{1,0:T(8,128)(2,1)} %bitcast.107, f32[1024,768]{1,0:T(8,128)S(1)} %get-tuple-element.88), kind=kOutput, calls=%fused_computation.79 | convolution fusion | flops 4845204480 | bytes 20453376 | tf_op jit(solution)/shard_map/dot_general | solution.py:27
  187.3 7.9 %multiply_reduce_fusion.1 = (bf16[768]{0:T(1024)(128)(2,1)S(1)}, f32[1024]{0:T(1024)S(1)}, f32[1024]{0:T(1024)S(1)}, bf16[768]{0:T(1024)(128)(2,1)S(1)}, f32[1024,768]{1,0:T(8,128)S(1)}) fusion(f32[1024,768]{1,0:T(8,128)} %get-tuple-element.106, f32[1024]{0:T(1024)S(1)} %add_rsqrt_fusion.1, f32[1024]{0:T(1024)S(1)} %broadcast_multiply_fusion.4, ...), kind=kOutput, calls=%fused_computation.15 | convolution fusion | flops 4839698432 | bytes 20469760 | tf_op jit(solution)/shard_map/dot_general | solution.py:27
  195.3 2.5 convert_reduce_fusion
  197.8 2.6 convolution_convert_fusion.3.g_ref
  200.4 10.7 %convolution_convert_fusion.1 = bf16[768,3072]{1,0:T(8,128)(2,1)} fusion(bf16[1024,3072]{1,0:T(8,128)(2,1)S(1)} %get-tuple-element.111, f32[1024,768]{1,0:T(8,128)} %get-tuple-element.106, f32[768]{0:T(1024)S(1)} %reduce.10, f32[768]{0:T(1024)S(1)} %reduce.9, f32[1024]{0:T(1024)S(1)} %add_rsqrt_fusion.1, f32[1024]{0:T(1024)S(1)} %broadcast_multiply_fusion.4), kind=kOutput, calls=%fused_computation.10 | convolution fusion | flops 4838129664 | bytes 14170112 | tf_op jit(solution)/shard_map/dot_general | solution.py:23
  211.1 7.0 %convolution_convert_fusion = bf16[3072,768]{1,0:T(8,128)(2,1)} fusion(bf16[1024,3072]{1,0:T(8,128)(2,1)S(1)} %bitcast.112, f32[1024,768]{1,0:T(8,128)S(1)} %get-tuple-element.88), kind=kOutput, calls=%fused_computation.9 | convolution fusion | flops 4834983936 | bytes 14155776 | tf_op jit(solution)/shard_map/dot_general | solution.py:23
  218.2 2.5 convolution_convert_fusion.4
  222.4 93.9 %attention_back.1 = (bf16[1024,2304]{1,0:T(8,128)(2,1)}, bf16[4,256,768]{2,1,0:T(8,128)(2,1)}, f32[24,3072]{1,0:T(8,128)}, f32[96,768]{1,0:T(8,128)}, f32[24,768]{1,0:T(8,128)}, /*index=5*/f32[8,256]{1,0:T(8,128)}) custom-call(bf16[1024,2304]{1,0:T(8,128)(2,1)} %add_convert_fusion.own_ref.all_ref.q_ref.k_ref.v_ref, ...), custom_call_target="tpu_custom_call" | custom-call | flops 64424509440 | bytes 9437184 | tf_op jit(solution)/shard_map/attention_back/pallas_call | solution.py:952
  316.4 9.4 %add_convert_fusion.1 = bf16[1024,768]{1,0:T(8,128)(2,1)} fusion(f32[1024,768]{1,0:T(8,128)} %copy-done.8, bf16[1024,2304]{1,0:T(8,128)(2,1)} %get-tuple-element.69, bf16[768,2304]{1,0:T(8,128)(2,1)} %bitcast.97), kind=kOutput, calls=%fused_computation.13 | convolution fusion | flops 3625451520 | bytes 12976128 | tf_op jit(solution)/shard_map/dot_general | solution.py:27
  325.8 4.4 %convolution_convert_fusion.2 = bf16[768,2304]{1,0:T(8,128)(2,1)S(1)} fusion(bf16[1024,768]{1,0:T(8,128)(2,1)S(1)} %bitcast.100, bf16[1024,2304]{1,0:T(8,128)(2,1)S(1)} %copy-done.9), kind=kOutput, calls=%fused_computation.11 | convolution fusion | flops 3625648128 | bytes 9830400 | tf_op jit(solution)/shard_map/dot_general | solution.py:23
  334.4 1.4 copy-done
  335.8 48.6 %end_exchange.1 = (bf16[4,256,768]{2,1,0:T(8,128)(2,1)S(1)}, f32[24,2304]{1,0:T(8,128)S(1)}, f32[8,128]{1,0:T(8,128)S(1)}) custom-call(bf16[4,256,768]{2,1,0:T(8,128)(2,1)S(1)} %bitcast.78, bf16[16,2,24,2304]{3,2,1,0:T(8,128)(2,1)S(1)} %bitcast.77, bf16[16,2,8,128]{3,2,1,0:T(8,128)(2,1)S(1)} %broadcast_in_dim.67.refs_1_), custom_call_target="tpu_custom_call" | custom-call | tf_op jit(solution)/shard_map/end_exchange/pallas_call | solution.py:543
  384.4 1.9 convert_element_type.136
  387.6 1.5 slice_bitcast_fusion
  (111 shorter events, 16.6 us)
Async XLA Ops:
  50.4 8.5 %copy-start.1 = (bf16[2048,128]{1,0:T(8,128)(2,1)S(1)}, bf16[2048,128]{1,0:T(8,128)(2,1)}, u32[]{:S(2)}) copy-start(bf16[2048,128]{1,0:T(8,128)(2,1)} %get-tuple-element.51.bias_ref) | copy-start | bytes 1572868
  50.4 8.5 %copy-start.2 = (bf16[24,3072]{1,0:T(8,128)(2,1)S(1)}, bf16[24,3072]{1,0:T(8,128)(2,1)}, u32[]{:S(2)}) copy-start(bf16[24,3072]{1,0:T(8,128)(2,1)} %refs_1_.1) | copy-start | bytes 442372
  50.4 8.5 %copy-start.3 = (bf16[96,768]{1,0:T(8,128)(2,1)S(1)}, bf16[96,768]{1,0:T(8,128)(2,1)}, u32[]{:S(2)}) copy-start(bf16[96,768]{1,0:T(8,128)(2,1)} %refs_2_.1) | copy-start | bytes 442372
  50.5 8.5 %copy-start.4 = (bf16[24,768]{1,0:T(8,128)(2,1)S(1)}, bf16[24,768]{1,0:T(8,128)(2,1)}, u32[]{:S(2)}) copy-start(bf16[24,768]{1,0:T(8,128)(2,1)} %refs_0_.1) | copy-start | bytes 110596
  59.0 75.0 %copy-start.20 = (f32[1,768]{1,0:T(1,128)S(1)}, f32[1,768]{1,0:T(1,128)}, u32[]{:S(2)}) copy-start(f32[1,768]{1,0:T(1,128)} %get-tuple-element.55) | copy-start | bytes 9220
  139.0 2.4 copy-start.18
  139.0 2.5 copy-start.17
  139.0 2.5 copy-start.22
  156.2 11.7 %copy-start.23 = (bf16[1024,3072]{1,0:T(8,128)(2,1)}, bf16[1024,3072]{1,0:T(8,128)(2,1)S(1)}, u32[]{:S(2)}) copy-start(bf16[1024,3072]{1,0:T(8,128)(2,1)S(1)} %get-tuple-element.60) | copy-start | bytes 18874372
  156.2 11.7 %copy-start.11 = (f32[1024,1]{1,0:T(8,128)S(1)}, f32[1024,1]{1,0:T(8,128)}, u32[]{:S(2)}) copy-start(f32[1024,1]{1,0:T(8,128)} %get-tuple-element.64) | copy-start | bytes 12292
  167.9 2.6 copy-start.16
  167.9 2.6 copy-start.15
  175.7 11.6 %slice-start = ((s8[4718592]{0:T(1024)(128)(4,1)}), s8[4194304]{0:T(1024)(128)(4,1)S(1)}, s32[]{:S(2)}) async-start(s8[4718592]{0:T(1024)(128)(4,1)} %bitcast.103), calls=%async_computation | async-start | bytes 8388608
  178.6 8.8 %slice-start.1 = ((s8[4718592]{0:T(1024)(128)(4,1)}), s8[524288]{0:T(1024)(128)(4,1)S(1)}, s32[]{:S(2)}) async-start(s8[4718592]{0:T(1024)(128)(4,1)} %bitcast.103), calls=%async_computation.1 | async-start | bytes 1048576
  197.8 20.3 %copy-start.8 = (f32[1024,768]{1,0:T(8,128)}, f32[1024,768]{1,0:T(8,128)S(1)}, u32[]{:S(2)}) copy-start(f32[1024,768]{1,0:T(8,128)S(1)} %get-tuple-element.90) | copy-start | bytes 9437188
  197.8 13.3 %slice-start.2 = ((s8[6291456]{0:T(1024)(128)(4,1)}), s8[4194304]{0:T(1024)(128)(4,1)S(1)}, s32[]{:S(2)}) async-start(s8[6291456]{0:T(1024)(128)(4,1)} %bitcast.111), calls=%async_computation.2 | async-start | bytes 8388608
  200.4 10.7 %slice-start.3 = ((s8[6291456]{0:T(1024)(128)(4,1)}), s8[2097152]{0:T(1024)(128)(4,1)S(1)}, s32[]{:S(2)}) async-start(s8[6291456]{0:T(1024)(128)(4,1)} %bitcast.111), calls=%async_computation.3 | async-start | bytes 4194304
  211.1 7.0 %copy-start.6 = (bf16[1024,768]{1,0:T(8,128)(2,1)S(1)}, bf16[1024,768]{1,0:T(8,128)(2,1)}, u32[]{:S(2)}) copy-start(bf16[1024,768]{1,0:T(8,128)(2,1)} %copy-done.5) | copy-start | bytes 4718596
  316.3 9.5 %copy-start.9 = (bf16[1024,2304]{1,0:T(8,128)(2,1)S(1)}, bf16[1024,2304]{1,0:T(8,128)(2,1)}, u32[]{:S(2)}) copy-start(bf16[1024,2304]{1,0:T(8,128)(2,1)} %get-tuple-element.69) | copy-start | bytes 14155780
  316.3 9.5 %copy-start.21 = (bf16[4,256,768]{2,1,0:T(8,128)(2,1)S(1)}, bf16[4,256,768]{2,1,0:T(8,128)(2,1)}, u32[]{:S(2)}) copy-start(bf16[4,256,768]{2,1,0:T(8,128)(2,1)} %get-tuple-element.47) | copy-start | bytes 4718596
  384.4 6.0 %copy-start.10 = (bf16[4,256,768]{2,1,0:T(8,128)(2,1)S(1)}, bf16[4,256,768]{2,1,0:T(8,128)(2,1)}, u32[]{:S(2)}) copy-start(bf16[4,256,768]{2,1,0:T(8,128)(2,1)} %get-tuple-element.131) | copy-start | bytes 4718596
  384.4 7.1 %copy-start.14 = (f32[24,768]{1,0:T(8,128)S(1)}, f32[24,768]{1,0:T(8,128)}, u32[]{:S(2)}) copy-start(f32[24,768]{1,0:T(8,128)} %get-tuple-element.136) | copy-start | bytes 221188
  384.4 7.7 %copy-start.13 = (f32[24,3072]{1,0:T(8,128)S(1)}, f32[24,3072]{1,0:T(8,128)}, u32[]{:S(2)}) copy-start(f32[24,3072]{1,0:T(8,128)} %get-tuple-element.137) | copy-start | bytes 884740
  386.3 6.5 %copy-start.12 = (f32[96,768]{1,0:T(8,128)S(1)}, f32[96,768]{1,0:T(8,128)}, u32[]{:S(2)}) copy-start(f32[96,768]{1,0:T(8,128)} %get-tuple-element.138) | copy-start | bytes 884740
  (4 other events, 5.6 us)

commit v8 on v7

--- a/solution.py
+++ b/solution.py
@@ -1061,7 +1061,7 @@
 
     first_sum = flat_in.astype(F32) + matmul(context, out_full) + out_add
     first_norm, first_unit, first_factor = normalize(first_sum, gain_one, shift_one)
-    first_low = first_norm.astype(BF)
+    first_low = lax.optimization_barrier(first_norm.astype(BF))
     up_pre = matmul(first_low, up_full) + up_add
     below = 0.5 * (1.0 + lax.erf(up_pre * ROOT_HALF))
     slope = (below + up_pre * INV_ROOT_TWO_PI * jnp.exp(-0.5 * up_pre * up_pre)).astype(BF)

time: 399 us -> 391 us (0.980)
  matrix products: 93.1 us -> 82.7 us
    dot_general x4, matrix products: 39.8 us -> 32.7 us  [matmul(): return jnp.dot(left, right, preferred_element_type=F32)]
where the time goes in v8:
time: 391 us; the launch traced here: 386 us
  Pallas kernels  263 us (67%)
  matrix products  82.7 us (21%)
  other arithmetic  23.3 us (6%)
  local copies, waits for them, and re-layouts  15 us (4%)
    pallas_call x1, Pallas kernels, attention_back(): pl.pallas_call(kernel, grid=(pairs, blocks), in_specs=[tile(), resident((...  93.7 us
    pallas_call x1, Pallas kernels, attention(): pl.pallas_call(kernel, grid=(pairs, blocks), in_specs=[resident((keys, 2...  73.3 us
    pallas_call x1, Pallas kernels, end_exchange(): pl.pallas_call(kernel, in_specs=[HBM] * (count + 1), out_specs=[HBM] + [p...  48.6 us
    pallas_call x1, Pallas kernels, start_exchange(): pl.pallas_call(kernel, in_specs=[HBM] * (parts + 2) + [pl.BlockSpec(memor...  47.6 us
    dot_general x4, matrix products, matmul(): return jnp.dot(left, right, preferred_element_type=F32)  32.7 us
    dot_general x4, matrix products, right_product(): lax.dot_general(left, right, (((1,), (1,)), ((), ())), preferred_element_...  28.9 us
    dot_general x4, matrix products, left_product(): lax.dot_general(left, right, (((0,), (0,)), ((), ())), preferred_element_...  21.2 us

profile of v8, /device:TPU:0, one launch (start us, length us, event | category | flops | bytes accessed | tf_op | source)
XLA Modules:
  0.0 385.7 jit_solution(14733634859862180793)
XLA Ops:
  2.1 47.6 %start_exchange.1 = (bf16[4,256,768]{2,1,0:T(8,128)(2,1)}, bf16[32,24,2304]{2,1,0:T(8,128)(2,1)}, bf16[32,16,128]{2,1,0:T(8,128)(2,1)}, bf16[2048,128]{1,0:T(8,1...) custom-call(bf16[4,256,768]{2,1,0:T(8,128)(2,1)} %tokens_ref.1, ...), custom_call_target="tpu_custom_call" | custom-call | tf_op jit(solution)/shard_map/start_exchange/pallas_call | solution.py:296
  50.5 8.5 %add_convert_fusion.own_ref.all_ref.q_ref.k_ref.v_ref = bf16[1024,2304]{1,0:T(8,128)(2,1)} fusion(bf16[1024,768]{1,0:T(8,128)(2,1)} %bitcast.100, bf16[768,2304]{1,0:T(8,128)(2,1)} %bitcast.98, f32[2304]{0:T(1024)S(1)} %fusion.10), kind=kOutput, calls=%fused_computation.8 | convolution fusion | flops 3628597248 | bytes 9839616 | tf_op jit(solution)/shard_map/dot_general | solution.py:19
  59.0 73.3 %attention.1 = (bf16[1024,768]{1,0:T(8,128)(2,1)S(1)}, f32[6,8,1024]{2,1,0:T(8,128)S(1)}, bf16[4,256,768]{2,1,0:T(8,128)(2,1)S(1)}, bf16[32,24,768]{2,1,0:T(8,12...) custom-call(bf16[2048,128]{1,0:T(8,128)(2,1)S(1)} %copy-done.1, ...), custom_call_target="tpu_custom_call" | custom-call | flops 25769803776 | bytes 6291456 | tf_op jit(solution)/shard_map/attention/pallas_call | solution.py:718
  134.1 5.0 %fusion.16 = (f32[1024]{0:T(1024)S(1)}, f32[1024,768]{1,0:T(8,128)}) fusion(f32[768]{0:T(1024)S(1)} %reduce.8, bf16[1024,768]{1,0:T(8,128)(2,1)} %copy-done.5, bf16[768,768]{1,0:T(8,128)(2,1)S(1)} %bitcast.81, bf16[1024,768]{1,0:T(8,128)(2,1)} %bitcast.101), kind=kOutput, calls=%fused_computation.77 | convolution fusion | flops 1211104256 | bytes 7478272 | tf_op jit(solution)/shard_map/dot_general | solution.py:19
  139.1 2.4 multiply_reduce_fusion.6
  141.6 2.6 add_convert_fusion.2
  144.2 12.4 %fusion.3 = (bf16[1024,3072]{1,0:T(8,128)(2,1)}, bf16[1024,3072]{1,0:T(8,128)(2,1)S(1)}) fusion(f32[3072]{0:T(1024)S(1)} %bitcast.103, bf16[1024,768]{1,0:T(8,128)(2,1)S(1)} %add_convert_fusion.2, bf16[768,3072]{1,0:T(8,128)(2,1)} %bitcast.104), kind=kOutput, calls=%fused_computation.4 | convolution fusion | flops 4869586944 | bytes 18886656 | tf_op jit(solution)/shard_map/dot_general | solution.py:19
  156.7 6.8 %fusion.17 = (f32[1024]{0:T(1024)S(1)}, f32[1024,768]{1,0:T(8,128)}) fusion(f32[768]{0:T(1024)S(1)} %reduce.11, bf16[1024,3072]{1,0:T(8,128)(2,1)S(1)} %get-tuple-element.60, bf16[3072,768]{1,0:T(8,128)(2,1)S(1)} %bitcast.111, bf16[1024,768]{1,0:T(8,128)(2,1)S(1)} %add_convert_fusion.2), kind=kOutput, calls=%fused_computation.78 | convolution fusion | flops 4834982912 | bytes 15735808 | tf_op jit(solution)/shard_map/dot_general | solution.py:19
  163.7 2.4 multiply_reduce_fusion.5
  166.1 4.1 %multiply_reduce_fusion = (bf16[768]{0:T(1024)(128)(2,1)S(1)}, f32[1024]{0:T(1024)S(1)}, bf16[1024,768]{1,0:T(8,128)(2,1)}) fusion(bf16[4,256,768]{2,1,0:T(8,128)(2,1)S(1)} %get-tuple-element.63, f32[1024,768]{1,0:T(8,128)} %get-tuple-element.108, f32[1024]{0:T(1024)S(1)} %reduce.12, f32[1024]{0:T(1024)S(1)} %add_rsqrt_fusion, ...), kind=kLoop, calls=%fused_computation.14 | loop fusion | flops 10221824 | bytes 6315520 | tf_op jit(solution)/shard_map/reduce_sum | solution.py:1074
  171.0 2.9 convert_reduce_fusion.1
  173.9 8.9 %fusion.18 = (bf16[3072]{0:T(1024)(128)(2,1)S(1)}, bf16[1024,3072]{1,0:T(8,128)(2,1)S(1)}) fusion(bf16[1024,3072]{1,0:T(8,128)(2,1)} %get-tuple-element.66, bf16[3072,768]{1,0:T(8,128)(2,1)} %bitcast.108, f32[1024,768]{1,0:T(8,128)S(1)} %get-tuple-element.88), kind=kOutput, calls=%fused_computation.79 | convolution fusion | flops 4845204480 | bytes 20453376 | tf_op jit(solution)/shard_map/dot_general | solution.py:27
  182.9 7.9 %multiply_reduce_fusion.1 = (bf16[768]{0:T(1024)(128)(2,1)S(1)}, f32[1024]{0:T(1024)S(1)}, f32[1024]{0:T(1024)S(1)}, bf16[768]{0:T(1024)(128)(2,1)S(1)}, f32[1024,768]{1,0:T(8,128)S(1)}) fusion(f32[1024,768]{1,0:T(8,128)} %get-tuple-element.106, f32[1024]{0:T(1024)S(1)} %add_rsqrt_fusion.1, f32[1024]{0:T(1024)S(1)} %broadcast_multiply_fusion.4, ...), kind=kOutput, calls=%fused_computation.15 | convolution fusion | flops 4839698432 | bytes 20469760 | tf_op jit(solution)/shard_map/dot_general | solution.py:27
  190.8 2.5 convert_reduce_fusion
  193.4 2.6 convolution_convert_fusion.3.g_ref
  196.0 6.9 %convolution_convert_fusion.1 = bf16[768,3072]{1,0:T(8,128)(2,1)} fusion(bf16[1024,768]{1,0:T(8,128)(2,1)S(1)} %copy-done.12, bf16[1024,3072]{1,0:T(8,128)(2,1)S(1)} %get-tuple-element.111), kind=kOutput, calls=%fused_computation.10 | convolution fusion | flops 4834197504 | bytes 12582912 | tf_op jit(solution)/shard_map/dot_general | solution.py:23
  202.9 7.3 %convolution_convert_fusion = bf16[3072,768]{1,0:T(8,128)(2,1)} fusion(bf16[1024,3072]{1,0:T(8,128)(2,1)S(1)} %bitcast.116, f32[1024,768]{1,0:T(8,128)S(1)} %get-tuple-element.88), kind=kOutput, calls=%fused_computation.9 | convolution fusion | flops 4834983936 | bytes 14155776 | tf_op jit(solution)/shard_map/dot_general | solution.py:23
  210.3 2.5 convolution_convert_fusion.4
  214.5 93.7 %attention_back.1 = (bf16[1024,2304]{1,0:T(8,128)(2,1)}, bf16[4,256,768]{2,1,0:T(8,128)(2,1)}, f32[24,3072]{1,0:T(8,128)}, f32[96,768]{1,0:T(8,128)}, f32[24,768]{1,0:T(8,128)}, /*index=5*/f32[8,256]{1,0:T(8,128)}) custom-call(bf16[1024,2304]{1,0:T(8,128)(2,1)} %add_convert_fusion.own_ref.all_ref.q_ref.k_ref.v_ref, ...), custom_call_target="tpu_custom_call" | custom-call | flops 64424509440 | bytes 9437184 | tf_op jit(solution)/shard_map/attention_back/pallas_call | solution.py:952
  308.3 9.4 %add_convert_fusion.1 = bf16[1024,768]{1,0:T(8,128)(2,1)} fusion(f32[1024,768]{1,0:T(8,128)} %copy-done.8, bf16[1024,2304]{1,0:T(8,128)(2,1)} %get-tuple-element.69, bf16[768,2304]{1,0:T(8,128)(2,1)} %bitcast.99), kind=kOutput, calls=%fused_computation.13 | convolution fusion | flops 3625451520 | bytes 12976128 | tf_op jit(solution)/shard_map/dot_general | solution.py:27
  317.7 4.5 %convolution_convert_fusion.2 = bf16[768,2304]{1,0:T(8,128)(2,1)S(1)} fusion(bf16[1024,768]{1,0:T(8,128)(2,1)S(1)} %bitcast.102, bf16[1024,2304]{1,0:T(8,128)(2,1)S(1)} %copy-done.9), kind=kOutput, calls=%fused_computation.11 | convolution fusion | flops 3625648128 | bytes 9830400 | tf_op jit(solution)/shard_map/dot_general | solution.py:23
  327.7 48.6 %end_exchange.1 = (bf16[4,256,768]{2,1,0:T(8,128)(2,1)S(1)}, f32[24,2304]{1,0:T(8,128)S(1)}, f32[8,128]{1,0:T(8,128)S(1)}) custom-call(bf16[4,256,768]{2,1,0:T(8,128)(2,1)S(1)} %bitcast.80, bf16[16,2,24,2304]{3,2,1,0:T(8,128)(2,1)S(1)} %bitcast.79, bf16[16,2,8,128]{3,2,1,0:T(8,128)(2,1)S(1)} %broadcast_in_dim.67.refs_1_), custom_call_target="tpu_custom_call" | custom-call | tf_op jit(solution)/shard_map/end_exchange/pallas_call | solution.py:543
  376.3 1.9 convert_element_type.136
  379.5 1.5 slice_bitcast_fusion
  (121 shorter events, 18.0 us)
Async XLA Ops:
  50.4 8.5 %copy-start.1 = (bf16[2048,128]{1,0:T(8,128)(2,1)S(1)}, bf16[2048,128]{1,0:T(8,128)(2,1)}, u32[]{:S(2)}) copy-start(bf16[2048,128]{1,0:T(8,128)(2,1)} %get-tuple-element.51.bias_ref) | copy-start | bytes 1572868
  50.4 8.5 %copy-start.2 = (bf16[24,3072]{1,0:T(8,128)(2,1)S(1)}, bf16[24,3072]{1,0:T(8,128)(2,1)}, u32[]{:S(2)}) copy-start(bf16[24,3072]{1,0:T(8,128)(2,1)} %refs_1_.1) | copy-start | bytes 442372
  50.4 8.5 %copy-start.3 = (bf16[96,768]{1,0:T(8,128)(2,1)S(1)}, bf16[96,768]{1,0:T(8,128)(2,1)}, u32[]{:S(2)}) copy-start(bf16[96,768]{1,0:T(8,128)(2,1)} %refs_2_.1) | copy-start | bytes 442372
  50.5 8.5 %copy-start.4 = (bf16[24,768]{1,0:T(8,128)(2,1)S(1)}, bf16[24,768]{1,0:T(8,128)(2,1)}, u32[]{:S(2)}) copy-start(bf16[24,768]{1,0:T(8,128)(2,1)} %refs_0_.1) | copy-start | bytes 110596
  59.0 75.1 %copy-start.22 = (f32[1,768]{1,0:T(1,128)S(1)}, f32[1,768]{1,0:T(1,128)}, u32[]{:S(2)}) copy-start(f32[1,768]{1,0:T(1,128)} %get-tuple-element.55) | copy-start | bytes 9220
  141.5 2.7 copy-start.24
  141.6 15.1 %slice-start.2 = ((s8[4718592]{0:T(1024)(128)(4,1)}), s8[4194304]{0:T(1024)(128)(4,1)S(1)}, s32[]{:S(2)}) async-start(s8[4718592]{0:T(1024)(128)(4,1)} %bitcast.109), calls=%async_computation.2 | async-start | bytes 8388608
  144.2 12.4 %copy-start.11 = (bf16[1024,768]{1,0:T(8,128)(2,1)}, bf16[1024,768]{1,0:T(8,128)(2,1)S(1)}, u32[]{:S(2)}) copy-start(bf16[1024,768]{1,0:T(8,128)(2,1)S(1)} %add_convert_fusion.2) | copy-start | bytes 4718596
  144.2 12.4 %slice-start.3 = ((s8[4718592]{0:T(1024)(128)(4,1)}), s8[524288]{0:T(1024)(128)(4,1)S(1)}, s32[]{:S(2)}) async-start(s8[4718592]{0:T(1024)(128)(4,1)} %bitcast.109), calls=%async_computation.3 | async-start | bytes 1048576
  156.6 6.9 %copy-start.25 = (bf16[1024,3072]{1,0:T(8,128)(2,1)}, bf16[1024,3072]{1,0:T(8,128)(2,1)S(1)}, u32[]{:S(2)}) copy-start(bf16[1024,3072]{1,0:T(8,128)(2,1)S(1)} %get-tuple-element.60) | copy-start | bytes 18874372
  156.7 6.8 %copy-start.13 = (f32[1024,1]{1,0:T(8,128)S(1)}, f32[1024,1]{1,0:T(8,128)}, u32[]{:S(2)}) copy-start(f32[1024,1]{1,0:T(8,128)} %get-tuple-element.64) | copy-start | bytes 12292
  163.5 2.6 copy-start.17
  171.0 11.8 %slice-start = ((s8[4718592]{0:T(1024)(128)(4,1)}), s8[4194304]{0:T(1024)(128)(4,1)S(1)}, s32[]{:S(2)}) async-start(s8[4718592]{0:T(1024)(128)(4,1)} %bitcast.105), calls=%async_computation | async-start | bytes 8388608
  173.9 8.9 %slice-start.1 = ((s8[4718592]{0:T(1024)(128)(4,1)}), s8[524288]{0:T(1024)(128)(4,1)S(1)}, s32[]{:S(2)}) async-start(s8[4718592]{0:T(1024)(128)(4,1)} %bitcast.105), calls=%async_computation.1 | async-start | bytes 1048576
  193.4 16.9 %copy-start.8 = (f32[1024,768]{1,0:T(8,128)}, f32[1024,768]{1,0:T(8,128)S(1)}, u32[]{:S(2)}) copy-start(f32[1024,768]{1,0:T(8,128)S(1)} %get-tuple-element.90) | copy-start | bytes 9437188
  193.4 9.5 %slice-start.4 = ((s8[6291456]{0:T(1024)(128)(4,1)}), s8[4194304]{0:T(1024)(128)(4,1)S(1)}, s32[]{:S(2)}) async-start(s8[6291456]{0:T(1024)(128)(4,1)} %bitcast.115), calls=%async_computation.4 | async-start | bytes 8388608
  196.0 6.9 %slice-start.5 = ((s8[6291456]{0:T(1024)(128)(4,1)}), s8[2097152]{0:T(1024)(128)(4,1)S(1)}, s32[]{:S(2)}) async-start(s8[6291456]{0:T(1024)(128)(4,1)} %bitcast.115), calls=%async_computation.5 | async-start | bytes 4194304
  202.9 7.4 %copy-start.6 = (bf16[1024,768]{1,0:T(8,128)(2,1)S(1)}, bf16[1024,768]{1,0:T(8,128)(2,1)}, u32[]{:S(2)}) copy-start(bf16[1024,768]{1,0:T(8,128)(2,1)} %copy-done.5) | copy-start | bytes 4718596
  308.2 9.5 %copy-start.9 = (bf16[1024,2304]{1,0:T(8,128)(2,1)S(1)}, bf16[1024,2304]{1,0:T(8,128)(2,1)}, u32[]{:S(2)}) copy-start(bf16[1024,2304]{1,0:T(8,128)(2,1)} %get-tuple-element.69) | copy-start | bytes 14155780
  308.2 9.5 %copy-start.23 = (bf16[4,256,768]{2,1,0:T(8,128)(2,1)S(1)}, bf16[4,256,768]{2,1,0:T(8,128)(2,1)}, u32[]{:S(2)}) copy-start(bf16[4,256,768]{2,1,0:T(8,128)(2,1)} %get-tuple-element.47) | copy-start | bytes 4718596
  376.3 6.0 %copy-start.10 = (bf16[4,256,768]{2,1,0:T(8,128)(2,1)S(1)}, bf16[4,256,768]{2,1,0:T(8,128)(2,1)}, u32[]{:S(2)}) copy-start(bf16[4,256,768]{2,1,0:T(8,128)(2,1)} %get-tuple-element.131) | copy-start | bytes 4718596
  376.3 7.1 %copy-start.16 = (f32[24,768]{1,0:T(8,128)S(1)}, f32[24,768]{1,0:T(8,128)}, u32[]{:S(2)}) copy-start(f32[24,768]{1,0:T(8,128)} %get-tuple-element.136) | copy-start | bytes 221188
  376.3 7.8 %copy-start.15 = (f32[24,3072]{1,0:T(8,128)S(1)}, f32[24,3072]{1,0:T(8,128)}, u32[]{:S(2)}) copy-start(f32[24,3072]{1,0:T(8,128)} %get-tuple-element.137) | copy-start | bytes 884740
  378.2 6.5 %copy-start.14 = (f32[96,768]{1,0:T(8,128)S(1)}, f32[96,768]{1,0:T(8,128)}, u32[]{:S(2)}) copy-start(f32[96,768]{1,0:T(8,128)} %get-tuple-element.138) | copy-start | bytes 884740
  (8 other events, 15.8 us)

commit v9 on v8

--- a/solution.py
+++ b/solution.py
@@ -1097,6 +1097,17 @@
         table = jnp.pad(table, ((0, 0), (0, -size % 128)))
         return jnp.broadcast_to(table[:, None, :], (devices, 8, table.shape[1])).reshape(devices * 8, -1)
 
+    def spread_pack(grads):
+        count = len(grads)
+        place = jnp.arange(count * width, dtype=jnp.int32)
+        lane = (place // width) * slim + place % slim
+        owner = (place % width) // slim
+        row = jnp.concatenate(grads).astype(BF)[None, :]
+        apart = jnp.where(jnp.arange(devices, dtype=jnp.int32)[:, None] == owner[None, :], row, jnp.zeros_like(row))
+        lanes = -(-count * slim // 128) * 128
+        table = matmul(apart, (lane[:, None] == jnp.arange(lanes, dtype=jnp.int32)[None, :]).astype(BF)).astype(BF)
+        return jnp.broadcast_to(table[:, None, :], (devices, 8, lanes)).reshape(devices * 8, lanes)
+
     middle = pack(
         [grad_out_add, grad_down_add, grad_gain_one, grad_shift_one, grad_gain_two, grad_shift_two],
         (grad_up_add.reshape(devices, tall),),
@@ -1115,7 +1126,7 @@
     tokens_grad = right_product(low, into_full) + grad_residual
     wholes = [
         by_place(grid, left_product(flat_in, low).astype(BF), slim),
-        by_place(grid, pack([query_adds, value_adds]), 8),
+        by_place(grid, spread_pack([query_adds, value_adds]), 8),
     ]
     tokens_grad = tokens_grad.astype(BF).reshape(seqs, length, width)
     tokens_grad, grad_into_own, last_own = end_exchange(grid, tokens_grad, wholes)

time: 391 us -> 385 us (0.985)
    dot_general x4 -> x5, matrix products: 32.7 us -> 31.3 us  [matmul(): return jnp.dot(left, right, preferred_element_type=F32)]
where the time goes in v9:
time: 385 us; the launch traced here: 380 us
  Pallas kernels  263 us (68%)
  matrix products  81.9 us (21%)
  other arithmetic  19.8 us (5%)
  local copies, waits for them, and re-layouts  13.1 us (3%)
    pallas_call x1, Pallas kernels, attention_back(): pl.pallas_call(kernel, grid=(pairs, blocks), in_specs=[tile(), resident((...  93.8 us
    pallas_call x1, Pallas kernels, attention(): pl.pallas_call(kernel, grid=(pairs, blocks), in_specs=[resident((keys, 2...  73.2 us
    pallas_call x1, Pallas kernels, end_exchange(): pl.pallas_call(kernel, in_specs=[HBM] * (count + 1), out_specs=[HBM] + [p...  48.6 us
    pallas_call x1, Pallas kernels, start_exchange(): pl.pallas_call(kernel, in_specs=[HBM] * (parts + 2) + [pl.BlockSpec(memor...  47.6 us
    dot_general x5, matrix products, matmul(): return jnp.dot(left, right, preferred_element_type=F32)  31.3 us
    dot_general x4, matrix products, right_product(): lax.dot_general(left, right, (((1,), (1,)), ((), ())), preferred_element_...  29.6 us
    dot_general x4, matrix products, left_product(): lax.dot_general(left, right, (((0,), (0,)), ((), ())), preferred_element_...  20.9 us

profile of v9, /device:TPU:0, one launch (start us, length us, event | category | flops | bytes accessed | tf_op | source)
XLA Modules:
  0.0 379.7 jit_solution(5211351585895071800)
XLA Ops:
  2.1 47.6 %start_exchange.1 = (bf16[4,256,768]{2,1,0:T(8,128)(2,1)}, bf16[32,24,2304]{2,1,0:T(8,128)(2,1)}, bf16[32,16,128]{2,1,0:T(8,128)(2,1)}, bf16[2048,128]{1,0:T(8,1...) custom-call(bf16[4,256,768]{2,1,0:T(8,128)(2,1)} %tokens_ref.1, ...), custom_call_target="tpu_custom_call" | custom-call | tf_op jit(solution)/shard_map/start_exchange/pallas_call | solution.py:296
  50.5 8.5 %add_convert_fusion.own_ref.all_ref.q_ref.k_ref.v_ref = bf16[1024,2304]{1,0:T(8,128)(2,1)} fusion(bf16[1024,768]{1,0:T(8,128)(2,1)} %bitcast.96, bf16[768,2304]{1,0:T(8,128)(2,1)} %bitcast.94, f32[2304]{0:T(1024)S(1)} %fusion.20), kind=kOutput, calls=%fused_computation.8 | convolution fusion | flops 3628597248 | bytes 9839616 | tf_op jit(solution)/shard_map/dot_general | solution.py:19
  59.0 73.2 %attention.1 = (bf16[1024,768]{1,0:T(8,128)(2,1)S(1)}, f32[6,8,1024]{2,1,0:T(8,128)S(1)}, bf16[4,256,768]{2,1,0:T(8,128)(2,1)S(1)}, bf16[32,24,768]{2,1,0:T(8,12...) custom-call(bf16[2048,128]{1,0:T(8,128)(2,1)S(1)} %copy-done, ...), custom_call_target="tpu_custom_call" | custom-call | flops 25769803776 | bytes 6291456 | tf_op jit(solution)/shard_map/attention/pallas_call | solution.py:718
  134.1 3.4 fusion.36
  137.6 1.6 copy-done.7
  139.8 2.6 add_convert_fusion.2
  142.5 12.1 %fusion.3 = (bf16[1024,3072]{1,0:T(8,128)(2,1)}, bf16[1024,3072]{1,0:T(8,128)(2,1)S(1)}) fusion(f32[3072]{0:T(1024)S(1)} %bitcast.99, bf16[1024,768]{1,0:T(8,128)(2,1)S(1)} %add_convert_fusion.2, bf16[768,3072]{1,0:T(8,128)(2,1)} %bitcast.100), kind=kOutput, calls=%fused_computation.4 | convolution fusion | flops 4869586944 | bytes 18886656 | tf_op jit(solution)/shard_map/dot_general | solution.py:19
  154.6 6.8 %fusion.37 = (f32[1024]{0:T(1024)S(1)}, f32[1024,768]{1,0:T(8,128)}) fusion(f32[768]{0:T(1024)S(1)} %reduce.11, bf16[1024,3072]{1,0:T(8,128)(2,1)S(1)} %get-tuple-element.60, bf16[3072,768]{1,0:T(8,128)(2,1)S(1)} %bitcast.107, bf16[1024,768]{1,0:T(8,128)(2,1)S(1)} %add_convert_fusion.2), kind=kOutput, calls=%fused_computation.109 | convolution fusion | flops 4834982912 | bytes 15735808 | tf_op jit(solution)/shard_map/dot_general | solution.py:19
  161.7 2.4 multiply_reduce_fusion.5
  164.2 4.1 %multiply_reduce_fusion = (bf16[768]{0:T(1024)(128)(2,1)S(1)}, f32[1024]{0:T(1024)S(1)}, bf16[1024,768]{1,0:T(8,128)(2,1)}) fusion(bf16[4,256,768]{2,1,0:T(8,128)(2,1)S(1)} %get-tuple-element.63, f32[1024,768]{1,0:T(8,128)} %get-tuple-element.108, f32[1024]{0:T(1024)S(1)} %reduce.12, f32[1024]{0:T(1024)S(1)} %add_rsqrt_fusion, ...), kind=kLoop, calls=%fused_computation.14 | loop fusion | flops 10221824 | bytes 6315520 | tf_op jit(solution)/shard_map/reduce_sum | solution.py:1074
  169.0 2.9 convert_reduce_fusion.1
  172.0 10.5 %fusion.38 = (bf16[3072]{0:T(1024)(128)(2,1)S(1)}, bf16[1024,3072]{1,0:T(8,128)(2,1)}) fusion(bf16[1024,3072]{1,0:T(8,128)(2,1)} %get-tuple-element.66, bf16[3072,768]{1,0:T(8,128)(2,1)} %bitcast.104, f32[1024,768]{1,0:T(8,128)S(1)} %get-tuple-element.88), kind=kOutput, calls=%fused_computation.110 | convolution fusion | flops 4845204480 | bytes 20453376 | tf_op jit(solution)/shard_map/dot_general | solution.py:27
  182.5 8.2 %multiply_reduce_fusion.1 = (bf16[768]{0:T(1024)(128)(2,1)S(1)}, f32[1024]{0:T(1024)S(1)}, f32[1024]{0:T(1024)S(1)}, bf16[768]{0:T(1024)(128)(2,1)S(1)}, f32[1024,768]{1,0:T(8,128)S(1)}) fusion(f32[1024,768]{1,0:T(8,128)S(1)} %copy-done.8, f32[1024]{0:T(1024)S(1)} %add_rsqrt_fusion.1, f32[1024]{0:T(1024)S(1)} %broadcast_multiply_fusion.4, ...), kind=kOutput, calls=%fused_computation.15 | convolution fusion | flops 4839698432 | bytes 20469760 | tf_op jit(solution)/shard_map/dot_general | solution.py:27
  190.7 1.6 convert_reduce_fusion
  192.4 2.6 convolution_convert_fusion.3.g_ref
  195.8 6.9 %convolution_convert_fusion.1 = bf16[768,3072]{1,0:T(8,128)(2,1)} fusion(bf16[1024,768]{1,0:T(8,128)(2,1)S(1)} %copy-done.13, bf16[1024,3072]{1,0:T(8,128)(2,1)S(1)} %copy-done.26), kind=kOutput, calls=%fused_computation.10 | convolution fusion | flops 4834197504 | bytes 12582912 | tf_op jit(solution)/shard_map/dot_general | solution.py:23
  202.7 7.1 %convolution_convert_fusion = bf16[3072,768]{1,0:T(8,128)(2,1)} fusion(bf16[1024,3072]{1,0:T(8,128)(2,1)S(1)} %bitcast.112, f32[1024,768]{1,0:T(8,128)S(1)} %get-tuple-element.88), kind=kOutput, calls=%fused_computation.9 | convolution fusion | flops 4834983936 | bytes 14155776 | tf_op jit(solution)/shard_map/dot_general | solution.py:23
  209.8 2.5 convolution_convert_fusion.4
  214.0 93.8 %attention_back.1 = (bf16[1024,2304]{1,0:T(8,128)(2,1)}, bf16[4,256,768]{2,1,0:T(8,128)(2,1)}, f32[24,3072]{1,0:T(8,128)}, f32[96,768]{1,0:T(8,128)}, f32[24,768]{1,0:T(8,128)}, /*index=5*/f32[8,256]{1,0:T(8,128)}) custom-call(bf16[1024,2304]{1,0:T(8,128)(2,1)} %add_convert_fusion.own_ref.all_ref.q_ref.k_ref.v_ref, ...), custom_call_target="tpu_custom_call" | custom-call | flops 64424509440 | bytes 9437184 | tf_op jit(solution)/shard_map/attention_back/pallas_call | solution.py:952
  307.9 8.3 %add_convert_fusion.1 = bf16[1024,768]{1,0:T(8,128)(2,1)S(1)} fusion(f32[1024,768]{1,0:T(8,128)} %copy-done.9, bf16[1024,2304]{1,0:T(8,128)(2,1)} %get-tuple-element.69, bf16[768,2304]{1,0:T(8,128)(2,1)} %bitcast.95), kind=kOutput, calls=%fused_computation.13 | convolution fusion | flops 3625451520 | bytes 12976128 | tf_op jit(solution)/shard_map/dot_general | solution.py:27
  316.2 4.4 %convolution_convert_fusion.2 = bf16[768,2304]{1,0:T(8,128)(2,1)S(1)} fusion(bf16[1024,768]{1,0:T(8,128)(2,1)S(1)} %bitcast.98, bf16[1024,2304]{1,0:T(8,128)(2,1)S(1)} %copy-done.10), kind=kOutput, calls=%fused_computation.11 | convolution fusion | flops 3625648128 | bytes 9830400 | tf_op jit(solution)/shard_map/dot_general | solution.py:23
  321.6 48.6 %end_exchange.1 = (bf16[4,256,768]{2,1,0:T(8,128)(2,1)S(1)}, f32[24,2304]{1,0:T(8,128)S(1)}, f32[8,128]{1,0:T(8,128)S(1)}) custom-call(bf16[4,256,768]{2,1,0:T(8,128)(2,1)S(1)} %bitcast.77, bf16[16,2,24,2304]{3,2,1,0:T(8,128)(2,1)S(1)} %bitcast.76, bf16[16,2,8,128]{3,2,1,0:T(8,128)(2,1)S(1)} %broadcast_in_dim.91.refs_1_), custom_call_target="tpu_custom_call" | custom-call | tf_op jit(solution)/shard_map/end_exchange/pallas_call | solution.py:543
  370.3 1.9 convert_element_type.135
  373.5 1.5 slice_bitcast_fusion
  (122 shorter events, 14.8 us)
Async XLA Ops:
  50.4 8.6 %copy-start = (bf16[2048,128]{1,0:T(8,128)(2,1)S(1)}, bf16[2048,128]{1,0:T(8,128)(2,1)}, u32[]{:S(2)}) copy-start(bf16[2048,128]{1,0:T(8,128)(2,1)} %get-tuple-element.51.bias_ref) | copy-start | bytes 1572868
  50.4 8.6 %copy-start.1 = (bf16[24,3072]{1,0:T(8,128)(2,1)S(1)}, bf16[24,3072]{1,0:T(8,128)(2,1)}, u32[]{:S(2)}) copy-start(bf16[24,3072]{1,0:T(8,128)(2,1)} %refs_1_.1) | copy-start | bytes 442372
  50.5 8.6 %copy-start.2 = (bf16[96,768]{1,0:T(8,128)(2,1)S(1)}, bf16[96,768]{1,0:T(8,128)(2,1)}, u32[]{:S(2)}) copy-start(bf16[96,768]{1,0:T(8,128)(2,1)} %refs_2_.1) | copy-start | bytes 442372
  50.5 8.6 %copy-start.3 = (bf16[24,768]{1,0:T(8,128)(2,1)S(1)}, bf16[24,768]{1,0:T(8,128)(2,1)}, u32[]{:S(2)}) copy-start(bf16[24,768]{1,0:T(8,128)(2,1)} %refs_0_.1) | copy-start | bytes 110596
  59.0 75.0 %copy-start.23 = (f32[1,768]{1,0:T(1,128)S(1)}, f32[1,768]{1,0:T(1,128)}, u32[]{:S(2)}) copy-start(f32[1,768]{1,0:T(1,128)} %get-tuple-element.55) | copy-start | bytes 9220
  139.8 14.8 %slice-start.2 = ((s8[4718592]{0:T(1024)(128)(4,1)}), s8[4194304]{0:T(1024)(128)(4,1)S(1)}, s32[]{:S(2)}) async-start(s8[4718592]{0:T(1024)(128)(4,1)} %bitcast.105), calls=%async_computation.2 | async-start | bytes 8388608
  142.4 12.2 %copy-start.12 = (bf16[1024,768]{1,0:T(8,128)(2,1)}, bf16[1024,768]{1,0:T(8,128)(2,1)S(1)}, u32[]{:S(2)}) copy-start(bf16[1024,768]{1,0:T(8,128)(2,1)S(1)} %add_convert_fusion.2) | copy-start | bytes 4718596
  142.5 12.2 %slice-start.3 = ((s8[4718592]{0:T(1024)(128)(4,1)}), s8[524288]{0:T(1024)(128)(4,1)S(1)}, s32[]{:S(2)}) async-start(s8[4718592]{0:T(1024)(128)(4,1)} %bitcast.105), calls=%async_computation.3 | async-start | bytes 1048576
  154.6 6.9 %copy-start.27 = (bf16[1024,3072]{1,0:T(8,128)(2,1)}, bf16[1024,3072]{1,0:T(8,128)(2,1)S(1)}, u32[]{:S(2)}) copy-start(bf16[1024,3072]{1,0:T(8,128)(2,1)S(1)} %get-tuple-element.60) | copy-start | bytes 18874372
  154.6 6.9 %copy-start.14 = (f32[1024,1]{1,0:T(8,128)S(1)}, f32[1024,1]{1,0:T(8,128)}, u32[]{:S(2)}) copy-start(f32[1024,1]{1,0:T(8,128)} %get-tuple-element.64) | copy-start | bytes 12292
  169.0 13.4 %slice-start = ((s8[4718592]{0:T(1024)(128)(4,1)}), s8[4194304]{0:T(1024)(128)(4,1)S(1)}, s32[]{:S(2)}) async-start(s8[4718592]{0:T(1024)(128)(4,1)} %bitcast.101), calls=%async_computation | async-start | bytes 8388608
  171.9 10.5 %copy-start.8 = (f32[1024,768]{1,0:T(8,128)S(1)}, f32[1024,768]{1,0:T(8,128)}, u32[]{:S(2)}) copy-start(f32[1024,768]{1,0:T(8,128)} %copy-done.7) | copy-start | bytes 9437188
  171.9 10.5 %slice-start.1 = ((s8[4718592]{0:T(1024)(128)(4,1)}), s8[524288]{0:T(1024)(128)(4,1)S(1)}, s32[]{:S(2)}) async-start(s8[4718592]{0:T(1024)(128)(4,1)} %bitcast.101), calls=%async_computation.1 | async-start | bytes 1048576
  190.7 4.3 %copy-start.26 = (bf16[1024,3072]{1,0:T(8,128)(2,1)S(1)}, bf16[1024,3072]{1,0:T(8,128)(2,1)}, u32[]{:S(2)}) copy-start(bf16[1024,3072]{1,0:T(8,128)(2,1)} %get-tuple-element.111) | copy-start | bytes 18874372
  192.3 17.4 %copy-start.9 = (f32[1024,768]{1,0:T(8,128)}, f32[1024,768]{1,0:T(8,128)S(1)}, u32[]{:S(2)}) copy-start(f32[1024,768]{1,0:T(8,128)S(1)} %get-tuple-element.90) | copy-start | bytes 9437188
  192.4 10.3 %slice-start.4 = ((s8[6291456]{0:T(1024)(128)(4,1)}), s8[4194304]{0:T(1024)(128)(4,1)S(1)}, s32[]{:S(2)}) async-start(s8[6291456]{0:T(1024)(128)(4,1)} %bitcast.111), calls=%async_computation.4 | async-start | bytes 8388608
  195.8 6.9 %slice-start.5 = ((s8[6291456]{0:T(1024)(128)(4,1)}), s8[2097152]{0:T(1024)(128)(4,1)S(1)}, s32[]{:S(2)}) async-start(s8[6291456]{0:T(1024)(128)(4,1)} %bitcast.111), calls=%async_computation.5 | async-start | bytes 4194304
  202.7 7.1 %copy-start.5 = (bf16[1024,768]{1,0:T(8,128)(2,1)S(1)}, bf16[1024,768]{1,0:T(8,128)(2,1)}, u32[]{:S(2)}) copy-start(bf16[1024,768]{1,0:T(8,128)(2,1)} %copy-done.4) | copy-start | bytes 4718596
  307.8 8.3 %copy-start.10 = (bf16[1024,2304]{1,0:T(8,128)(2,1)S(1)}, bf16[1024,2304]{1,0:T(8,128)(2,1)}, u32[]{:S(2)}) copy-start(bf16[1024,2304]{1,0:T(8,128)(2,1)} %get-tuple-element.69) | copy-start | bytes 14155780
  307.8 8.3 %copy-start.24 = (bf16[4,256,768]{2,1,0:T(8,128)(2,1)S(1)}, bf16[4,256,768]{2,1,0:T(8,128)(2,1)}, u32[]{:S(2)}) copy-start(bf16[4,256,768]{2,1,0:T(8,128)(2,1)} %get-tuple-element.47) | copy-start | bytes 4718596
  370.3 6.0 %copy-start.11 = (bf16[4,256,768]{2,1,0:T(8,128)(2,1)S(1)}, bf16[4,256,768]{2,1,0:T(8,128)(2,1)}, u32[]{:S(2)}) copy-start(bf16[4,256,768]{2,1,0:T(8,128)(2,1)} %get-tuple-element.133) | copy-start | bytes 4718596
  370.3 7.1 %copy-start.17 = (f32[24,768]{1,0:T(8,128)S(1)}, f32[24,768]{1,0:T(8,128)}, u32[]{:S(2)}) copy-start(f32[24,768]{1,0:T(8,128)} %get-tuple-element.138) | copy-start | bytes 221188
  370.3 7.8 %copy-start.16 = (f32[24,3072]{1,0:T(8,128)S(1)}, f32[24,3072]{1,0:T(8,128)}, u32[]{:S(2)}) copy-start(f32[24,3072]{1,0:T(8,128)} %get-tuple-element.139) | copy-start | bytes 884740
  372.2 6.5 %copy-start.15 = (f32[96,768]{1,0:T(8,128)S(1)}, f32[96,768]{1,0:T(8,128)}, u32[]{:S(2)}) copy-start(f32[96,768]{1,0:T(8,128)} %get-tuple-element.140) | copy-start | bytes 884740
  (10 other events, 21.5 us)
